TPU v7x, 32 devices: a whole 2x2x4 slice. The times are simulated.
32 devices in a mesh: groups: 2 (over y), tm: 4 (over x, core), rows: 4 (over z).
Axes of the slice: x: 2, y: 2, z: 4, core: 2. Of those that a mesh axis runs over, the one named last changes fastest.
Arguments:
- starts: float32 [8, 256, 4096], P(('groups', 'tm'), 'rows'), parts along dimension 0, may hold values from -1.2 to 1.2
- drive: float32 [256, 4096], P('rows'), may hold values from -0.6 to 0.6
Outputs:
- ends: float32 [8, 256, 4096], P(('groups', 'tm'), 'rows'), parts along dimension 0
There are 2 independent parts, one for each index of `groups`. A program takes and returns all parts, laid end to end along the dimension named above; an argument that names none is the same for every part. Nothing has to cross between parts.
All inputs are finite; a program needn't handle non-finite values.
Results may differ from a plain program's by a relative error of at most 0.00002.
Values sent between devices are 32-bit elements; how exact they have to be, the bound alone decides.
No kernel may reach another device: no remote copies, remote signals or barrier semaphores. Data moves between devices by JAX's collectives and lax.ppermute only.
A program may use at most 64 MiB of HBM per device.

v0:
```python
import jax
import jax.numpy as jnp
from jax import lax
from jax.sharding import PartitionSpec as P

FINE = 3


diffusion = 2.0
step_fine = 0.1


def with_halo(cells, sides, width):
    for axis, dim in sides:
        count = lax.axis_size(axis)
        ends = count - 1
        head = lax.slice_in_dim(cells, 0, width, axis=dim)
        tail = lax.slice_in_dim(cells, cells.shape[dim] - width, cells.shape[dim], axis=dim)
        cells = jnp.concatenate(
            [
                lax.ppermute(tail, axis, [(i, (i + 1) % count) for i in range(ends)]),
                cells,
                lax.ppermute(head, axis, [((i + 1) % count, i) for i in range(ends)]),
            ],
            axis=dim,
        )
    return cells


def shifted(block, axis, distance):
    devices = range(lax.axis_size(axis))
    route = [(i - distance, i) for i in devices if i - distance in devices]
    return lax.ppermute(block, axis, route)


def neighbour_sum(padded):
    centre = padded[1:-1]
    return padded[2:] + padded[:-2] + jnp.roll(centre, 1, axis=1) + jnp.roll(centre, -1, axis=1)


def fine_update(padded, drive):
    centre = padded[1:-1]
    nsum = neighbour_sum(padded)
    return centre + step_fine * (
        diffusion * (nsum - 4.0 * centre) + centre - centre * centre * centre + drive
    )


def coarse_apply(field, drive):
    coarse_step = FINE * step_fine
    padded = with_halo(field, (("rows", 0),), 1)
    centre = padded[1:-1]
    nsum = neighbour_sum(padded)
    return (
        centre + coarse_step * (diffusion * nsum + centre - centre * centre * centre + drive)
    ) / (1.0 + 4.0 * diffusion * coarse_step)


def fine_each(field, drive):
    for step in range(FINE):
        padded = with_halo(field, (("rows", 0),), 1)
        field = fine_update(padded, drive)
    return field


def on_device(starts, drive):
    start_field = starts[0]
    slice_index = lax.axis_index("tm")
    slice_count = lax.axis_size("tm")
    fine_field = fine_each(start_field, drive)
    delta = fine_field - coarse_apply(start_field, drive)

    def section_send(section, current):
        candidate = coarse_apply(current, drive) + delta
        arrived = shifted(candidate, "tm", 1)
        return jnp.where(slice_index == 0, start_field, arrived)

    current = lax.fori_loop(0, slice_count - 1, section_send, start_field)
    ends = coarse_apply(current, drive) + delta
    return ends[None]


def solution(mesh):
    in_specs = (P(("groups", "tm"), "rows", None), P("rows", None))
    out_specs = P(("groups", "tm"), "rows", None)
    return jax.shard_map(
        on_device, mesh=mesh, in_specs=in_specs, out_specs=out_specs, check_vma=False
    )
```

profile of v0, /device:TPU:2, one launch (start us, length us, event | category | flops | bytes accessed | tf_op | source)
XLA Modules:
  0.0 132.6 jit_solution(10011543308163625588)
XLA Ops:
  2.3 4.5 %collective-permute-start.4 = (f32[1,4096]{1,0:T(1,128)S(1)}, f32[1,4096]{1,0:T(1,128)S(1)}, u32[]{:S(2)}, u32[]{:S(2)}) collective-permute-start(f32[1,4096]{1,0:T(1,128)S(1)} %get-tuple-element.115), channel_id=1, source_target_pairs={{0,1},{1,2},{2,3},{4,5},{5,6},{6,7},{8,9},{9,10},{10,11},{12,13},{... | collective-permute-start | bytes 49160 | tf_op jit(solution)/shard_map/ppermute | solution.py:21
  6.9 3.4 %fusion.60 = (f32[64,4095]{1,0:T(8,128)}, f32[64,4095]{1,0:T(8,128)}) fusion(f32[64,4096]{1,0:T(8,128)} %bitcast.7), kind=kLoop, calls=%fused_computation.79 | loop fusion | bytes 4193280 | tf_op jit(solution)/shard_map/jit(_roll_static)/slice | solution.py:38
  11.5 2.2 %multiply_add_fusion = f32[64,4096]{1,0:T(8,128)S(1)} fusion(f32[64,4096]{1,0:T(8,128)S(1)} %bitcast.10, f32[64,4096]{1,0:T(8,128)S(1)} %copy-done.1, f32[64,1]{1,0:T(8,128)S(1)} %get-tuple-element.117, f32[64,4095]{1,0:T(8,128)} %get-tuple-element.119, f32[64,4095]{1,0:T(8,128)} %get-tuple-element.118, f32[64,1]{1,0:T(8,128)S(1)} %get-tuple-element.116, ...), kind=kLoop, calls=%fused_computation.63 | loop fusion | flops 4456448 | bytes 5275648 | tf_op jit(solution)/shard_map/add | solution.py:44
  15.4 4.5 %collective-permute-start.6 = (f32[1,4096]{1,0:T(1,128)S(1)}, f32[1,4096]{1,0:T(1,128)S(1)}, u32[]{:S(2)}, u32[]{:S(2)}) collective-permute-start(f32[1,4096]{1,0:T(1,128)S(1)} %get-tuple-element.113), channel_id=1, source_target_pairs={{0,1},{1,2},{2,3},{4,5},{5,6},{6,7},{8,9},{9,10},{10,11},{12,13},{... | collective-permute-start | bytes 49160 | tf_op jit(solution)/shard_map/ppermute | solution.py:21
  20.1 1.3 %collective-permute-done.6 = f32[1,4096]{1,0:T(1,128)S(1)} collective-permute-done((f32[1,4096]{1,0:T(1,128)S(1)}, f32[1,4096]{1,0:T(1,128)S(1)}, u32[]{:S(2)}, u32[]{:S(2)}) %collective-permute-start.6) | collective-permute-done | bytes 16416 | tf_op jit(solution)/shard_map/ppermute | solution.py:21
  22.5 1.4 %collective-permute-start.7 = (f32[1,4096]{1,0:T(1,128)S(1)}, f32[1,4096]{1,0:T(1,128)S(1)}, u32[]{:S(2)}, u32[]{:S(2)}) collective-permute-start(f32[1,4096]{1,0:T(1,128)S(1)} %get-tuple-element.106), channel_id=1, source_target_pairs={{1,0},{2,1},{3,2},{5,4},{6,5},{7,6},{9,8},{10,9},{11,10},{13,12},{... | collective-permute-start | bytes 49160 | tf_op jit(solution)/shard_map/ppermute | solution.py:23
  24.0 4.8 %collective-permute-start.8 = (f32[1,4096]{1,0:T(1,128)S(1)}, f32[1,4096]{1,0:T(1,128)S(1)}, u32[]{:S(2)}, u32[]{:S(2)}) collective-permute-start(f32[1,4096]{1,0:T(1,128)S(1)} %get-tuple-element.107), channel_id=1, source_target_pairs={{0,1},{1,2},{2,3},{4,5},{5,6},{6,7},{8,9},{9,10},{10,11},{12,13},{... | collective-permute-start | bytes 49160 | tf_op jit(solution)/shard_map/ppermute | solution.py:21
  28.9 1.3 %collective-permute-done.8 = f32[1,4096]{1,0:T(1,128)S(1)} collective-permute-done((f32[1,4096]{1,0:T(1,128)S(1)}, f32[1,4096]{1,0:T(1,128)S(1)}, u32[]{:S(2)}, u32[]{:S(2)}) %collective-permute-start.8) | collective-permute-done | bytes 16416 | tf_op jit(solution)/shard_map/ppermute | solution.py:21
  30.2 2.8 %fusion.19 = f32[64,4096]{1,0:T(8,128)} fusion(f32[64,4096]{1,0:T(8,128)S(1)} %fusion.14, f32[64,4096]{1,0:T(8,128)S(1)} %copy-done.1, f32[1,4096]{1,0:T(1,128)S(1)} %collective-permute-done.8, f32[1,4096]{1,0:T(1,128)S(1)} %collective-permute-done.7, f32[64,4095]{1,0:T(8,128)S(1)} %get-tuple-element.103, f32[64,1]{1,0:T(8,128)S(1)} %get-tuple-element.105, ...), kind=kLoop, calls=%fused_computation.27 | loop fusion | flops 8912896 | bytes 8454144 | tf_op jit(solution)/shard_map/sub | solution.py:71
  33.0 90.0 %while.12 = (s32[]{:T(128)}, f32[64,4096]{1,0:T(8,128)S(1)}, pred[]{:T(512)}, f32[64,4096]{1,0:T(8,128)S(1)}, f32[64,4096]{1,0:T(8,128)}, /*index=5*/f32[64,4096]{1,0:T(8,128)S(1)}, s32[]{:T(128)}) while((s32[]{:T(128)}, f32[64,4096]{1,0:T(8,128)S(1)}, pred[]{:T(512)}, f32[64,4096]{1,0:T(8,128)S(1)}, f32[64,4096]{1,0:T(8,128)}, ...), condition=%wide.region_1.2_spmd, body=%wide.region_0.1_spmd.sunk | while | flops 4718594 | bytes 26444028 | solution.py:78
  33.1 4.2 %collective-permute-start = (f32[1,4096]{1,0:T(1,128)S(1)}, f32[1,4096]{1,0:T(1,128)S(1)}, u32[]{:S(2)}, u32[]{:S(2)}) collective-permute-start(f32[1,4096]{1,0:T(1,128)S(1)} %get-tuple-element.163), channel_id=1, source_target_pairs={{0,1},{1,2},{2,3},{4,5},{5,6},{6,7},{8,9},{9,10},{10,11},{12,13},{... | collective-permute-start | bytes 49160 | tf_op jit(solution)/shard_map/while/body/eval_jaxpr/ppermute | solution.py:21
  37.3 1.4 %collective-permute-start.1 = (f32[1,4096]{1,0:T(1,128)S(1)}, f32[1,4096]{1,0:T(1,128)S(1)}, u32[]{:S(2)}, u32[]{:S(2)}) collective-permute-start(f32[1,4096]{1,0:T(1,128)S(1)} %get-tuple-element.164), channel_id=1, source_target_pairs={{1,0},{2,1},{3,2},{5,4},{6,5},{7,6},{9,8},{10,9},{11,10},{13,12},{... | collective-permute-start | bytes 49160 | tf_op jit(solution)/shard_map/while/body/eval_jaxpr/ppermute | solution.py:23
  39.2 3.9 %collective-permute-done.1 = f32[1,4096]{1,0:T(1,128)S(1)} collective-permute-done((f32[1,4096]{1,0:T(1,128)S(1)}, f32[1,4096]{1,0:T(1,128)S(1)}, u32[]{:S(2)}, u32[]{:S(2)}) %collective-permute-start.1) | collective-permute-done | bytes 16416 | tf_op jit(solution)/shard_map/while/body/eval_jaxpr/ppermute | solution.py:23
  43.1 1.7 %fusion.68 = f32[64,4096]{1,0:T(8,128)} fusion(f32[64,4096]{1,0:T(8,128)S(1)} %copy-done.2, f32[64,4096]{1,0:T(8,128)S(1)} %get-tuple-element.177, f32[64,4096]{1,0:T(8,128)S(1)} %get-tuple-element.186, f32[1,4096]{1,0:T(1,128)S(1)} %collective-permute-done, f32[1,4096]{1,0:T(1,128)S(1)} %collective-permute-done.1, ...), kind=kLoop, calls=%fused_computation.6.clone.1 | loop fusion | flops 4456448 | bytes 6324224 | tf_op jit(solution)/shard_map/while/body/eval_jaxpr/add | solution.py:74
  44.7 1.9 %collective-permute-start.2 = (f32[64,4096]{1,0:T(8,128)}, f32[64,4096]{1,0:T(8,128)S(1)}, u32[]{:S(2)}, u32[]{:S(2)}) collective-permute-start(f32[64,4096]{1,0:T(8,128)} %fusion.68), channel_id=1, source_target_pairs={{0,4},{4,8},{8,12},{1,5},{5,9},{9,13},{2,6},{6,10},{10,14},{3,7},{... | collective-permute-start | bytes 3145736 | tf_op jit(solution)/shard_map/while/body/eval_jaxpr/ppermute | solution.py:33
  46.6 14.4 %collective-permute-done.2 = f32[64,4096]{1,0:T(8,128)S(1)} collective-permute-done((f32[64,4096]{1,0:T(8,128)}, f32[64,4096]{1,0:T(8,128)S(1)}, u32[]{:S(2)}, u32[]{:S(2)}) %collective-permute-start.2) | collective-permute-done | bytes 1048608 | tf_op jit(solution)/shard_map/while/body/eval_jaxpr/ppermute | solution.py:33
  62.0 1.3 %broadcast_select_fusion.2 = f32[64,4096]{1,0:T(8,128)S(1)} fusion(f32[64,4096]{1,0:T(8,128)S(1)} %get-tuple-element.188, f32[64,4096]{1,0:T(8,128)} %copy-done.4, pred[]{:T(512)} %get-tuple-element.185), kind=kLoop, calls=%fused_computation.14.clone.1 | loop fusion | flops 262144 | bytes 3145729 | tf_op jit(solution)/shard_map/while/body/eval_jaxpr/jit(_where)/select_n | solution.py:76
  63.4 3.9 %collective-permute-start = (f32[1,4096]{1,0:T(1,128)S(1)}, f32[1,4096]{1,0:T(1,128)S(1)}, u32[]{:S(2)}, u32[]{:S(2)}) collective-permute-start(f32[1,4096]{1,0:T(1,128)S(1)} %get-tuple-element.163), channel_id=1, source_target_pairs={{0,1},{1,2},{2,3},{4,5},{5,6},{6,7},{8,9},{9,10},{10,11},{12,13},{... | collective-permute-start | bytes 49160 | tf_op jit(solution)/shard_map/while/body/eval_jaxpr/ppermute | solution.py:21
  67.3 1.4 %collective-permute-start.1 = (f32[1,4096]{1,0:T(1,128)S(1)}, f32[1,4096]{1,0:T(1,128)S(1)}, u32[]{:S(2)}, u32[]{:S(2)}) collective-permute-start(f32[1,4096]{1,0:T(1,128)S(1)} %get-tuple-element.164), channel_id=1, source_target_pairs={{1,0},{2,1},{3,2},{5,4},{6,5},{7,6},{9,8},{10,9},{11,10},{13,12},{... | collective-permute-start | bytes 49160 | tf_op jit(solution)/shard_map/while/body/eval_jaxpr/ppermute | solution.py:23
  69.2 3.9 %collective-permute-done.1 = f32[1,4096]{1,0:T(1,128)S(1)} collective-permute-done((f32[1,4096]{1,0:T(1,128)S(1)}, f32[1,4096]{1,0:T(1,128)S(1)}, u32[]{:S(2)}, u32[]{:S(2)}) %collective-permute-start.1) | collective-permute-done | bytes 16416 | tf_op jit(solution)/shard_map/while/body/eval_jaxpr/ppermute | solution.py:23
  73.1 1.7 %fusion.68 = f32[64,4096]{1,0:T(8,128)} fusion(f32[64,4096]{1,0:T(8,128)S(1)} %copy-done.2, f32[64,4096]{1,0:T(8,128)S(1)} %get-tuple-element.177, f32[64,4096]{1,0:T(8,128)S(1)} %get-tuple-element.186, f32[1,4096]{1,0:T(1,128)S(1)} %collective-permute-done, f32[1,4096]{1,0:T(1,128)S(1)} %collective-permute-done.1, ...), kind=kLoop, calls=%fused_computation.6.clone.1 | loop fusion | flops 4456448 | bytes 6324224 | tf_op jit(solution)/shard_map/while/body/eval_jaxpr/add | solution.py:74
  74.8 1.9 %collective-permute-start.2 = (f32[64,4096]{1,0:T(8,128)}, f32[64,4096]{1,0:T(8,128)S(1)}, u32[]{:S(2)}, u32[]{:S(2)}) collective-permute-start(f32[64,4096]{1,0:T(8,128)} %fusion.68), channel_id=1, source_target_pairs={{0,4},{4,8},{8,12},{1,5},{5,9},{9,13},{2,6},{6,10},{10,14},{3,7},{... | collective-permute-start | bytes 3145736 | tf_op jit(solution)/shard_map/while/body/eval_jaxpr/ppermute | solution.py:33
  76.7 14.4 %collective-permute-done.2 = f32[64,4096]{1,0:T(8,128)S(1)} collective-permute-done((f32[64,4096]{1,0:T(8,128)}, f32[64,4096]{1,0:T(8,128)S(1)}, u32[]{:S(2)}, u32[]{:S(2)}) %collective-permute-start.2) | collective-permute-done | bytes 1048608 | tf_op jit(solution)/shard_map/while/body/eval_jaxpr/ppermute | solution.py:33
  93.4 3.5 %collective-permute-start = (f32[1,4096]{1,0:T(1,128)S(1)}, f32[1,4096]{1,0:T(1,128)S(1)}, u32[]{:S(2)}, u32[]{:S(2)}) collective-permute-start(f32[1,4096]{1,0:T(1,128)S(1)} %get-tuple-element.163), channel_id=1, source_target_pairs={{0,1},{1,2},{2,3},{4,5},{5,6},{6,7},{8,9},{9,10},{10,11},{12,13},{... | collective-permute-start | bytes 49160 | tf_op jit(solution)/shard_map/while/body/eval_jaxpr/ppermute | solution.py:21
  97.0 1.4 %collective-permute-start.1 = (f32[1,4096]{1,0:T(1,128)S(1)}, f32[1,4096]{1,0:T(1,128)S(1)}, u32[]{:S(2)}, u32[]{:S(2)}) collective-permute-start(f32[1,4096]{1,0:T(1,128)S(1)} %get-tuple-element.164), channel_id=1, source_target_pairs={{1,0},{2,1},{3,2},{5,4},{6,5},{7,6},{9,8},{10,9},{11,10},{13,12},{... | collective-permute-start | bytes 49160 | tf_op jit(solution)/shard_map/while/body/eval_jaxpr/ppermute | solution.py:23
  98.8 3.9 %collective-permute-done.1 = f32[1,4096]{1,0:T(1,128)S(1)} collective-permute-done((f32[1,4096]{1,0:T(1,128)S(1)}, f32[1,4096]{1,0:T(1,128)S(1)}, u32[]{:S(2)}, u32[]{:S(2)}) %collective-permute-start.1) | collective-permute-done | bytes 16416 | tf_op jit(solution)/shard_map/while/body/eval_jaxpr/ppermute | solution.py:23
  102.7 1.7 %fusion.68 = f32[64,4096]{1,0:T(8,128)} fusion(f32[64,4096]{1,0:T(8,128)S(1)} %copy-done.2, f32[64,4096]{1,0:T(8,128)S(1)} %get-tuple-element.177, f32[64,4096]{1,0:T(8,128)S(1)} %get-tuple-element.186, f32[1,4096]{1,0:T(1,128)S(1)} %collective-permute-done, f32[1,4096]{1,0:T(1,128)S(1)} %collective-permute-done.1, ...), kind=kLoop, calls=%fused_computation.6.clone.1 | loop fusion | flops 4456448 | bytes 6324224 | tf_op jit(solution)/shard_map/while/body/eval_jaxpr/add | solution.py:74
  104.4 1.9 %collective-permute-start.2 = (f32[64,4096]{1,0:T(8,128)}, f32[64,4096]{1,0:T(8,128)S(1)}, u32[]{:S(2)}, u32[]{:S(2)}) collective-permute-start(f32[64,4096]{1,0:T(8,128)} %fusion.68), channel_id=1, source_target_pairs={{0,4},{4,8},{8,12},{1,5},{5,9},{9,13},{2,6},{6,10},{10,14},{3,7},{... | collective-permute-start | bytes 3145736 | tf_op jit(solution)/shard_map/while/body/eval_jaxpr/ppermute | solution.py:33
  106.3 14.4 %collective-permute-done.2 = f32[64,4096]{1,0:T(8,128)S(1)} collective-permute-done((f32[64,4096]{1,0:T(8,128)}, f32[64,4096]{1,0:T(8,128)S(1)}, u32[]{:S(2)}, u32[]{:S(2)}) %collective-permute-start.2) | collective-permute-done | bytes 1048608 | tf_op jit(solution)/shard_map/while/body/eval_jaxpr/ppermute | solution.py:33
  123.4 1.9 %collective-permute-start.10 = (f32[1,4096]{1,0:T(1,128)S(1)}, f32[1,4096]{1,0:T(1,128)S(1)}, u32[]{:S(2)}, u32[]{:S(2)}) collective-permute-start(f32[1,4096]{1,0:T(1,128)S(1)} %get-tuple-element.101), channel_id=1, source_target_pairs={{0,1},{1,2},{2,3},{4,5},{5,6},{6,7},{8,9},{9,10},{10,11},{12,13},{... | collective-permute-start | bytes 49160 | tf_op jit(solution)/shard_map/ppermute | solution.py:21
  126.8 4.2 %collective-permute-done.9 = f32[1,4096]{1,0:T(1,128)S(1)} collective-permute-done((f32[1,4096]{1,0:T(1,128)S(1)}, f32[1,4096]{1,0:T(1,128)S(1)}, u32[]{:S(2)}, u32[]{:S(2)}) %collective-permute-start.9) | collective-permute-done | bytes 16416 | tf_op jit(solution)/shard_map/ppermute | solution.py:23
  131.0 1.7 %fusion.26 = f32[1,64,4096]{2,1,0:T(8,128)} fusion(f32[64,4096]{1,0:T(8,128)S(1)} %copy-done.3, f32[64,4096]{1,0:T(8,128)S(1)} %get-tuple-element.77, f32[64,4096]{1,0:T(8,128)S(1)} %get-tuple-element.190, f32[1,4096]{1,0:T(1,128)S(1)} %collective-permute-done.10, f32[1,4096]{1,0:T(1,128)S(1)} %collective-permute-done.9, ...), kind=kLoop, calls=%fused_computation.34 | loop fusion | flops 4456448 | bytes 6324224 | tf_op jit(solution)/shard_map/broadcast_in_dim | solution.py:80
  (57 shorter events, 15.2 us)
Async XLA Ops:
  1.0 9.4 %collective-permute-start.3 = (f32[1,4096]{1,0:T(1,128)S(1)}, f32[1,4096]{1,0:T(1,128)S(1)}, u32[]{:S(2)}, u32[]{:S(2)}) collective-permute-start(f32[1,4096]{1,0:T(1,128)S(1)} %get-tuple-element.114), channel_id=1, source_target_pairs={{1,0},{2,1},{3,2},{5,4},{6,5},{7,6},{9,8},{10,9},{11,10},{13,12},{... | collective-permute-start | bytes 49160 | tf_op jit(solution)/shard_map/ppermute | solution.py:23
  2.3 8.1 %collective-permute-start.4 = (f32[1,4096]{1,0:T(1,128)S(1)}, f32[1,4096]{1,0:T(1,128)S(1)}, u32[]{:S(2)}, u32[]{:S(2)}) collective-permute-start(f32[1,4096]{1,0:T(1,128)S(1)} %get-tuple-element.115), channel_id=1, source_target_pairs={{0,1},{1,2},{2,3},{4,5},{5,6},{6,7},{8,9},{9,10},{10,11},{12,13},{... | collective-permute-start | bytes 49160 | tf_op jit(solution)/shard_map/ppermute | solution.py:21
  6.8 3.4 %copy-start = (f32[1,64,4096]{2,1,0:T(8,128)S(1)}, f32[1,64,4096]{2,1,0:T(8,128)}, u32[]{:S(2)}) copy-start(f32[1,64,4096]{2,1,0:T(8,128)} %param.4) | copy-start | bytes 3145732
  10.3 1.2 copy-start.1
  14.1 5.9 %collective-permute-start.5 = (f32[1,4096]{1,0:T(1,128)S(1)}, f32[1,4096]{1,0:T(1,128)S(1)}, u32[]{:S(2)}, u32[]{:S(2)}) collective-permute-start(f32[1,4096]{1,0:T(1,128)S(1)} %get-tuple-element.112), channel_id=1, source_target_pairs={{1,0},{2,1},{3,2},{5,4},{6,5},{7,6},{9,8},{10,9},{11,10},{13,12},{... | collective-permute-start | bytes 49160 | tf_op jit(solution)/shard_map/ppermute | solution.py:23
  15.4 6.0 %collective-permute-start.6 = (f32[1,4096]{1,0:T(1,128)S(1)}, f32[1,4096]{1,0:T(1,128)S(1)}, u32[]{:S(2)}, u32[]{:S(2)}) collective-permute-start(f32[1,4096]{1,0:T(1,128)S(1)} %get-tuple-element.113), channel_id=1, source_target_pairs={{0,1},{1,2},{2,3},{4,5},{5,6},{6,7},{8,9},{9,10},{10,11},{12,13},{... | collective-permute-start | bytes 49160 | tf_op jit(solution)/shard_map/ppermute | solution.py:21
  22.1 8.1 %copy-start.5 = (f32[64,4095]{1,0:T(8,128)S(1)}, f32[64,4095]{1,0:T(8,128)}, u32[]{:S(2)}) copy-start(f32[64,4095]{1,0:T(8,128)} %get-tuple-element.118) | copy-start | bytes 3144964
  22.1 8.1 %copy-start.6 = (f32[64,4095]{1,0:T(8,128)S(1)}, f32[64,4095]{1,0:T(8,128)}, u32[]{:S(2)}) copy-start(f32[64,4095]{1,0:T(8,128)} %get-tuple-element.119) | copy-start | bytes 3144964
  22.5 6.3 %collective-permute-start.7 = (f32[1,4096]{1,0:T(1,128)S(1)}, f32[1,4096]{1,0:T(1,128)S(1)}, u32[]{:S(2)}, u32[]{:S(2)}) collective-permute-start(f32[1,4096]{1,0:T(1,128)S(1)} %get-tuple-element.106), channel_id=1, source_target_pairs={{1,0},{2,1},{3,2},{5,4},{6,5},{7,6},{9,8},{10,9},{11,10},{13,12},{... | collective-permute-start | bytes 49160 | tf_op jit(solution)/shard_map/ppermute | solution.py:23
  24.0 6.3 %collective-permute-start.8 = (f32[1,4096]{1,0:T(1,128)S(1)}, f32[1,4096]{1,0:T(1,128)S(1)}, u32[]{:S(2)}, u32[]{:S(2)}) collective-permute-start(f32[1,4096]{1,0:T(1,128)S(1)} %get-tuple-element.107), channel_id=1, source_target_pairs={{0,1},{1,2},{2,3},{4,5},{5,6},{6,7},{8,9},{9,10},{10,11},{12,13},{... | collective-permute-start | bytes 49160 | tf_op jit(solution)/shard_map/ppermute | solution.py:21
  33.1 6.1 %collective-permute-start = (f32[1,4096]{1,0:T(1,128)S(1)}, f32[1,4096]{1,0:T(1,128)S(1)}, u32[]{:S(2)}, u32[]{:S(2)}) collective-permute-start(f32[1,4096]{1,0:T(1,128)S(1)} %get-tuple-element.163), channel_id=1, source_target_pairs={{0,1},{1,2},{2,3},{4,5},{5,6},{6,7},{8,9},{9,10},{10,11},{12,13},{... | collective-permute-start | bytes 49160 | tf_op jit(solution)/shard_map/while/body/eval_jaxpr/ppermute | solution.py:21
  37.3 5.8 %copy-start.2 = (f32[64,4096]{1,0:T(8,128)S(1)}, f32[64,4096]{1,0:T(8,128)}, u32[]{:S(2)}) copy-start(f32[64,4096]{1,0:T(8,128)} %get-tuple-element.187) | copy-start | bytes 3145732 | tf_op jit(solution)/shard_map/while
  37.3 5.8 %collective-permute-start.1 = (f32[1,4096]{1,0:T(1,128)S(1)}, f32[1,4096]{1,0:T(1,128)S(1)}, u32[]{:S(2)}, u32[]{:S(2)}) collective-permute-start(f32[1,4096]{1,0:T(1,128)S(1)} %get-tuple-element.164), channel_id=1, source_target_pairs={{1,0},{2,1},{3,2},{5,4},{6,5},{7,6},{9,8},{10,9},{11,10},{13,12},{... | collective-permute-start | bytes 49160 | tf_op jit(solution)/shard_map/while/body/eval_jaxpr/ppermute | solution.py:23
  44.7 16.3 %collective-permute-start.2 = (f32[64,4096]{1,0:T(8,128)}, f32[64,4096]{1,0:T(8,128)S(1)}, u32[]{:S(2)}, u32[]{:S(2)}) collective-permute-start(f32[64,4096]{1,0:T(8,128)} %fusion.68), channel_id=1, source_target_pairs={{0,4},{4,8},{8,12},{1,5},{5,9},{9,13},{2,6},{6,10},{10,14},{3,7},{... | collective-permute-start | bytes 3145736 | tf_op jit(solution)/shard_map/while/body/eval_jaxpr/ppermute | solution.py:33
  61.0 1.0 copy-start.4
  63.4 5.8 %collective-permute-start = (f32[1,4096]{1,0:T(1,128)S(1)}, f32[1,4096]{1,0:T(1,128)S(1)}, u32[]{:S(2)}, u32[]{:S(2)}) collective-permute-start(f32[1,4096]{1,0:T(1,128)S(1)} %get-tuple-element.163), channel_id=1, source_target_pairs={{0,1},{1,2},{2,3},{4,5},{5,6},{6,7},{8,9},{9,10},{10,11},{12,13},{... | collective-permute-start | bytes 49160 | tf_op jit(solution)/shard_map/while/body/eval_jaxpr/ppermute | solution.py:21
  67.3 5.8 %copy-start.2 = (f32[64,4096]{1,0:T(8,128)S(1)}, f32[64,4096]{1,0:T(8,128)}, u32[]{:S(2)}) copy-start(f32[64,4096]{1,0:T(8,128)} %get-tuple-element.187) | copy-start | bytes 3145732 | tf_op jit(solution)/shard_map/while
  67.3 5.8 %collective-permute-start.1 = (f32[1,4096]{1,0:T(1,128)S(1)}, f32[1,4096]{1,0:T(1,128)S(1)}, u32[]{:S(2)}, u32[]{:S(2)}) collective-permute-start(f32[1,4096]{1,0:T(1,128)S(1)} %get-tuple-element.164), channel_id=1, source_target_pairs={{1,0},{2,1},{3,2},{5,4},{6,5},{7,6},{9,8},{10,9},{11,10},{13,12},{... | collective-permute-start | bytes 49160 | tf_op jit(solution)/shard_map/while/body/eval_jaxpr/ppermute | solution.py:23
  74.8 16.3 %collective-permute-start.2 = (f32[64,4096]{1,0:T(8,128)}, f32[64,4096]{1,0:T(8,128)S(1)}, u32[]{:S(2)}, u32[]{:S(2)}) collective-permute-start(f32[64,4096]{1,0:T(8,128)} %fusion.68), channel_id=1, source_target_pairs={{0,4},{4,8},{8,12},{1,5},{5,9},{9,13},{2,6},{6,10},{10,14},{3,7},{... | collective-permute-start | bytes 3145736 | tf_op jit(solution)/shard_map/while/body/eval_jaxpr/ppermute | solution.py:33
  91.1 1.0 copy-start.4
  93.4 5.4 %collective-permute-start = (f32[1,4096]{1,0:T(1,128)S(1)}, f32[1,4096]{1,0:T(1,128)S(1)}, u32[]{:S(2)}, u32[]{:S(2)}) collective-permute-start(f32[1,4096]{1,0:T(1,128)S(1)} %get-tuple-element.163), channel_id=1, source_target_pairs={{0,1},{1,2},{2,3},{4,5},{5,6},{6,7},{8,9},{9,10},{10,11},{12,13},{... | collective-permute-start | bytes 49160 | tf_op jit(solution)/shard_map/while/body/eval_jaxpr/ppermute | solution.py:21
  96.9 5.8 %copy-start.2 = (f32[64,4096]{1,0:T(8,128)S(1)}, f32[64,4096]{1,0:T(8,128)}, u32[]{:S(2)}) copy-start(f32[64,4096]{1,0:T(8,128)} %get-tuple-element.187) | copy-start | bytes 3145732 | tf_op jit(solution)/shard_map/while
  97.0 5.8 %collective-permute-start.1 = (f32[1,4096]{1,0:T(1,128)S(1)}, f32[1,4096]{1,0:T(1,128)S(1)}, u32[]{:S(2)}, u32[]{:S(2)}) collective-permute-start(f32[1,4096]{1,0:T(1,128)S(1)} %get-tuple-element.164), channel_id=1, source_target_pairs={{1,0},{2,1},{3,2},{5,4},{6,5},{7,6},{9,8},{10,9},{11,10},{13,12},{... | collective-permute-start | bytes 49160 | tf_op jit(solution)/shard_map/while/body/eval_jaxpr/ppermute | solution.py:23
  104.4 16.3 %collective-permute-start.2 = (f32[64,4096]{1,0:T(8,128)}, f32[64,4096]{1,0:T(8,128)S(1)}, u32[]{:S(2)}, u32[]{:S(2)}) collective-permute-start(f32[64,4096]{1,0:T(8,128)} %fusion.68), channel_id=1, source_target_pairs={{0,4},{4,8},{8,12},{1,5},{5,9},{9,13},{2,6},{6,10},{10,14},{3,7},{... | collective-permute-start | bytes 3145736 | tf_op jit(solution)/shard_map/while/body/eval_jaxpr/ppermute | solution.py:33
  120.7 1.0 copy-start.4
  123.0 8.0 %copy-start.3 = (f32[64,4096]{1,0:T(8,128)S(1)}, f32[64,4096]{1,0:T(8,128)}, u32[]{:S(2)}) copy-start(f32[64,4096]{1,0:T(8,128)} %get-tuple-element.191) | copy-start | bytes 3145732
  123.4 3.4 %collective-permute-start.10 = (f32[1,4096]{1,0:T(1,128)S(1)}, f32[1,4096]{1,0:T(1,128)S(1)}, u32[]{:S(2)}, u32[]{:S(2)}) collective-permute-start(f32[1,4096]{1,0:T(1,128)S(1)} %get-tuple-element.101), channel_id=1, source_target_pairs={{0,1},{1,2},{2,3},{4,5},{5,6},{6,7},{8,9},{9,10},{10,11},{12,13},{... | collective-permute-start | bytes 49160 | tf_op jit(solution)/shard_map/ppermute | solution.py:21
  125.3 5.6 %collective-permute-start.9 = (f32[1,4096]{1,0:T(1,128)S(1)}, f32[1,4096]{1,0:T(1,128)S(1)}, u32[]{:S(2)}, u32[]{:S(2)}) collective-permute-start(f32[1,4096]{1,0:T(1,128)S(1)} %get-tuple-element.100), channel_id=1, source_target_pairs={{1,0},{2,1},{3,2},{5,4},{6,5},{7,6},{9,8},{10,9},{11,10},{13,12},{... | collective-permute-start | bytes 49160 | tf_op jit(solution)/shard_map/ppermute | solution.py:23
where the time goes:
time: 133 us
  waiting for transfers between devices  61.9 us (47%)
  starting transfers between devices  42.7 us (32%)
  other arithmetic  16.4 us (12%)
  local copies, waits for them, and re-layouts  11.3 us (8%)
    ppermute x3, waiting for transfers between devices, shifted(): return lax.ppermute(block, axis, route)  43.2 us
    ppermute x7, starting transfers between devices, with_halo(): lax.ppermute(tail, axis, [(i, (i + 1) % count) for i in range(ends)])  27.4 us
    ppermute x7, waiting for transfers between devices, with_halo(): lax.ppermute(head, axis, [((i + 1) % count, i) for i in range(ends)])  15.9 us
    ppermute x7, starting transfers between devices, with_halo(): lax.ppermute(head, axis, [((i + 1) % count, i) for i in range(ends)])  9.57 us
    ppermute x3, starting transfers between devices, shifted(): return lax.ppermute(block, axis, route)  5.72 us
    add x3, other arithmetic, section_send(): candidate = coarse_apply(current, drive) + delta  4.99 us
    select_n x3, other arithmetic, section_send(): return jnp.where(slice_index == 0, start_field, arrived)  4.01 us
    slice x2, local copies, waits for them, and re-layouts, neighbour_sum(): jnp.roll(centre, 1, axis=1)  3.44 us
  transfers between devices with their start and end apart: 17, of which 9 were waited for; matrix products, arithmetic and copies ran while one was open for 4% of the time, Pallas kernels for 0%

commit v1 on v0

v1 whole, which is shorter than its diff:
```python
import jax
import jax.numpy as jnp
from jax import lax
from jax.sharding import PartitionSpec as P

FINE = 3
WIDE = 8


diffusion = 2.0
step_fine = 0.1
coarse_step = FINE * step_fine

AXES = ("groups", "tm", "rows")


def routed(block, route):
    groups, slices, rows = (lax.axis_size(a) for a in AXES)
    pairs = []
    for g in range(groups):
        for t in range(slices):
            for r in range(rows):
                to_t, to_r = route(t, r)
                pairs.append(((g * slices + t) * rows + r, (g * slices + to_t) * rows + to_r))
    return lax.ppermute(block, AXES, pairs)


def partner(t, r):
    return t ^ 1, r


def outward(slices, rows):
    def route(t, r):
        to_r = r + 1 if t & 1 else r - 1
        if 0 <= to_r < rows:
            return t ^ 1, to_r
        other = t ^ 2
        return (other, r) if other < slices else (t, r)

    return route


def stage_swap(stage, slices):
    def route(t, r):
        chip = t // 2
        if chip == stage:
            return t + 2, r
        if chip == stage + 1:
            return t - 2, r
        return t, r

    return route


def neighbour_sum(field):
    return (
        jnp.roll(field, 1, axis=0)
        + jnp.roll(field, -1, axis=0)
        + jnp.roll(field, 1, axis=1)
        + jnp.roll(field, -1, axis=1)
    )


def fine_update(v, drive, inside):
    nsum = neighbour_sum(v)
    new = v + step_fine * (diffusion * (nsum - 4.0 * v) + v - v * v * v + drive)
    return jnp.where(inside, new, 0.0)


def coarse_update(v, drive, inside):
    nsum = neighbour_sum(v)
    new = (v + coarse_step * (diffusion * nsum + v - v * v * v + drive)) / (
        1.0 + 4.0 * diffusion * coarse_step
    )
    return jnp.where(inside, new, 0.0)


def on_device(starts, drive):
    own = starts[0]
    height = own.shape[0]
    half = height // 2
    slices, rows = lax.axis_size("tm"), lax.axis_size("rows")
    chips = slices // 2
    t, r = lax.axis_index("tm"), lax.axis_index("rows")
    core, chip = t % 2, t // 2
    first = core == 0
    away = outward(slices, rows)

    other = routed(own, partner)
    s_a = jnp.where(first, own, other)
    s_b = jnp.where(first, other, own)

    edge = core * (height - WIDE)
    near = core * (half - WIDE)

    def cut(field, start, size):
        return lax.dynamic_slice_in_dim(field, start, size, axis=0)

    sent = jnp.concatenate([cut(f, edge, WIDE) for f in (s_a, s_b, drive)])
    got = routed(sent, away)

    def window(field, place):
        body = cut(field, near, half + WIDE)
        side = got[place * WIDE : (place + 1) * WIDE]
        return jnp.where(
            first, jnp.concatenate([side, body]), jnp.concatenate([body, side])
        )

    w_a, w_b, w_d = (window(f, i) for i, f in enumerate((s_a, s_b, drive)))
    span = half + 2 * WIDE
    row = r * height + core * half - WIDE + lax.broadcasted_iota(jnp.int32, (span, 1), 0)
    inside = (row >= 0) & (row < rows * height)
    w_a = jnp.where(inside, w_a, 0.0)
    w_b = jnp.where(inside, w_b, 0.0)

    def fine(v):
        for _ in range(FINE):
            v = fine_update(v, w_d, inside)
        return v

    d_a = fine(w_a) - coarse_update(w_a, w_d, inside)
    d_b = fine(w_b) - coarse_update(w_b, w_d, inside)

    def chain(v):
        e_a = coarse_update(v, w_d, inside) + d_a
        e_b = coarse_update(e_a, w_d, inside) + d_b
        return e_a, e_b

    def extended(v):
        inner = routed(cut(v, jnp.where(first, WIDE + half - 2, WIDE), 2), partner)
        outer = routed(cut(v, jnp.where(first, WIDE, WIDE + half - 2), 2), away)
        body = v[WIDE : WIDE + half]
        above = jnp.where(first, outer, inner)
        below = jnp.where(first, inner, outer)
        return jnp.concatenate([above, body, below])

    e_a, e_b = chain(w_a)
    for stage in range(chips - 1):
        moved = e_b[WIDE - 2 : WIDE + half + 2] if stage == 0 else extended(e_b)
        arrived = routed(moved, stage_swap(stage, slices))
        current = jnp.pad(arrived, ((WIDE - 2, WIDE - 2), (0, 0)))
        current = jnp.where(inside, current, 0.0)
        n_a, n_b = chain(current)
        here = chip == stage + 1
        e_a = jnp.where(here, n_a, e_a)
        e_b = jnp.where(here, n_b, e_b)

    e_a, e_b = e_a[WIDE : WIDE + half], e_b[WIDE : WIDE + half]
    back = routed(jnp.where(first, e_b, e_a), partner)
    top = jnp.where(first, e_a, back)
    low = jnp.where(first, back, e_b)
    return jnp.concatenate([top, low])[None]


def solution(mesh):
    in_specs = (P(("groups", "tm"), "rows", None), P("rows", None))
    out_specs = P(("groups", "tm"), "rows", None)
    return jax.shard_map(
        on_device, mesh=mesh, in_specs=in_specs, out_specs=out_specs, check_vma=False
    )
```

time: 133 us -> 49.3 us (0.37)
  the two profiles are of different devices: /device:TPU:2 before, /device:TPU:0 now
where the time goes in v1:
time: 49.3 us; the launch traced here: 49.1 us
  waiting for transfers between devices  23.9 us (48%)
  other arithmetic  11.3 us (23%)
  local copies, waits for them, and re-layouts  8.15 us (17%)
  starting transfers between devices  5.5 us (11%)
    ppermute x4, waiting for transfers between devices, routed(): return lax.ppermute(block, AXES, pairs)  23.9 us
    ppermute x4, starting transfers between devices, routed(): return lax.ppermute(block, AXES, pairs)  5.5 us
    add x1, other arithmetic, chain(): e_b = coarse_update(e_a, w_d, inside) + d_b  2.69 us
    add x2, other arithmetic, chain(): e_a = coarse_update(v, w_d, inside) + d_a  2.61 us
    select_n x4, other arithmetic, fine_update(): return jnp.where(inside, new, 0.0)  2.46 us
    dynamic_slice x4, local copies, waits for them, and re-layouts, cut(): return lax.dynamic_slice_in_dim(field, start, size, axis=0)  2.16 us
    slice x10, local copies, waits for them, and re-layouts, neighbour_sum(): jnp.roll(field, -1, axis=1)  1.74 us
    slice x8, local copies, waits for them, and re-layouts, neighbour_sum(): jnp.roll(field, 1, axis=1)  1.41 us
  transfers between devices with their start and end apart: 4, of which 4 were waited for; matrix products, arithmetic and copies ran while one was open for 3% of the time, Pallas kernels for 0%

profile of v1, /device:TPU:0, one launch (start us, length us, event | category | flops | bytes accessed | tf_op | source)
XLA Modules:
  0.0 49.1 jit_solution(14167103615794758858)
XLA Ops:
  0.0 0.5 %collective-permute-start = (f32[64,4096]{1,0:T(8,128)}, f32[64,4096]{1,0:T(8,128)S(1)}, u32[]{:S(2)}, u32[]{:S(2)}) collective-permute-start(f32[64,4096]{1,0:T(8,128)} %bitcast.5), channel_id=1, source_target_pairs={{0,4},{1,5},{2,6},{3,7},{4,0},{5,1},{6,2},{7,3},{8,12},{9,13},{10,... | collective-permute-start | bytes 3145736 | tf_op jit(solution)/shard_map/ppermute | solution.py:25
  0.5 1.1 %constant_dynamic-slice_fusion.1 = f32[40,4096]{1,0:T(8,128)S(1)} fusion(f32[64,4096]{1,0:T(8,128)} %param.3, s32[]{:T(128)S(6)} %select_n.128), kind=kLoop, calls=%fused_computation.117 | loop fusion | bytes 1310724 | tf_op jit(solution)/shard_map/dynamic_slice | solution.py:97
  1.6 1.4 %collective-permute-done = f32[64,4096]{1,0:T(8,128)S(1)} collective-permute-done((f32[64,4096]{1,0:T(8,128)}, f32[64,4096]{1,0:T(8,128)S(1)}, u32[]{:S(2)}, u32[]{:S(2)}) %collective-permute-start) | collective-permute-done | bytes 1048608 | tf_op jit(solution)/shard_map/ppermute | solution.py:25
  3.0 0.2 broadcast_select_fusion
  3.2 0.9 %constant_dynamic-slice_fusion.3 = (f32[8,4096]{1,0:T(8,128)S(1)}, f32[8,4096]{1,0:T(8,128)S(1)}) fusion(f32[64,4096]{1,0:T(8,128)} %param.3, s32[]{:T(128)S(6)} %select_n.126, f32[64,4096]{1,0:T(8,128)S(1)} %get-tuple-element.15), kind=kLoop, calls=%fused_computation.119 | loop fusion | bytes 524292 | tf_op jit(solution)/shard_map/dynamic_slice | solution.py:97
  4.2 2.9 %collective-permute-start.1 = (f32[24,4096]{1,0:T(8,128)S(1)}, f32[24,4096]{1,0:T(8,128)S(1)}, u32[]{:S(2)}, u32[]{:S(2)}) collective-permute-start(f32[24,4096]{1,0:T(8,128)S(1)} %pad_maximum_fusion), channel_id=1, source_target_pairs={{0,8},{1,4},{2,5},{3,6},{4,1},{5,2},{6,3},{7,15},{8,0},{9,12},{10,... | collective-permute-start | bytes 1179656 | tf_op jit(solution)/shard_map/ppermute | solution.py:25
  7.2 5.7 %collective-permute-done.1 = f32[24,4096]{1,0:T(8,128)S(1)} collective-permute-done((f32[24,4096]{1,0:T(8,128)S(1)}, f32[24,4096]{1,0:T(8,128)S(1)}, u32[]{:S(2)}, u32[]{:S(2)}) %collective-permute-start.1) | collective-permute-done | bytes 393248 | tf_op jit(solution)/shard_map/ppermute | solution.py:25
  13.1 0.3 fusion.103
  13.5 0.6 %add_select_fusion = (f32[48,4096]{1,0:T(8,128)S(1)}, f32[48,4096]{1,0:T(8,128)S(1)}) fusion(f32[48,4096]{1,0:T(8,128)S(1)} %fusion.55, pred[48]{0:T(512)(128)(4,1)S(1)} %compare_and_fusion, f32[8,4096]{1,0:T(8,128)S(1)} %get-tuple-element.92, f32[40,4096]{1,0:T(8,128)S(1)} %constant_dynamic-slice_fusion.1, pred[]{:T(512)S(6)} %eq.8, ...), kind=kLoop, calls=%fused_computation.99 | loop fusion | flops 4128768 | bytes 6291505 | tf_op jit(solution)/shard_map/jit(_where)/select_n | solution.py:67
  14.3 0.3 fusion.96
  14.6 0.6 %fusion.22 = (f32[48,4096]{1,0:T(8,128)S(1)}, f32[48,4096]{1,0:T(8,128)S(1)}) fusion(f32[48,4096]{1,0:T(8,128)S(1)} %get-tuple-element.13, f32[47,4096]{1,0:T(8,128)S(1)} %get-tuple-element.46, f32[1,4096]{1,0:T(1,128)S(1)} %get-tuple-element.48, f32[1,4096]{1,0:T(1,128)S(1)} %get-tuple-element.47, f32[47,4096]{1,0:T(8,128)S(1)} %get-tuple-element.45, ...), kind=kLoop, calls=%fused_computation.32 | loop fusion | flops 4915200 | bytes 7077937 | tf_op jit(solution)/shard_map/jit(_where)/select_n | solution.py:67
  15.3 0.3 fusion.119
  15.7 0.6 %add_select_fusion.1 = (f32[48,4096]{1,0:T(8,128)S(1)}, f32[48,4096]{1,0:T(8,128)S(1)}) fusion(f32[48,4096]{1,0:T(8,128)S(1)} %get-tuple-element.95, pred[48]{0:T(512)(128)(4,1)S(1)} %compare_and_fusion, f32[8,4096]{1,0:T(8,128)S(1)} %get-tuple-element.92, f32[40,4096]{1,0:T(8,128)S(1)} %constant_dynamic-slice_fusion.1, pred[]{:T(512)S(6)} %eq.8, ...), kind=kLoop, calls=%fused_computation.100 | loop fusion | flops 4128768 | bytes 6291505 | tf_op jit(solution)/shard_map/jit(_where)/select_n | solution.py:67
  16.5 0.3 fusion.112
  16.9 0.6 %fusion.4 = f32[48,4096]{1,0:T(8,128)S(1)} fusion(f32[48,4096]{1,0:T(8,128)S(1)} %get-tuple-element.11, f32[47,4096]{1,0:T(8,128)S(1)} %get-tuple-element.78, f32[1,4096]{1,0:T(1,128)S(1)} %get-tuple-element.80, f32[1,4096]{1,0:T(1,128)S(1)} %get-tuple-element.79, f32[47,4096]{1,0:T(8,128)S(1)} %get-tuple-element.77, f32[48,4095]{1,0:T(8,128)S(1)} %get-tuple-element.74, ...), kind=kLoop, calls=%fused_computation.14 | loop fusion | flops 4128768 | bytes 5505073 | tf_op jit(solution)/shard_map/jit(_where)/select_n | solution.py:67
  17.6 0.3 fusion.111
  18.0 0.8 %fusion.79 = (f32[48,4096]{1,0:T(8,128)S(1)}, f32[48,4096]{1,0:T(8,128)S(1)}) fusion(f32[48,4096]{1,0:T(8,128)S(1)} %get-tuple-element.95, f32[48,4096]{1,0:T(8,128)S(1)} %get-tuple-element.12, pred[48]{0:T(512)(128)(4,1)S(1)} %compare_and_fusion, f32[8,4096]{1,0:T(8,128)S(1)} %get-tuple-element.92, f32[40,4096]{1,0:T(8,128)S(1)} %constant_dynamic-slice_fusion.1, ...), kind=kLoop, calls=%fused_computation.122 | loop fusion | flops 6488064 | bytes 7864369 | tf_op jit(solution)/shard_map/add | solution.py:125
  19.0 0.3 fusion.104
  19.4 0.3 fusion.95
  19.9 2.7 %fusion.17 = (f32[48,4096]{1,0:T(8,128)S(1)}, f32[48,4096]{1,0:T(8,128)}) fusion(f32[48,4096]{1,0:T(8,128)S(1)} %get-tuple-element.9, f32[47,4096]{1,0:T(8,128)S(1)} %get-tuple-element.62, f32[1,4096]{1,0:T(1,128)S(1)} %get-tuple-element.64, f32[1,4096]{1,0:T(1,128)S(1)} %get-tuple-element.63, f32[47,4096]{1,0:T(8,128)S(1)} %get-tuple-element.61, ...), kind=kLoop, calls=%fused_computation.27 | loop fusion | flops 9830400 | bytes 11796529 | tf_op jit(solution)/shard_map/add | solution.py:126
  22.5 0.9 %slice.403 = f32[36,4096]{1,0:T(8,128)} slice(f32[48,4096]{1,0:T(8,128)S(1)} %get-tuple-element.7), slice={[6:42], [0:4096]} | slice | bytes 1179648 | tf_op jit(solution)/shard_map/slice | solution.py:139
  23.5 2.0 %collective-permute-start.2 = (f32[36,4096]{1,0:T(8,128)}, f32[36,4096]{1,0:T(8,128)}, u32[]{:S(2)}, u32[]{:S(2)}) collective-permute-start(f32[36,4096]{1,0:T(8,128)} %slice.403), channel_id=1, source_target_pairs={{0,8},{1,9},{2,10},{3,11},{4,12},{5,13},{6,14},{7,15},{8,0},{9,1},... | collective-permute-start | bytes 1769480 | tf_op jit(solution)/shard_map/ppermute | solution.py:25
  25.6 15.0 %collective-permute-done.2 = f32[36,4096]{1,0:T(8,128)} collective-permute-done((f32[36,4096]{1,0:T(8,128)}, f32[36,4096]{1,0:T(8,128)}, u32[]{:S(2)}, u32[]{:S(2)}) %collective-permute-start.2) | collective-permute-done | bytes 589856 | tf_op jit(solution)/shard_map/ppermute | solution.py:25
  40.5 1.2 %pad_select_fusion = f32[48,4096]{1,0:T(8,128)S(1)} fusion(f32[36,4096]{1,0:T(8,128)} %collective-permute-done.2, pred[48]{0:T(512)(128)(4,1)S(1)} %compare_and_fusion), kind=kLoop, calls=%fused_computation.98 | loop fusion | flops 196608 | bytes 1376304 | tf_op jit(solution)/shard_map/jit(_where)/select_n | solution.py:142
  41.9 0.3 fusion.88
  42.3 1.8 %fusion.35 = f32[48,4096]{1,0:T(8,128)S(1)} fusion(f32[48,4096]{1,0:T(8,128)S(1)} %get-tuple-element.10, f32[47,4096]{1,0:T(8,128)S(1)} %get-tuple-element.30, f32[1,4096]{1,0:T(1,128)S(1)} %get-tuple-element.32, f32[1,4096]{1,0:T(1,128)S(1)} %get-tuple-element.31, f32[47,4096]{1,0:T(8,128)S(1)} %get-tuple-element.29, f32[48,4095]{1,0:T(8,128)S(1)} %get-tuple-element.26, ...), kind=kLoop, calls=%fused_computation.45 | loop fusion | flops 4325376 | bytes 6094897 | tf_op jit(solution)/shard_map/add | solution.py:125
  44.2 0.3 fusion.84
  44.6 0.6 %fusion.37 = f32[48,4096]{1,0:T(8,128)S(1)} fusion(f32[48,4096]{1,0:T(8,128)S(1)} %fusion.35, f32[47,4096]{1,0:T(8,128)S(1)} %get-tuple-element.22, f32[1,4096]{1,0:T(1,128)S(1)} %get-tuple-element.24, f32[1,4096]{1,0:T(1,128)S(1)} %get-tuple-element.23, f32[47,4096]{1,0:T(8,128)S(1)} %get-tuple-element.21, f32[48,4095]{1,0:T(8,128)S(1)} %get-tuple-element.18, ...), kind=kLoop, calls=%fused_computation.47 | loop fusion | flops 3145728 | bytes 5505025 | tf_op jit(solution)/shard_map/add | solution.py:72
  45.1 0.6 %copy-done = f32[48,4096]{1,0:T(8,128)S(1)} copy-done((f32[48,4096]{1,0:T(8,128)S(1)}, f32[48,4096]{1,0:T(8,128)}, u32[]{:S(2)}) %copy-start) | copy-done | bytes 786456
  45.7 0.2 broadcast_select_fusion.4
  46.0 1.9 %collective-permute-done.3 = f32[32,4096]{1,0:T(8,128)S(1)} collective-permute-done((f32[32,4096]{1,0:T(8,128)S(1)}, f32[32,4096]{1,0:T(8,128)S(1)}, u32[]{:S(2)}, u32[]{:S(2)}) %collective-permute-start.3) | collective-permute-done | bytes 524320 | tf_op jit(solution)/shard_map/ppermute | solution.py:25
  48.0 1.0 %maximum_bitcast_fusion = f32[1,64,4096]{2,1,0:T(8,128)} fusion(f32[32,4096]{1,0:T(8,128)S(1)} %get-tuple-element.90, f32[32,4096]{1,0:T(8,128)S(1)} %get-tuple-element.89), kind=kLoop, calls=%fused_computation.9 | loop fusion | flops 262144 | bytes 2097152 | tf_op jit(solution)/shard_map/broadcast_in_dim | solution.py:152
  (39 shorter events, 2.5 us)
Async XLA Ops:
  0.0 3.0 %copy-start.1 = (f32[1,64,4096]{2,1,0:T(8,128)S(1)}, f32[1,64,4096]{2,1,0:T(8,128)}, u32[]{:S(2)}) copy-start(f32[1,64,4096]{2,1,0:T(8,128)} %param.2) | copy-start | bytes 3145732
  0.0 3.0 %collective-permute-start = (f32[64,4096]{1,0:T(8,128)}, f32[64,4096]{1,0:T(8,128)S(1)}, u32[]{:S(2)}, u32[]{:S(2)}) collective-permute-start(f32[64,4096]{1,0:T(8,128)} %bitcast.5), channel_id=1, source_target_pairs={{0,4},{1,5},{2,6},{3,7},{4,0},{5,1},{6,2},{7,3},{8,12},{9,13},{10,... | collective-permute-start | bytes 3145736 | tf_op jit(solution)/shard_map/ppermute | solution.py:25
  4.2 8.7 %collective-permute-start.1 = (f32[24,4096]{1,0:T(8,128)S(1)}, f32[24,4096]{1,0:T(8,128)S(1)}, u32[]{:S(2)}, u32[]{:S(2)}) collective-permute-start(f32[24,4096]{1,0:T(8,128)S(1)} %pad_maximum_fusion), channel_id=1, source_target_pairs={{0,8},{1,4},{2,5},{3,6},{4,1},{5,2},{6,3},{7,15},{8,0},{9,12},{10,... | collective-permute-start | bytes 1179656 | tf_op jit(solution)/shard_map/ppermute | solution.py:25
  23.5 17.1 %collective-permute-start.2 = (f32[36,4096]{1,0:T(8,128)}, f32[36,4096]{1,0:T(8,128)}, u32[]{:S(2)}, u32[]{:S(2)}) collective-permute-start(f32[36,4096]{1,0:T(8,128)} %slice.403), channel_id=1, source_target_pairs={{0,8},{1,9},{2,10},{3,11},{4,12},{5,13},{6,14},{7,15},{8,0},{9,1},... | collective-permute-start | bytes 1769480 | tf_op jit(solution)/shard_map/ppermute | solution.py:25
  44.6 1.1 %copy-start = (f32[48,4096]{1,0:T(8,128)S(1)}, f32[48,4096]{1,0:T(8,128)}, u32[]{:S(2)}) copy-start(f32[48,4096]{1,0:T(8,128)} %get-tuple-element.8) | copy-start | bytes 2359300
  45.9 2.0 %collective-permute-start.3 = (f32[32,4096]{1,0:T(8,128)S(1)}, f32[32,4096]{1,0:T(8,128)S(1)}, u32[]{:S(2)}, u32[]{:S(2)}) collective-permute-start(f32[32,4096]{1,0:T(8,128)S(1)} %get-tuple-element.5), channel_id=1, source_target_pairs={{0,4},{1,5},{2,6},{3,7},{4,0},{5,1},{6,2},{7,3},{8,12},{9,13},{10,... | collective-permute-start | bytes 1572872 | tf_op jit(solution)/shard_map/ppermute | solution.py:25

commit v2 on v0

v2 whole, which is shorter than its diff:
```python
import functools

import jax
import jax.numpy as jnp
from jax import lax
from jax.experimental import pallas as pl
from jax.experimental.pallas import tpu as pltpu
from jax.sharding import PartitionSpec as P

FINE = 3
WIDE = 8
CUT = 4


diffusion = 2.0
step_fine = 0.1
coarse_step = FINE * step_fine
damping = 1.0 + 4.0 * diffusion * coarse_step

AXES = ("groups", "tm", "rows")


def routed(block, route):
    groups, slices, rows = (lax.axis_size(a) for a in AXES)
    pairs = []
    for g in range(groups):
        for t in range(slices):
            for r in range(rows):
                to_g, to_t, to_r = route(g, t, r)
                source = (g * slices + t) * rows + r
                pairs.append((source, (to_g * slices + to_t) * rows + to_r))
    return lax.ppermute(block, AXES, pairs)


def partner(g, t, r):
    return g, t ^ 1, r


def outward(groups, rows):
    def route(g, t, r):
        to_r = r + 1 if t & 1 else r - 1
        if 0 <= to_r < rows:
            return g, t ^ 1, to_r
        other = g ^ 1
        return (other, t, r) if other < groups else (g, t, r)

    return route


def stage_swap(stage):
    def route(g, t, r):
        chip = t // 2
        if chip == stage:
            return g, t + 2, r
        if chip == stage + 1:
            return g, t - 2, r
        return g, t, r

    return route


def around(v):
    height, width = v.shape
    return (pltpu.roll(v, 1, 0) + pltpu.roll(v, height - 1, 0)) + (
        pltpu.roll(v, 1, 1) + pltpu.roll(v, width - 1, 1)
    )


def fine_of(v, nsum, drive):
    return (
        step_fine * diffusion * nsum
        + v * ((1.0 + step_fine - 4.0 * step_fine * diffusion) - step_fine * (v * v))
        + step_fine * drive
    )


def coarse_of(v, nsum, drive):
    scale = coarse_step / damping
    return (
        scale * diffusion * nsum
        + v * ((1.0 + coarse_step) / damping - scale * (v * v))
        + scale * drive
    )


def compute(kernel, outs, args, **kwargs):
    shapes = [jax.ShapeDtypeStruct(o, jnp.float32) for o in outs]
    vmem = pl.BlockSpec(memory_space=pltpu.VMEM)
    return pl.pallas_call(
        kernel,
        out_shape=shapes,
        in_specs=[vmem] * len(args),
        out_specs=[vmem] * len(outs),
        compiler_params=pltpu.CompilerParams(vmem_limit_bytes=12 << 20),
        **kwargs,
    )(*args)


def first_pass(a, b, drive, inside=None):
    def kept(v):
        return v if inside is None else jnp.where(inside, v, 0.0)

    def delta(v):
        nsum = around(v)
        coarse = coarse_of(v, nsum, drive)
        fine = kept(fine_of(v, nsum, drive))
        for _ in range(FINE - 1):
            fine = kept(fine_of(fine, around(fine), drive))
        return kept(coarse), kept(fine - coarse)

    coarse_a, d_a = delta(a)
    _, d_b = delta(b)
    e_a = coarse_a + d_a
    e_b = kept(coarse_of(e_a, around(e_a), drive) + d_b)
    return d_a, d_b, e_b


def chain(current, d_a, d_b, drive, inside=None):
    e_a = coarse_of(current, around(current), drive) + d_a
    if inside is not None:
        e_a = jnp.where(inside, e_a, 0.0)
    e_b = coarse_of(e_a, around(e_a), drive) + d_b
    return e_a, e_b


def picked(first, own, other):
    return jnp.where(first, own, other), jnp.where(first, other, own)


def tiles(ref, kind, start, count):
    height = ref.shape[0] // 4
    return ref[pl.ds(kind * height + 8 * start, 8 * count), :]


def put(ref, kind, start, value):
    height = ref.shape[0] // 4
    ref[pl.ds(kind * height + 8 * start, value.shape[0]), :] = value


def mixed(upper, lower):
    row = lax.broadcasted_iota(jnp.int32, upper.shape, 0)
    return jnp.where(row < CUT, upper, lower)


def inner_kernel(half, own, other, drive, sent, state, edge):
    core = lax.axis_index("tm") % 2
    first = core == 0
    height = 2 * half
    row = pl.multiple_of(half - 16 + 8 * core, 8)
    a, b = picked(first, own[pl.ds(row, 24), :], other[pl.ds(row, 24), :])
    d = drive[pl.ds(row, 24), :]
    d_a, d_b, e_b = first_pass(a, b, d)
    sent[...] = pltpu.roll(e_b, 24 - CUT, 0)[:16]
    for kind, v in enumerate((d_a, d_b, d, a)):
        put(state, kind, 0, v)
    row = pl.multiple_of((height - WIDE) * core, 8)
    a, b = picked(first, own[pl.ds(row, 8), :], other[pl.ds(row, 8), :])
    edge[0:8, :] = a
    edge[8:16, :] = b
    edge[16:24, :] = drive[pl.ds(row, 8), :]


def middle_kernel(half, own, other, drive, inner, sent, state):
    core = lax.axis_index("tm") % 2
    first = core == 0
    row = pl.multiple_of((half + 8) * core, 8)
    a, b = picked(first, own[pl.ds(row, 24), :], other[pl.ds(row, 24), :])
    d = drive[pl.ds(row, 24), :]
    d_a, d_b, e_b = first_pass(a, b, d)
    sent[...] = pltpu.roll(e_b, 24 - CUT, 0)[:16]
    fields = (d_a, d_b, d, a)

    @pl.when(first)
    def _():
        for kind, v in enumerate(fields):
            put(state, kind, 0, v[:16])
            put(state, kind, 2, mixed(v[16:], tiles(inner, kind, 0, 1)))
            put(state, kind, 3, tiles(inner, kind, 1, 1))

    @pl.when(core == 1)
    def _():
        for kind, v in enumerate(fields):
            put(state, kind, 0, tiles(inner, kind, 1, 1))
            put(state, kind, 1, mixed(tiles(inner, kind, 2, 1), v[:8]))
            put(state, kind, 2, v[8:])


def at_edge(core):
    r, rows = lax.axis_index("rows"), lax.axis_size("rows")
    return ((core == 0) & (r == 0)) | ((core == 1) & (r == rows - 1))


def outer_kernel(half, own, other, drive, got, middle, sent, state):
    core = lax.axis_index("tm") % 2
    first = core == 0
    height = 2 * half
    row = pl.multiple_of((height - WIDE) * core, 8)
    a, b = picked(first, own[pl.ds(row, 8), :], other[pl.ds(row, 8), :])
    near = (a, b, drive[pl.ds(row, 8), :])
    far = [got[8 * i : 8 * i + 8, :] for i in range(3)]
    upper = [jnp.where(first, f, n) for f, n in zip(far, near)]
    lower = [jnp.where(first, n, f) for f, n in zip(far, near)]
    a, b, d = (jnp.concatenate(p) for p in zip(upper, lower))
    tile = lax.broadcasted_iota(jnp.int32, a.shape, 0) // 8
    inside = ~(at_edge(core) & (tile == core))
    a, b = jnp.where(inside, a, 0.0), jnp.where(inside, b, 0.0)
    d_a, d_b, e_b = first_pass(a, b, d, inside)
    sent[...] = pltpu.roll(e_b, 16 - CUT, 0)[:8]
    fields = (d_a, d_b, d, a)

    @pl.when(first)
    def _():
        for kind, v in enumerate(fields):
            put(state, kind, 0, v[:8])
            put(state, kind, 1, mixed(v[8:], tiles(middle, kind, 0, 1)))
            put(state, kind, 2, tiles(middle, kind, 1, 1))

    @pl.when(core == 1)
    def _():
        for kind, v in enumerate(fields):
            put(state, kind, 0, tiles(middle, kind, 2, 1))
            put(state, kind, 1, mixed(tiles(middle, kind, 3, 1), v[:8]))
            put(state, kind, 2, v[8:])


def finish(current, state, low, high, keep, send, inside=None):
    first = lax.axis_index("tm") % 2 == 0
    count = state.shape[0] // 32
    chip = lax.axis_index("tm") // 2
    d_a, d_b, d, a = (tiles(state, kind, 0, count) for kind in range(4))
    current = jnp.where(chip == 0, a, current)
    e_a, e_b = chain(current, d_a, d_b, d, inside)
    kept, sent = picked(first, e_a[low:high], e_b[low:high])
    keep[...] = kept
    send[...] = sent


def inner_end(arrived, state, keep, send):
    v = arrived[...]
    current = pltpu.roll(jnp.concatenate([v, v[:8]]), CUT, 0)
    finish(current, state, 8, 16, keep, send)


def middle_end(inner, middle, state, keep, send, current):
    core = lax.axis_index("tm") % 2

    @pl.when(core == 0)
    def _():
        current[...] = pltpu.roll(jnp.concatenate([middle[...], inner[...]]), CUT, 0)

    @pl.when(core == 1)
    def _():
        current[...] = pltpu.roll(jnp.concatenate([inner[...], middle[...]]), 32 - CUT, 0)

    finish(current[...], state, 8, 24, keep, send)


def outer_end(middle, outer, state, keep, send, current):
    core = lax.axis_index("tm") % 2

    @pl.when(core == 0)
    def _():
        current[...] = pltpu.roll(jnp.concatenate([outer[...], middle[...]]), CUT, 0)

    @pl.when(core == 1)
    def _():
        current[...] = pltpu.roll(jnp.concatenate([middle[...], outer[...]]), 24 - CUT, 0)

    tile = lax.broadcasted_iota(jnp.int32, current.shape, 0) // 8
    inside = ~(at_edge(core) & (tile == 2 * core))
    finish(current[...], state, 8, 16, keep, send, inside)


def joined_kernel(half, *refs):
    pieces, out, sems = refs[:6], refs[6], refs[7]
    core = lax.axis_index("tm") % 2
    copies = []
    for i, piece in enumerate(pieces):
        upper = (half - 8, 8, 0)[i % 3]
        lower = (half, half + 8, 2 * half - 8)[i % 3]
        where_upper = core == 0 if i < 3 else core == 1
        row = pl.multiple_of(jnp.where(where_upper, upper, lower), 8)
        copy = pltpu.make_async_copy(
            piece, out.at[0, pl.ds(row, piece.shape[0]), :], sems.at[i]
        )
        copy.start()
        copies.append(copy)
    for copy in copies:
        copy.wait()


def after(value, earlier):
    return lax.optimization_barrier((value, earlier))[0]


def masked_update(update, v, drive, inside):
    wide = (
        jnp.roll(v, 1, axis=0) + jnp.roll(v, -1, axis=0)
    ) + (jnp.roll(v, 1, axis=1) + jnp.roll(v, -1, axis=1))
    return jnp.where(inside, update(v, wide, drive), 0.0)


def long_chain(own, drive):
    height = own.shape[0]
    half = height // 2
    groups, slices, rows = (lax.axis_size(a) for a in AXES)
    t, r = lax.axis_index("tm"), lax.axis_index("rows")
    core, chip = t % 2, t // 2
    first = core == 0
    away = outward(groups, rows)

    def cut(field, start, size):
        return lax.dynamic_slice_in_dim(field, start, size, axis=0)

    other = routed(own, partner)
    s_a, s_b = picked(first, own, other)
    edge = core * (height - WIDE)
    got = routed(jnp.concatenate([cut(f, edge, WIDE) for f in (s_a, s_b, drive)]), away)

    def sided(body, outer, inner):
        return jnp.where(
            first,
            jnp.concatenate([outer, body, inner]),
            jnp.concatenate([inner, body, outer]),
        )

    def window(field, place):
        body = cut(field, core * half, half)
        inner = cut(field, jnp.where(first, half, half - WIDE), WIDE)
        return sided(body, got[place * WIDE : (place + 1) * WIDE], inner)

    w_a, w_b, w_d = (window(f, i) for i, f in enumerate((s_a, s_b, drive)))
    row = lax.broadcasted_iota(jnp.int32, (half + 2 * WIDE, 1), 0)
    row = row + r * height + core * half - WIDE
    inside = (row >= 0) & (row < rows * height)
    w_a, w_b = jnp.where(inside, w_a, 0.0), jnp.where(inside, w_b, 0.0)

    def delta(v):
        fine = v
        for _ in range(FINE):
            fine = masked_update(fine_of, fine, w_d, inside)
        return fine - masked_update(coarse_of, v, w_d, inside)

    d_a, d_b = delta(w_a), delta(w_b)

    def both(v):
        e_a = masked_update(coarse_of, v, w_d, inside) + d_a
        return e_a, masked_update(coarse_of, e_a, w_d, inside) + d_b

    def extended(v):
        last = WIDE + half - 2
        inner = routed(cut(v, jnp.where(first, last, WIDE), 2), partner)
        outer = routed(cut(v, jnp.where(first, WIDE, last), 2), away)
        return sided(v[WIDE : WIDE + half], outer, inner)

    e_a, e_b = both(w_a)
    for stage in range(slices // 2 - 1):
        moved = e_b[WIDE - 2 : WIDE + half + 2] if stage == 0 else extended(e_b)
        arrived = routed(moved, stage_swap(stage))
        current = jnp.pad(arrived, ((WIDE - 2, WIDE - 2), (0, 0)))
        n_a, n_b = both(jnp.where(inside, current, 0.0))
        here = chip == stage + 1
        e_a, e_b = jnp.where(here, n_a, e_a), jnp.where(here, n_b, e_b)

    kept, sent = picked(first, e_a[WIDE : WIDE + half], e_b[WIDE : WIDE + half])
    back = routed(sent, partner)
    return jnp.concatenate(picked(first, kept, back))[None]


def on_device(starts, drive):
    own = starts[0]
    if lax.axis_size("tm") != 4:
        return long_chain(own, drive)
    height, width = own.shape
    half = height // 2
    groups, rows = lax.axis_size("groups"), lax.axis_size("rows")

    other = routed(own, partner)
    sent_1, state_1, edge = compute(
        functools.partial(inner_kernel, half),
        [(16, width), (4 * 24, width), (24, width)],
        (own, other, drive),
        name="inner",
    )
    here_1 = routed(sent_1, stage_swap(0))
    got = routed(edge, outward(groups, rows))
    sent_2, state_2 = compute(
        functools.partial(middle_kernel, half),
        [(16, width), (4 * 32, width)],
        (own, other, drive, state_1),
        name="middle",
    )
    here_2 = routed(sent_2, stage_swap(0))
    sent_3, state_3 = compute(
        functools.partial(outer_kernel, half),
        [(8, width), (4 * 24, width)],
        (own, other, drive, got, state_2),
        name="outer",
    )
    here_3 = routed(sent_3, stage_swap(0))

    keep_1, send_1 = compute(
        inner_end, [(8, width)] * 2, (here_1, after(state_1, sent_3)), name="inner_end"
    )
    back_1 = routed(send_1, partner)
    keep_2, send_2 = compute(
        middle_end,
        [(16, width)] * 2,
        (here_1, here_2, state_2),
        scratch_shapes=[pltpu.VMEM((32, width), jnp.float32)],
        name="middle_end",
    )
    back_2 = routed(send_2, partner)
    keep_3, send_3 = compute(
        outer_end,
        [(8, width)] * 2,
        (here_2, here_3, state_3),
        scratch_shapes=[pltpu.VMEM((24, width), jnp.float32)],
        name="outer_end",
    )
    back_3 = routed(send_3, partner)
    pieces = (keep_1, keep_2, keep_3, back_1, back_2, back_3)
    return pl.pallas_call(
        functools.partial(joined_kernel, half),
        out_shape=jax.ShapeDtypeStruct((1, height, width), jnp.float32),
        in_specs=[pl.BlockSpec(memory_space=pltpu.VMEM)] * 6,
        out_specs=pl.BlockSpec(memory_space=pl.ANY),
        scratch_shapes=[pltpu.SemaphoreType.DMA((6,))],
        compiler_params=pltpu.CompilerParams(vmem_limit_bytes=12 << 20),
        name="joined",
    )(*pieces)


def solution(mesh):
    in_specs = (P(("groups", "tm"), "rows", None), P("rows", None))
    out_specs = P(("groups", "tm"), "rows", None)
    return jax.shard_map(
        on_device, mesh=mesh, in_specs=in_specs, out_specs=out_specs, check_vma=False
    )
```

time: 133 us -> 30.4 us (0.23)
  the two profiles are of different devices: /device:TPU:2 before, /device:TPU:0 now
where the time goes in v2:
time: 30.4 us; the launch traced here: 30.2 us
  waiting for transfers between devices  10.9 us (36%)
  Pallas kernels  8.48 us (28%)
  starting transfers between devices  8.27 us (27%)
  local copies, waits for them, and re-layouts  2.45 us (8%)
    ppermute x8, waiting for transfers between devices, routed(): return lax.ppermute(block, AXES, pairs)  10.9 us
    ppermute x8, starting transfers between devices, routed(): return lax.ppermute(block, AXES, pairs)  8.27 us
    pallas_call x6, Pallas kernels, compute(): pl.pallas_call(kernel, out_shape=shapes, in_specs=[vmem] * len(args), out...  7.47 us
    unnamed x4, local copies, waits for them, and re-layouts  2.45 us
    pallas_call x1, Pallas kernels, on_device(): pl.pallas_call(functools.partial(joined_kernel, half), out_shape=jax.Shap...  1.01 us
  transfers between devices with their start and end apart: 8, of which 6 were waited for; matrix products, arithmetic and copies ran while one was open for 0% of the time, Pallas kernels for 18%

profile of v2, /device:TPU:0, one launch (start us, length us, event | category | flops | bytes accessed | tf_op | source)
XLA Modules:
  0.0 30.2 jit_solution(408561807136849029)
XLA Ops:
  0.0 0.5 %collective-permute-start = (f32[64,4096]{1,0:T(8,128)}, f32[64,4096]{1,0:T(8,128)S(1)}, u32[]{:S(2)}, u32[]{:S(2)}) collective-permute-start(f32[64,4096]{1,0:T(8,128)} %bitcast.1), channel_id=1, source_target_pairs={{0,4},{1,5},{2,6},{3,7},{4,0},{5,1},{6,2},{7,3},{8,12},{9,13},{10,... | collective-permute-start | bytes 3145736 | tf_op jit(solution)/shard_map/ppermute | solution.py:32
  0.5 2.5 %collective-permute-done.other = f32[64,4096]{1,0:T(8,128)S(1)} collective-permute-done((f32[64,4096]{1,0:T(8,128)}, f32[64,4096]{1,0:T(8,128)S(1)}, u32[]{:S(2)}, u32[]{:S(2)}) %collective-permute-start) | collective-permute-done | bytes 1048608 | tf_op jit(solution)/shard_map/ppermute | solution.py:32
  3.0 0.0 copy-start
  3.0 1.2 %copy-done = f32[1,64,4096]{2,1,0:T(8,128)S(1)} copy-done((f32[1,64,4096]{2,1,0:T(8,128)S(1)}, f32[1,64,4096]{2,1,0:T(8,128)}, u32[]{:S(2)}) %copy-start) | copy-done | bytes 1048600
  4.2 0.0 copy-start.1
  4.2 1.2 %copy-done.1 = f32[64,4096]{1,0:T(8,128)S(1)} copy-done((f32[64,4096]{1,0:T(8,128)S(1)}, f32[64,4096]{1,0:T(8,128)}, u32[]{:S(2)}) %copy-start.1) | copy-done | bytes 1048600
  5.4 2.1 %inner.1 = (f32[16,4096]{1,0:T(8,128)S(1)}, f32[96,4096]{1,0:T(8,128)S(1)}, f32[24,4096]{1,0:T(8,128)S(1)}) custom-call(f32[64,4096]{1,0:T(8,128)S(1)} %bitcast.2, f32[64,4096]{1,0:T(8,128)S(1)} %collective-permute-done.other, f32[64,4096]{1,0:T(8,128)S(1)} %copy-done.1), custom_call_target="tpu_custom_call" | custom-call | tf_op jit(solution)/shard_map/inner/pallas_call | solution.py:89
  7.5 2.9 %collective-permute-start.2 = (f32[24,4096]{1,0:T(8,128)S(1)}, f32[24,4096]{1,0:T(8,128)S(1)}, u32[]{:S(2)}, u32[]{:S(2)}) collective-permute-start(f32[24,4096]{1,0:T(8,128)S(1)} %get-tuple-element.21), channel_id=1, source_target_pairs={{0,16},{1,4},{2,5},{3,6},{4,1},{5,2},{6,3},{7,23},{8,24},{9,12},{1... | collective-permute-start | bytes 1179656 | tf_op jit(solution)/shard_map/ppermute | solution.py:32
  10.5 1.5 %collective-permute-start.1 = (f32[16,4096]{1,0:T(8,128)S(1)}, f32[16,4096]{1,0:T(8,128)S(1)}, u32[]{:S(2)}, u32[]{:S(2)}) collective-permute-start(f32[16,4096]{1,0:T(8,128)S(1)} %get-tuple-element.19), channel_id=1, source_target_pairs={{0,8},{1,9},{2,10},{3,11},{4,12},{5,13},{6,14},{7,15},{8,0},{9,1},... | collective-permute-start | bytes 786440 | tf_op jit(solution)/shard_map/ppermute | solution.py:32
  11.9 2.2 %middle.1 = (f32[16,4096]{1,0:T(8,128)S(1)}, f32[128,4096]{1,0:T(8,128)S(1)}) custom-call(f32[64,4096]{1,0:T(8,128)S(1)} %bitcast.3, f32[64,4096]{1,0:T(8,128)S(1)} %collective-permute-done.other, f32[64,4096]{1,0:T(8,128)S(1)} %copy-done.1, f32[96,4096]{1,0:T(8,128)S(1)} %get-tuple-element.24.inner.state), custom_call_target="tpu_custom_call" | custom-call | tf_op jit(solution)/shard_map/middle/pallas_call | solution.py:89
  14.1 0.6 %collective-permute-start.3 = (f32[16,4096]{1,0:T(8,128)S(1)}, f32[16,4096]{1,0:T(8,128)S(1)}, u32[]{:S(2)}, u32[]{:S(2)}) collective-permute-start(f32[16,4096]{1,0:T(8,128)S(1)} %get-tuple-element.26), channel_id=1, source_target_pairs={{0,8},{1,9},{2,10},{3,11},{4,12},{5,13},{6,14},{7,15},{8,0},{9,1},... | collective-permute-start | bytes 786440 | tf_op jit(solution)/shard_map/ppermute | solution.py:32
  14.7 1.5 %collective-permute-done.2.got = f32[24,4096]{1,0:T(8,128)S(1)} collective-permute-done((f32[24,4096]{1,0:T(8,128)S(1)}, f32[24,4096]{1,0:T(8,128)S(1)}, u32[]{:S(2)}, u32[]{:S(2)}) %collective-permute-start.2) | collective-permute-done | bytes 393248 | tf_op jit(solution)/shard_map/ppermute | solution.py:32
  16.2 1.5 %outer.1 = (f32[8,4096]{1,0:T(8,128)S(1)}, f32[96,4096]{1,0:T(8,128)S(1)}) custom-call(f32[64,4096]{1,0:T(8,128)S(1)} %bitcast.4, f32[64,4096]{1,0:T(8,128)S(1)} %collective-permute-done.other, f32[64,4096]{1,0:T(8,128)S(1)} %copy-done.1, f32[24,4096]{1,0:T(8,128)S(1)} %collective-permute-done.2.got, f32[128,4096]{1,0:T(8,128)S(1)} %get-tuple-element.22.middle.state), custom_call_target="tpu_custom_call" | custom-call | tf_op jit(solution)/shard_map/outer/pallas_call | solution.py:89
  17.8 2.1 %collective-permute-start.4 = (f32[8,4096]{1,0:T(8,128)S(1)}, f32[8,4096]{1,0:T(8,128)S(1)}, u32[]{:S(2)}, u32[]{:S(2)}) collective-permute-start(f32[8,4096]{1,0:T(8,128)S(1)} %get-tuple-element.23), channel_id=1, source_target_pairs={{0,8},{1,9},{2,10},{3,11},{4,12},{5,13},{6,14},{7,15},{8,0},{9,1},... | collective-permute-start | bytes 393224 | tf_op jit(solution)/shard_map/ppermute | solution.py:32
  19.8 0.0 collective-permute-done.1.arrived.inner
  19.8 5.4 %collective-permute-done.3.middle = f32[16,4096]{1,0:T(8,128)S(1)} collective-permute-done((f32[16,4096]{1,0:T(8,128)S(1)}, f32[16,4096]{1,0:T(8,128)S(1)}, u32[]{:S(2)}, u32[]{:S(2)}) %collective-permute-start.3) | collective-permute-done | bytes 262176 | tf_op jit(solution)/shard_map/ppermute | solution.py:32
  25.2 0.7 %middle_end.1 = (f32[16,4096]{1,0:T(8,128)S(1)}, f32[16,4096]{1,0:T(8,128)S(1)}) custom-call(f32[16,4096]{1,0:T(8,128)S(1)} %collective-permute-done.1.arrived.inner, f32[16,4096]{1,0:T(8,128)S(1)} %collective-permute-done.3.middle, f32[128,4096]{1,0:T(8,128)S(1)} %get-tuple-element.22.middle.state), custom_call_target="tpu_custom_call" | custom-call | tf_op jit(solution)/shard_map/middle_end/pallas_call | solution.py:89
  26.0 0.1 collective-permute-start.6
  26.1 0.5 %inner_end.1 = (f32[8,4096]{1,0:T(8,128)S(1)}, f32[8,4096]{1,0:T(8,128)S(1)}) custom-call(f32[16,4096]{1,0:T(8,128)S(1)} %collective-permute-done.1.arrived.inner, f32[96,4096]{1,0:T(8,128)S(1)} %get-tuple-element.24.inner.state), custom_call_target="tpu_custom_call" | custom-call | tf_op jit(solution)/shard_map/inner_end/pallas_call | solution.py:89
  26.5 0.6 %collective-permute-start.5 = (f32[8,4096]{1,0:T(8,128)S(1)}, f32[8,4096]{1,0:T(8,128)S(1)}, u32[]{:S(2)}, u32[]{:S(2)}) collective-permute-start(f32[8,4096]{1,0:T(8,128)S(1)} %get-tuple-element.30), channel_id=1, source_target_pairs={{0,4},{1,5},{2,6},{3,7},{4,0},{5,1},{6,2},{7,3},{8,12},{9,13},{10,... | collective-permute-start | bytes 393224 | tf_op jit(solution)/shard_map/ppermute | solution.py:32
  27.1 0.2 collective-permute-done.4.outer
  27.3 0.5 %outer_end.1 = (f32[8,4096]{1,0:T(8,128)S(1)}, f32[8,4096]{1,0:T(8,128)S(1)}) custom-call(f32[16,4096]{1,0:T(8,128)S(1)} %collective-permute-done.3.middle, f32[8,4096]{1,0:T(8,128)S(1)} %collective-permute-done.4.outer, f32[96,4096]{1,0:T(8,128)S(1)} %get-tuple-element.28.state), custom_call_target="tpu_custom_call" | custom-call | tf_op jit(solution)/shard_map/outer_end/pallas_call | solution.py:89
  27.8 0.1 collective-permute-start.7
  27.9 0.2 collective-permute-done.5.refs_3_
  28.1 0.0 collective-permute-done.6.refs_4_
  28.1 1.1 %collective-permute-done.7.refs_5_ = f32[8,4096]{1,0:T(8,128)S(1)} collective-permute-done((f32[8,4096]{1,0:T(8,128)S(1)}, f32[8,4096]{1,0:T(8,128)S(1)}, u32[]{:S(2)}, u32[]{:S(2)}) %collective-permute-start.7) | collective-permute-done | bytes 131104 | tf_op jit(solution)/shard_map/ppermute | solution.py:32
  29.2 1.0 %joined.1 = f32[1,64,4096]{2,1,0:T(8,128)} custom-call(f32[8,4096]{1,0:T(8,128)S(1)} %get-tuple-element.25.refs_0_, f32[16,4096]{1,0:T(8,128)S(1)} %get-tuple-element.27.refs_1_, f32[8,4096]{1,0:T(8,128)S(1)} %get-tuple-element.29.refs_2_, f32[8,4096]{1,0:T(8,128)S(1)} %collective-permute-done.5.refs_3_, f32[16,4096]{1,0:T(8,128)S(1)} %collective-permute-done.6.refs_4_, ...), custom_call_target="tpu_custom_call" | custom-call | tf_op jit(solution)/shard_map/joined/pallas_call | solution.py:423
Async XLA Ops:
  0.0 3.0 %collective-permute-start = (f32[64,4096]{1,0:T(8,128)}, f32[64,4096]{1,0:T(8,128)S(1)}, u32[]{:S(2)}, u32[]{:S(2)}) collective-permute-start(f32[64,4096]{1,0:T(8,128)} %bitcast.1), channel_id=1, source_target_pairs={{0,4},{1,5},{2,6},{3,7},{4,0},{5,1},{6,2},{7,3},{8,12},{9,13},{10,... | collective-permute-start | bytes 3145736 | tf_op jit(solution)/shard_map/ppermute | solution.py:32
  3.0 1.2 %copy-start = (f32[1,64,4096]{2,1,0:T(8,128)S(1)}, f32[1,64,4096]{2,1,0:T(8,128)}, u32[]{:S(2)}) copy-start(f32[1,64,4096]{2,1,0:T(8,128)} %param.2) | copy-start | bytes 3145732
  4.2 1.2 %copy-start.1 = (f32[64,4096]{1,0:T(8,128)S(1)}, f32[64,4096]{1,0:T(8,128)}, u32[]{:S(2)}) copy-start(f32[64,4096]{1,0:T(8,128)} %drive.5) | copy-start | bytes 3145732
  7.5 8.7 %collective-permute-start.2 = (f32[24,4096]{1,0:T(8,128)S(1)}, f32[24,4096]{1,0:T(8,128)S(1)}, u32[]{:S(2)}, u32[]{:S(2)}) collective-permute-start(f32[24,4096]{1,0:T(8,128)S(1)} %get-tuple-element.21), channel_id=1, source_target_pairs={{0,16},{1,4},{2,5},{3,6},{4,1},{5,2},{6,3},{7,23},{8,24},{9,12},{1... | collective-permute-start | bytes 1179656 | tf_op jit(solution)/shard_map/ppermute | solution.py:32
  10.5 9.4 %collective-permute-start.1 = (f32[16,4096]{1,0:T(8,128)S(1)}, f32[16,4096]{1,0:T(8,128)S(1)}, u32[]{:S(2)}, u32[]{:S(2)}) collective-permute-start(f32[16,4096]{1,0:T(8,128)S(1)} %get-tuple-element.19), channel_id=1, source_target_pairs={{0,8},{1,9},{2,10},{3,11},{4,12},{5,13},{6,14},{7,15},{8,0},{9,1},... | collective-permute-start | bytes 786440 | tf_op jit(solution)/shard_map/ppermute | solution.py:32
  14.1 11.1 %collective-permute-start.3 = (f32[16,4096]{1,0:T(8,128)S(1)}, f32[16,4096]{1,0:T(8,128)S(1)}, u32[]{:S(2)}, u32[]{:S(2)}) collective-permute-start(f32[16,4096]{1,0:T(8,128)S(1)} %get-tuple-element.26), channel_id=1, source_target_pairs={{0,8},{1,9},{2,10},{3,11},{4,12},{5,13},{6,14},{7,15},{8,0},{9,1},... | collective-permute-start | bytes 786440 | tf_op jit(solution)/shard_map/ppermute | solution.py:32
  17.8 9.5 %collective-permute-start.4 = (f32[8,4096]{1,0:T(8,128)S(1)}, f32[8,4096]{1,0:T(8,128)S(1)}, u32[]{:S(2)}, u32[]{:S(2)}) collective-permute-start(f32[8,4096]{1,0:T(8,128)S(1)} %get-tuple-element.23), channel_id=1, source_target_pairs={{0,8},{1,9},{2,10},{3,11},{4,12},{5,13},{6,14},{7,15},{8,0},{9,1},... | collective-permute-start | bytes 393224 | tf_op jit(solution)/shard_map/ppermute | solution.py:32
  26.0 2.1 %collective-permute-start.6 = (f32[16,4096]{1,0:T(8,128)S(1)}, f32[16,4096]{1,0:T(8,128)S(1)}, u32[]{:S(2)}, u32[]{:S(2)}) collective-permute-start(f32[16,4096]{1,0:T(8,128)S(1)} %get-tuple-element.31), channel_id=1, source_target_pairs={{0,4},{1,5},{2,6},{3,7},{4,0},{5,1},{6,2},{7,3},{8,12},{9,13},{10,... | collective-permute-start | bytes 786440 | tf_op jit(solution)/shard_map/ppermute | solution.py:32
  26.5 1.5 %collective-permute-start.5 = (f32[8,4096]{1,0:T(8,128)S(1)}, f32[8,4096]{1,0:T(8,128)S(1)}, u32[]{:S(2)}, u32[]{:S(2)}) collective-permute-start(f32[8,4096]{1,0:T(8,128)S(1)} %get-tuple-element.30), channel_id=1, source_target_pairs={{0,4},{1,5},{2,6},{3,7},{4,0},{5,1},{6,2},{7,3},{8,12},{9,13},{10,... | collective-permute-start | bytes 393224 | tf_op jit(solution)/shard_map/ppermute | solution.py:32
  27.8 1.4 %collective-permute-start.7 = (f32[8,4096]{1,0:T(8,128)S(1)}, f32[8,4096]{1,0:T(8,128)S(1)}, u32[]{:S(2)}, u32[]{:S(2)}) collective-permute-start(f32[8,4096]{1,0:T(8,128)S(1)} %get-tuple-element.32), channel_id=1, source_target_pairs={{0,4},{1,5},{2,6},{3,7},{4,0},{5,1},{6,2},{7,3},{8,12},{9,13},{10,... | collective-permute-start | bytes 393224 | tf_op jit(solution)/shard_map/ppermute | solution.py:32

commit v3 on v2

v3 whole, which is shorter than its diff:
```python
import functools

import jax
import jax.numpy as jnp
from jax import lax
from jax.experimental import pallas as pl
from jax.experimental.pallas import tpu as pltpu
from jax.sharding import PartitionSpec as P


FINE = 3
WIDE = 8
CUT = 4


diffusion = 2.0
step_fine = 0.1
coarse_step = FINE * step_fine
damping = 1.0 + 4.0 * diffusion * coarse_step

AXES = ("groups", "tm", "rows")


def routed(block, route):
    groups, slices, rows = (lax.axis_size(a) for a in AXES)
    pairs = []
    for g in range(groups):
        for t in range(slices):
            for r in range(rows):
                to_g, to_t, to_r = route(g, t, r)
                source = (g * slices + t) * rows + r
                pairs.append((source, (to_g * slices + to_t) * rows + to_r))
    return lax.ppermute(block, AXES, pairs)


def partner(g, t, r):
    return g, t ^ 1, r


def outward(groups, rows):
    def route(g, t, r):
        to_r = r + 1 if t & 1 else r - 1
        if 0 <= to_r < rows:
            return g, t ^ 1, to_r
        other = g ^ 1
        return (other, t, r) if other < groups else (g, t, r)

    return route


def stage_swap(stage):
    def route(g, t, r):
        chip = t // 2
        if chip == stage:
            return g, t + 2, r
        if chip == stage + 1:
            return g, t - 2, r
        return g, t, r

    return route


def around(v):
    height, width = v.shape
    return (pltpu.roll(v, 1, 0) + pltpu.roll(v, height - 1, 0)) + (
        pltpu.roll(v, 1, 1) + pltpu.roll(v, width - 1, 1)
    )


def fine_of(v, nsum, drive):
    return (
        step_fine * diffusion * nsum
        + v * ((1.0 + step_fine - 4.0 * step_fine * diffusion) - step_fine * (v * v))
        + step_fine * drive
    )


def coarse_of(v, nsum, drive):
    scale = coarse_step / damping
    return (
        scale * diffusion * nsum
        + v * ((1.0 + coarse_step) / damping - scale * (v * v))
        + scale * drive
    )


def compute(kernel, outs, args, **kwargs):
    shapes = [jax.ShapeDtypeStruct(o, jnp.float32) for o in outs]
    vmem = pl.BlockSpec(memory_space=pltpu.VMEM)
    return pl.pallas_call(
        kernel,
        out_shape=shapes,
        in_specs=[vmem] * len(args),
        out_specs=[vmem] * len(outs),
        compiler_params=pltpu.CompilerParams(vmem_limit_bytes=16 << 20),
        **kwargs,
    )(*args)


def same(v):
    return v


def start_of(v, drive, kept=same):
    nsum = around(v)
    coarse = kept(coarse_of(v, nsum, drive))
    fine = kept(fine_of(v, nsum, drive))
    for _ in range(FINE - 1):
        fine = kept(fine_of(fine, around(fine), drive))
    return fine, coarse


def ends_of(first, mine, theirs, drive, kept=same):
    f_a, f_b = picked(first, mine[0], theirs[0])
    g_a, g_b = picked(first, mine[1], theirs[1])
    e_a = g_a + (f_a - g_a)
    e_b = kept(coarse_of(e_a, around(e_a), drive)) + (f_b - g_b)
    return e_a, e_b


def chain(current, d_a, d_b, drive, kept=same):
    e_a = kept(coarse_of(current, around(current), drive)) + d_a
    e_b = kept(coarse_of(e_a, around(e_a), drive)) + d_b
    return e_a, e_b


def picked(first, own, other):
    return jnp.where(first, own, other), jnp.where(first, other, own)


def field(ref, kind, kinds, start, size):
    height = ref.shape[0] // kinds
    return ref.at[pl.ds(pl.multiple_of(kind * height + start, 8), size), :]


def mixed(upper, lower):
    row = lax.broadcasted_iota(jnp.int32, upper.shape, 0)
    return jnp.where(row < CUT, upper, lower)


def place():
    t = lax.axis_index("tm")
    return t % 2, t // 2


def at_edge(core):
    r, rows = lax.axis_index("rows"), lax.axis_size("rows")
    return ((core == 0) & (r == 0)) | ((core == 1) & (r == rows - 1))


def inner_row(half, core):
    return pl.multiple_of(half - 16 + 8 * core, 8)


def middle_row(half, core):
    return pl.multiple_of((half + 8) * core, 8)


def outer_row(half, core):
    return pl.multiple_of((2 * half - WIDE) * core, 8)


def load_kernel(half, starts, drive, own, held, inner, middle, sems):
    core, chip = place()
    copies = []
    for i, (row, size) in enumerate(((half - 16, 32), (0, half - 16), (half + 16, half - 16))):
        rows = pl.ds(row, size)
        pair = (
            pltpu.make_async_copy(starts.at[0, rows, :], own.at[rows, :], sems.at[2 * i]),
            pltpu.make_async_copy(drive.at[rows, :], held.at[rows, :], sems.at[2 * i + 1]),
        )
        for copy in pair:
            copy.start()
        copies.append(pair)

    def window(row, into):
        @pl.when(chip == 0)
        def _():
            fine, coarse = start_of(own[pl.ds(row, 24), :], held[pl.ds(row, 24), :])
            into[0:24, :] = fine
            into[24:48, :] = coarse

    for copy in copies[0]:
        copy.wait()
    window(inner_row(half, core), inner)
    for copy in (*copies[1], *copies[2]):
        copy.wait()
    window(middle_row(half, core), middle)


def inner_kernel(half, own, other, drive, mine, sent, ends, edge):
    core, chip = place()
    first = core == 0

    @pl.when(chip == 0)
    def _():
        rows = pl.ds(inner_row(half, core), 24)
        d = drive[rows, :]
        theirs = start_of(other[rows, :], d)
        e_a, e_b = ends_of(first, (mine[0:24, :], mine[24:48, :]), theirs, d)
        sent[...] = pltpu.roll(e_b, 24 - CUT, 0)[:16]
        ends[0:24, :] = e_a
        ends[24:48, :] = e_b

    rows = pl.ds(outer_row(half, core), 8)
    a, b = picked(first, own[rows, :], other[rows, :])
    edge[0:8, :] = a
    edge[8:16, :] = b
    edge[16:24, :] = drive[rows, :]


def middle_kernel(half, own, other, drive, mine, sent, ends, state):
    core, chip = place()
    first = core == 0

    @pl.when(chip == 0)
    def _():
        rows = pl.ds(middle_row(half, core), 24)
        d = drive[rows, :]
        theirs = start_of(other[rows, :], d)
        e_a, e_b = ends_of(first, (mine[0:24, :], mine[24:48, :]), theirs, d)
        sent[...] = pltpu.roll(e_b, 24 - CUT, 0)[:16]
        ends[0:24, :] = e_a
        ends[24:48, :] = e_b

    @pl.when(chip > 0)
    def _():
        size = half + WIDE
        rows = pl.ds(pl.multiple_of((half - WIDE) * core, 8), size)
        d = drive[rows, :]
        state[2 * size : 3 * size, :] = d
        for mine_first, ref in ((True, own), (False, other)):
            fine, coarse = start_of(ref[rows, :], d)
            kind = jnp.where(first == mine_first, 0, 1)
            field(state, kind, 3, 0, size)[...] = fine - coarse


def outer_kernel(half, own, other, drive, got, inner_state, sent, ends, state):
    core, chip = place()
    first = core == 0
    rows = pl.ds(outer_row(half, core), 8)
    a, b = picked(first, own[rows, :], other[rows, :])
    near = (a, b, drive[rows, :])
    far = [got[8 * i : 8 * i + 8, :] for i in range(3)]
    upper = [jnp.where(first, f, n) for f, n in zip(far, near)]
    lower = [jnp.where(first, n, f) for f, n in zip(far, near)]
    a, b, d = (jnp.concatenate(p) for p in zip(upper, lower))
    tile = lax.broadcasted_iota(jnp.int32, a.shape, 0) // 8
    inside = ~(at_edge(core) & (tile == core))

    def kept(v):
        return jnp.where(inside, v, 0.0)

    f_a, g_a = start_of(kept(a), d, kept)
    f_b, g_b = start_of(kept(b), d, kept)

    @pl.when(chip == 0)
    def _():
        e_a = g_a + (f_a - g_a)
        e_b = kept(coarse_of(e_a, around(e_a), d)) + (f_b - g_b)
        sent[...] = pltpu.roll(e_b, 16 - CUT, 0)[:8]
        ends[0:16, :] = e_a
        ends[16:32, :] = e_b

    size = half + WIDE
    fields = (f_a - g_a, f_b - g_b, d)

    @pl.when((chip > 0) & first)
    def _():
        for kind, v in enumerate(fields):
            before = field(inner_state, kind, 3, 0, 16)[...]
            field(state, kind, 3, 0, 8)[...] = v[:8]
            field(state, kind, 3, 8, 8)[...] = mixed(v[8:], before[:8])
            field(state, kind, 3, 16, 8)[...] = before[8:]

    @pl.when((chip > 0) & (core == 1))
    def _():
        for kind, v in enumerate(fields):
            before = field(inner_state, kind, 3, size - 16, 16)[...]
            field(state, kind, 3, 0, 8)[...] = before[:8]
            field(state, kind, 3, 8, 8)[...] = mixed(before[8:], v[:8])
            field(state, kind, 3, 16, 8)[...] = v[8:]


def put_ends(first, e_a, e_b, keep, send):
    kept, sent = picked(first, e_a, e_b)
    keep[...] = kept
    send[...] = sent


def inner_end(half, arrived, state, ends, keep, send):
    core, chip = place()
    first = core == 0

    @pl.when(chip == 0)
    def _():
        put_ends(first, ends[8:16, :], ends[32:40, :], keep, send)

    @pl.when(chip > 0)
    def _():
        v = arrived[...]
        current = pltpu.roll(jnp.concatenate([v, v[:8]]), CUT, 0)
        row = (half - 16) * (1 - core)
        d_a, d_b, d = (field(state, kind, 3, row, 24)[...] for kind in range(3))
        e_a, e_b = chain(current, d_a, d_b, d)
        put_ends(first, e_a[8:16], e_b[8:16], keep, send)


def middle_end(inner, middle, state, inner_ends, ends, keep, send, current):
    core, chip = place()
    first = core == 0

    def known(kind):
        near = field(inner_ends, kind, 2, 16 * core, 8)[...]
        rows = [field(ends, kind, 2, 8 * i, 8)[...] for i in range(3)]
        upper = jnp.where(first, rows[1], mixed(near, rows[0]))
        lower = jnp.where(first, mixed(rows[2], near), rows[1])
        return jnp.concatenate([upper, lower])

    @pl.when(chip == 0)
    def _():
        put_ends(first, known(0), known(1), keep, send)

    @pl.when((chip > 0) & first)
    def _():
        current[...] = pltpu.roll(jnp.concatenate([middle[...], inner[...]]), CUT, 0)

    @pl.when((chip > 0) & (core == 1))
    def _():
        current[...] = pltpu.roll(jnp.concatenate([inner[...], middle[...]]), 32 - CUT, 0)

    @pl.when(chip > 0)
    def _():
        d_a, d_b, d = (field(state, kind, 3, 8 * core, 32)[...] for kind in range(3))
        e_a, e_b = chain(current[...], d_a, d_b, d)
        put_ends(first, e_a[8:24], e_b[8:24], keep, send)


def outer_end(middle, outer, state, middle_ends, ends, keep, send, current):
    core, chip = place()
    first = core == 0

    def known(kind):
        near = field(middle_ends, kind, 2, 16 * core, 8)[...]
        far = field(ends, kind, 2, 8 * (1 - core), 8)[...]
        return jnp.where(first, mixed(far, near), mixed(near, far))

    @pl.when(chip == 0)
    def _():
        put_ends(first, known(0), known(1), keep, send)

    @pl.when((chip > 0) & first)
    def _():
        current[...] = pltpu.roll(jnp.concatenate([outer[...], middle[...]]), CUT, 0)

    @pl.when((chip > 0) & (core == 1))
    def _():
        current[...] = pltpu.roll(jnp.concatenate([middle[...], outer[...]]), 24 - CUT, 0)

    @pl.when(chip > 0)
    def _():
        d_a, d_b, d = (field(state, kind, 3, 0, 24)[...] for kind in range(3))
        tile = lax.broadcasted_iota(jnp.int32, d.shape, 0) // 8
        inside = ~(at_edge(core) & (tile == 2 * core))
        e_a = coarse_of(current[...], around(current[...]), d) + d_a
        e_a = jnp.where(inside, e_a, 0.0)
        e_b = coarse_of(e_a, around(e_a), d) + d_b
        put_ends(first, e_a[8:16], e_b[8:16], keep, send)


def write_kernel(half, order, *refs):
    count = len(order)
    pieces, out, sems = refs[:count], refs[-2], refs[-1]
    core, _ = place()
    copies = []
    for i, (mine, part) in enumerate(order):
        upper = (half - 8, 8, 0)[part]
        lower = (half, half + 8, 2 * half - 8)[part]
        row = pl.multiple_of(jnp.where((core == 0) == mine, upper, lower), 8)
        piece = pieces[i]
        copy = pltpu.make_async_copy(
            piece, out.at[0, pl.ds(row, piece.shape[0]), :], sems.at[i]
        )
        copy.start()
        copies.append(copy)
    for copy in copies:
        copy.wait()


def written(half, order, pieces, shape, into=None):
    vmem, anywhere = pl.BlockSpec(memory_space=pltpu.VMEM), pl.BlockSpec(memory_space=pl.ANY)
    count = len(pieces)
    extra = () if into is None else (into,)
    return pl.pallas_call(
        functools.partial(write_kernel, half, order),
        out_shape=jax.ShapeDtypeStruct(shape, jnp.float32),
        in_specs=[vmem] * count + [anywhere] * len(extra),
        out_specs=anywhere,
        input_output_aliases={count: 0} if extra else {},
        scratch_shapes=[pltpu.SemaphoreType.DMA((count,))],
        compiler_params=pltpu.CompilerParams(vmem_limit_bytes=16 << 20),
    )(*pieces, *extra)


def after(value, earlier):
    return lax.optimization_barrier((value, earlier))[0]


def masked_update(update, v, drive, inside):
    wide = (
        jnp.roll(v, 1, axis=0) + jnp.roll(v, -1, axis=0)
    ) + (jnp.roll(v, 1, axis=1) + jnp.roll(v, -1, axis=1))
    return jnp.where(inside, update(v, wide, drive), 0.0)


def long_chain(own, drive):
    height = own.shape[0]
    half = height // 2
    groups, slices, rows = (lax.axis_size(a) for a in AXES)
    t, r = lax.axis_index("tm"), lax.axis_index("rows")
    core, chip = t % 2, t // 2
    first = core == 0
    away = outward(groups, rows)

    def cut(field, start, size):
        return lax.dynamic_slice_in_dim(field, start, size, axis=0)

    other = routed(own, partner)
    s_a, s_b = picked(first, own, other)
    edge = core * (height - WIDE)
    got = routed(jnp.concatenate([cut(f, edge, WIDE) for f in (s_a, s_b, drive)]), away)

    def sided(body, outer, inner):
        return jnp.where(
            first,
            jnp.concatenate([outer, body, inner]),
            jnp.concatenate([inner, body, outer]),
        )

    def window(field, place):
        body = cut(field, core * half, half)
        inner = cut(field, jnp.where(first, half, half - WIDE), WIDE)
        return sided(body, got[place * WIDE : (place + 1) * WIDE], inner)

    w_a, w_b, w_d = (window(f, i) for i, f in enumerate((s_a, s_b, drive)))
    row = lax.broadcasted_iota(jnp.int32, (half + 2 * WIDE, 1), 0)
    row = row + r * height + core * half - WIDE
    inside = (row >= 0) & (row < rows * height)
    w_a, w_b = jnp.where(inside, w_a, 0.0), jnp.where(inside, w_b, 0.0)

    def delta(v):
        fine = v
        for _ in range(FINE):
            fine = masked_update(fine_of, fine, w_d, inside)
        return fine - masked_update(coarse_of, v, w_d, inside)

    d_a, d_b = delta(w_a), delta(w_b)

    def both(v):
        e_a = masked_update(coarse_of, v, w_d, inside) + d_a
        return e_a, masked_update(coarse_of, e_a, w_d, inside) + d_b

    def extended(v):
        last = WIDE + half - 2
        inner = routed(cut(v, jnp.where(first, last, WIDE), 2), partner)
        outer = routed(cut(v, jnp.where(first, WIDE, last), 2), away)
        return sided(v[WIDE : WIDE + half], outer, inner)

    e_a, e_b = both(w_a)
    for stage in range(slices // 2 - 1):
        moved = e_b[WIDE - 2 : WIDE + half + 2] if stage == 0 else extended(e_b)
        arrived = routed(moved, stage_swap(stage))
        current = jnp.pad(arrived, ((WIDE - 2, WIDE - 2), (0, 0)))
        n_a, n_b = both(jnp.where(inside, current, 0.0))
        here = chip == stage + 1
        e_a, e_b = jnp.where(here, n_a, e_a), jnp.where(here, n_b, e_b)

    kept, sent = picked(first, e_a[WIDE : WIDE + half], e_b[WIDE : WIDE + half])
    back = routed(sent, partner)
    return jnp.concatenate(picked(first, kept, back))[None]


def on_device(starts, drive):
    own = starts[0]
    if lax.axis_size("tm") != 4:
        return long_chain(own, drive)
    return two_chips(starts, drive)


def two_chips(starts, drive):
    _, height, width = starts.shape
    half = height // 2
    groups, rows = lax.axis_size("groups"), lax.axis_size("rows")
    vmem, anywhere = pl.BlockSpec(memory_space=pltpu.VMEM), pl.BlockSpec(memory_space=pl.ANY)

    other = routed(starts[0], partner)
    own, held, mine_1, mine_2 = pl.pallas_call(
        functools.partial(load_kernel, half),
        out_shape=[
            jax.ShapeDtypeStruct((size, width), jnp.float32)
            for size in (height, height, 48, 48)
        ],
        in_specs=[anywhere] * 2,
        out_specs=[vmem] * 4,
        scratch_shapes=[pltpu.SemaphoreType.DMA((6,))],
        compiler_params=pltpu.CompilerParams(vmem_limit_bytes=16 << 20),
        cost_estimate=pl.CostEstimate(
            flops=60 * 48 * width, bytes_accessed=16 * height * width, transcendentals=0
        ),
        name="load",
    )(starts, drive)
    sent_1, ends_1, edge = compute(
        functools.partial(inner_kernel, half),
        [(16, width), (48, width), (24, width)],
        (own, other, held, mine_1),
        name="inner",
    )
    here_1 = routed(sent_1, stage_swap(0))
    got = routed(edge, outward(groups, rows))
    sent_2, ends_2, state = compute(
        functools.partial(middle_kernel, half),
        [(16, width), (48, width), (3 * (half + WIDE), width)],
        (own, other, held, mine_2),
        name="middle",
    )
    here_2 = routed(sent_2, stage_swap(0))
    sent_3, ends_3, state_3 = compute(
        functools.partial(outer_kernel, half),
        [(8, width), (32, width), (3 * 24, width)],
        (own, other, held, got, state),
        name="outer",
    )
    here_3 = routed(sent_3, stage_swap(0))

    keep_1, send_1 = compute(
        functools.partial(inner_end, half),
        [(8, width)] * 2,
        (here_1, state, after(ends_1, sent_3)),
        name="inner_end",
    )
    back_1 = routed(send_1, partner)
    keep_2, send_2 = compute(
        middle_end,
        [(16, width)] * 2,
        (here_1, here_2, state, ends_1, after(ends_2, keep_1)),
        scratch_shapes=[pltpu.VMEM((32, width), jnp.float32)],
        name="middle_end",
    )
    back_2 = routed(send_2, partner)
    out = written(half, ((True, 0), (True, 1), (False, 0)), (keep_1, keep_2, back_1), starts.shape)
    out, ends_3 = lax.optimization_barrier((out, ends_3))
    keep_3, send_3 = compute(
        outer_end,
        [(8, width)] * 2,
        (here_2, here_3, state_3, ends_2, ends_3),
        scratch_shapes=[pltpu.VMEM((24, width), jnp.float32)],
        name="outer_end",
    )
    back_3 = routed(send_3, partner)
    return written(
        half, ((False, 1), (True, 2), (False, 2)), (back_2, keep_3, back_3), starts.shape, into=out
    )


def solution(mesh):
    in_specs = (P(("groups", "tm"), "rows", None), P("rows", None))
    out_specs = P(("groups", "tm"), "rows", None)
    return jax.shard_map(
        on_device, mesh=mesh, in_specs=in_specs, out_specs=out_specs, check_vma=False
    )
```

time: 30.4 us -> 28.1 us (0.924)
  waiting for transfers between devices: 10.9 us -> 9.87 us
  starting transfers between devices: 8.27 us -> 7.57 us
  Pallas kernels: 8.48 us -> 7.95 us
    pallas_call x6, Pallas kernels: 7.47 us -> 4.33 us  [compute(): pl.pallas_call(kernel, out_shape=shapes, in_specs=[vmem] * len(args), out...]
    pallas_call x1 -> x3, Pallas kernels: 1.01 us -> 3.62 us  [the longest x1 1.99 us: two_chips(): pl.pallas_call(functools.partial(load_kernel, half), out_shape=[jax.Shape...]
    ppermute x8, waiting for transfers between devices: 10.9 us -> 9.87 us  [routed(): return lax.ppermute(block, AXES, pairs)]
    ppermute x8, starting transfers between devices: 8.27 us -> 7.57 us  [routed(): return lax.ppermute(block, AXES, pairs)]
  transfers between devices with their start and end apart: 8 -> 8, of which waited for: 6 -> 5; matrix products, arithmetic and copies ran while one was open for 0% -> 0% of each run, Pallas kernels for 18% -> 21%
where the time goes in v3:
time: 28.1 us; the launch traced here: 28 us
  waiting for transfers between devices  9.87 us (35%)
  Pallas kernels  7.95 us (28%)
  starting transfers between devices  7.57 us (27%)
  local copies, waits for them, and re-layouts  2.45 us (9%)
    ppermute x8, waiting for transfers between devices, routed(): return lax.ppermute(block, AXES, pairs)  9.87 us
    ppermute x8, starting transfers between devices, routed(): return lax.ppermute(block, AXES, pairs)  7.57 us
    pallas_call x6, Pallas kernels, compute(): pl.pallas_call(kernel, out_shape=shapes, in_specs=[vmem] * len(args), out...  4.33 us
    unnamed x4, local copies, waits for them, and re-layouts  2.45 us
    pallas_call x1, Pallas kernels, two_chips(): pl.pallas_call(functools.partial(load_kernel, half), out_shape=[jax.Shape...  1.99 us
    pallas_call x2, Pallas kernels, written(): pl.pallas_call(functools.partial(write_kernel, half, order), out_shape=ja...  1.64 us
  transfers between devices with their start and end apart: 8, of which 5 were waited for; matrix products, arithmetic and copies ran while one was open for 0% of the time, Pallas kernels for 21%

profile of v3, /device:TPU:0, one launch (start us, length us, event | category | flops | bytes accessed | tf_op | source)
XLA Modules:
  0.0 28.0 jit_solution(13759234136036308934)
XLA Ops:
  0.0 0.5 %collective-permute-start = (f32[64,4096]{1,0:T(8,128)}, f32[64,4096]{1,0:T(8,128)S(1)}, u32[]{:S(2)}, u32[]{:S(2)}) collective-permute-start(f32[64,4096]{1,0:T(8,128)} %bitcast.1), channel_id=1, source_target_pairs={{0,4},{1,5},{2,6},{3,7},{4,0},{5,1},{6,2},{7,3},{8,12},{9,13},{10,... | collective-permute-start | bytes 3145736 | tf_op jit(solution)/shard_map/ppermute | solution.py:33
  0.5 0.0 copy-start
  0.5 1.2 %copy-done = f32[64,4096]{1,0:T(8,128)S(1)} copy-done((f32[64,4096]{1,0:T(8,128)S(1)}, f32[64,4096]{1,0:T(8,128)}, u32[]{:S(2)}) %copy-start) | copy-done | bytes 1048600
  1.7 0.0 copy-start.1
  1.7 1.2 %copy-done.1 = f32[1,64,4096]{2,1,0:T(8,128)S(1)} copy-done((f32[1,64,4096]{2,1,0:T(8,128)S(1)}, f32[1,64,4096]{2,1,0:T(8,128)}, u32[]{:S(2)}) %copy-start.1) | copy-done | bytes 1048600
  2.9 2.0 %load.1 = (f32[64,4096]{1,0:T(8,128)S(1)}, f32[64,4096]{1,0:T(8,128)S(1)}, f32[48,4096]{1,0:T(8,128)S(1)}, f32[48,4096]{1,0:T(8,128)S(1)}) custom-call(f32[1,64,4096]{2,1,0:T(8,128)S(1)} %copy-done.1, f32[64,4096]{1,0:T(8,128)S(1)} %copy-done), custom_call_target="tpu_custom_call" | custom-call | flops 11796480 | bytes 4194304 | tf_op jit(solution)/shard_map/load/pallas_call | solution.py:497
  4.9 0.0 collective-permute-done.other
  5.0 1.3 %inner.1 = (f32[16,4096]{1,0:T(8,128)S(1)}, f32[48,4096]{1,0:T(8,128)S(1)}, f32[24,4096]{1,0:T(8,128)S(1)}) custom-call(f32[64,4096]{1,0:T(8,128)S(1)} %get-tuple-element.28.own, f32[64,4096]{1,0:T(8,128)S(1)} %collective-permute-done.other, f32[64,4096]{1,0:T(8,128)S(1)} %get-tuple-element.29.drive, f32[48,4096]{1,0:T(8,128)S(1)} %get-tuple-element.30.mine), custom_call_target="tpu_custom_call" | custom-call | tf_op jit(solution)/shard_map/inner/pallas_call | solution.py:90
  6.3 2.6 %collective-permute-start.3 = (f32[24,4096]{1,0:T(8,128)S(1)}, f32[24,4096]{1,0:T(8,128)S(1)}, u32[]{:S(2)}, u32[]{:S(2)}) collective-permute-start(f32[24,4096]{1,0:T(8,128)S(1)} %get-tuple-element.37), channel_id=1, source_target_pairs={{0,16},{1,4},{2,5},{3,6},{4,1},{5,2},{6,3},{7,23},{8,24},{9,12},{1... | collective-permute-start | bytes 1179656 | tf_op jit(solution)/shard_map/ppermute | solution.py:33
  8.9 0.0 collective-permute-start.1
  8.9 1.3 %middle.1 = (f32[16,4096]{1,0:T(8,128)S(1)}, f32[48,4096]{1,0:T(8,128)S(1)}, f32[120,4096]{1,0:T(8,128)S(1)}) custom-call(f32[64,4096]{1,0:T(8,128)S(1)} %get-tuple-element.28.own, f32[64,4096]{1,0:T(8,128)S(1)} %collective-permute-done.other, f32[64,4096]{1,0:T(8,128)S(1)} %get-tuple-element.29.drive, f32[48,4096]{1,0:T(8,128)S(1)} %get-tuple-element.32.mine), custom_call_target="tpu_custom_call" | custom-call | tf_op jit(solution)/shard_map/middle/pallas_call | solution.py:90
  10.2 3.8 %collective-permute-start.2 = (f32[16,4096]{1,0:T(8,128)S(1)}, f32[16,4096]{1,0:T(8,128)S(1)}, u32[]{:S(2)}, u32[]{:S(2)}) collective-permute-start(f32[16,4096]{1,0:T(8,128)S(1)} %get-tuple-element.33), channel_id=1, source_target_pairs={{0,8},{1,9},{2,10},{3,11},{4,12},{5,13},{6,14},{7,15},{8,0},{9,1},... | collective-permute-start | bytes 786440 | tf_op jit(solution)/shard_map/ppermute | solution.py:33
  14.0 0.6 %collective-permute-done.3.got = f32[24,4096]{1,0:T(8,128)S(1)} collective-permute-done((f32[24,4096]{1,0:T(8,128)S(1)}, f32[24,4096]{1,0:T(8,128)S(1)}, u32[]{:S(2)}, u32[]{:S(2)}) %collective-permute-start.3) | collective-permute-done | bytes 393248 | tf_op jit(solution)/shard_map/ppermute | solution.py:33
  14.6 1.5 %outer.1 = (f32[8,4096]{1,0:T(8,128)S(1)}, f32[32,4096]{1,0:T(8,128)S(1)}, f32[72,4096]{1,0:T(8,128)S(1)}) custom-call(f32[64,4096]{1,0:T(8,128)S(1)} %get-tuple-element.28.own, f32[64,4096]{1,0:T(8,128)S(1)} %collective-permute-done.other, f32[64,4096]{1,0:T(8,128)S(1)} %get-tuple-element.29.drive, f32[24,4096]{1,0:T(8,128)S(1)} %collective-permute-done.3.got, ...), custom_call_target="tpu_custom_call" | custom-call | tf_op jit(solution)/shard_map/outer/pallas_call | solution.py:90
  16.2 1.9 %collective-permute-done.1.arrived.inner = f32[16,4096]{1,0:T(8,128)S(1)} collective-permute-done((f32[16,4096]{1,0:T(8,128)S(1)}, f32[16,4096]{1,0:T(8,128)S(1)}, u32[]{:S(2)}, u32[]{:S(2)}) %collective-permute-start.1) | collective-permute-done | bytes 262176 | tf_op jit(solution)/shard_map/ppermute | solution.py:33
  18.1 0.1 collective-permute-start.6
  18.2 0.5 %collective-permute-start.5 = (f32[8,4096]{1,0:T(8,128)S(1)}, f32[8,4096]{1,0:T(8,128)S(1)}, u32[]{:S(2)}, u32[]{:S(2)}) collective-permute-start(f32[8,4096]{1,0:T(8,128)S(1)} %get-tuple-element.38), channel_id=1, source_target_pairs={{0,8},{1,9},{2,10},{3,11},{4,12},{5,13},{6,14},{7,15},{8,0},{9,1},... | collective-permute-start | bytes 393224 | tf_op jit(solution)/shard_map/ppermute | solution.py:33
  18.6 5.0 %collective-permute-done.2.middle = f32[16,4096]{1,0:T(8,128)S(1)} collective-permute-done((f32[16,4096]{1,0:T(8,128)S(1)}, f32[16,4096]{1,0:T(8,128)S(1)}, u32[]{:S(2)}, u32[]{:S(2)}) %collective-permute-start.2) | collective-permute-done | bytes 262176 | tf_op jit(solution)/shard_map/ppermute | solution.py:33
  23.7 0.1 middle_end.1
  23.8 0.1 collective-permute-start.4
  23.9 0.0 collective-permute-done.6.refs_2_
  23.9 0.8 %shard_map.28.refs_3_ = f32[1,64,4096]{2,1,0:T(8,128)} custom-call(f32[8,4096]{1,0:T(8,128)S(1)} %get-tuple-element.40.refs_0_, f32[16,4096]{1,0:T(8,128)S(1)} %get-tuple-element.44.refs_1_, f32[8,4096]{1,0:T(8,128)S(1)} %collective-permute-done.6.refs_2_), custom_call_target="tpu_custom_call" | custom-call | tf_op jit(solution)/shard_map/pallas_call | solution.py:394
  24.7 1.0 %collective-permute-done.5.outer = f32[8,4096]{1,0:T(8,128)S(1)} collective-permute-done((f32[8,4096]{1,0:T(8,128)S(1)}, f32[8,4096]{1,0:T(8,128)S(1)}, u32[]{:S(2)}, u32[]{:S(2)}) %collective-permute-start.5) | collective-permute-done | bytes 131104 | tf_op jit(solution)/shard_map/ppermute | solution.py:33
  25.7 0.1 collective-permute-start.7
  25.8 0.0 collective-permute-done.4.refs_0_
  25.8 1.3 %collective-permute-done.7.refs_2_ = f32[8,4096]{1,0:T(8,128)S(1)} collective-permute-done((f32[8,4096]{1,0:T(8,128)S(1)}, f32[8,4096]{1,0:T(8,128)S(1)}, u32[]{:S(2)}, u32[]{:S(2)}) %collective-permute-start.7) | collective-permute-done | bytes 131104 | tf_op jit(solution)/shard_map/ppermute | solution.py:33
  27.2 0.8 %shard_map.29 = f32[1,64,4096]{2,1,0:T(8,128)} custom-call(f32[16,4096]{1,0:T(8,128)S(1)} %collective-permute-done.4.refs_0_, f32[8,4096]{1,0:T(8,128)S(1)} %get-tuple-element.48.refs_1_, f32[8,4096]{1,0:T(8,128)S(1)} %collective-permute-done.7.refs_2_, f32[1,64,4096]{2,1,0:T(8,128)} %shard_map.28.refs_3_), custom_call_target="tpu_custom_call", output_to_operand_aliasing={{}: (3, {})} | custom-call | tf_op jit(solution)/shard_map/pallas_call | solution.py:394
  (2 shorter events, 0.1 us)
Async XLA Ops:
  0.0 4.9 %collective-permute-start = (f32[64,4096]{1,0:T(8,128)}, f32[64,4096]{1,0:T(8,128)S(1)}, u32[]{:S(2)}, u32[]{:S(2)}) collective-permute-start(f32[64,4096]{1,0:T(8,128)} %bitcast.1), channel_id=1, source_target_pairs={{0,4},{1,5},{2,6},{3,7},{4,0},{5,1},{6,2},{7,3},{8,12},{9,13},{10,... | collective-permute-start | bytes 3145736 | tf_op jit(solution)/shard_map/ppermute | solution.py:33
  0.5 1.2 %copy-start = (f32[64,4096]{1,0:T(8,128)S(1)}, f32[64,4096]{1,0:T(8,128)}, u32[]{:S(2)}) copy-start(f32[64,4096]{1,0:T(8,128)} %drive.1) | copy-start | bytes 3145732
  1.7 1.2 %copy-start.1 = (f32[1,64,4096]{2,1,0:T(8,128)S(1)}, f32[1,64,4096]{2,1,0:T(8,128)}, u32[]{:S(2)}) copy-start(f32[1,64,4096]{2,1,0:T(8,128)} %starts.1) | copy-start | bytes 3145732
  6.3 8.3 %collective-permute-start.3 = (f32[24,4096]{1,0:T(8,128)S(1)}, f32[24,4096]{1,0:T(8,128)S(1)}, u32[]{:S(2)}, u32[]{:S(2)}) collective-permute-start(f32[24,4096]{1,0:T(8,128)S(1)} %get-tuple-element.37), channel_id=1, source_target_pairs={{0,16},{1,4},{2,5},{3,6},{4,1},{5,2},{6,3},{7,23},{8,24},{9,12},{1... | collective-permute-start | bytes 1179656 | tf_op jit(solution)/shard_map/ppermute | solution.py:33
  8.9 9.2 %collective-permute-start.1 = (f32[16,4096]{1,0:T(8,128)S(1)}, f32[16,4096]{1,0:T(8,128)S(1)}, u32[]{:S(2)}, u32[]{:S(2)}) collective-permute-start(f32[16,4096]{1,0:T(8,128)S(1)} %get-tuple-element.31), channel_id=1, source_target_pairs={{0,8},{1,9},{2,10},{3,11},{4,12},{5,13},{6,14},{7,15},{8,0},{9,1},... | collective-permute-start | bytes 786440 | tf_op jit(solution)/shard_map/ppermute | solution.py:33
  10.2 13.5 %collective-permute-start.2 = (f32[16,4096]{1,0:T(8,128)S(1)}, f32[16,4096]{1,0:T(8,128)S(1)}, u32[]{:S(2)}, u32[]{:S(2)}) collective-permute-start(f32[16,4096]{1,0:T(8,128)S(1)} %get-tuple-element.33), channel_id=1, source_target_pairs={{0,8},{1,9},{2,10},{3,11},{4,12},{5,13},{6,14},{7,15},{8,0},{9,1},... | collective-permute-start | bytes 786440 | tf_op jit(solution)/shard_map/ppermute | solution.py:33
  18.1 5.8 %collective-permute-start.6 = (f32[8,4096]{1,0:T(8,128)S(1)}, f32[8,4096]{1,0:T(8,128)S(1)}, u32[]{:S(2)}, u32[]{:S(2)}) collective-permute-start(f32[8,4096]{1,0:T(8,128)S(1)} %get-tuple-element.45), channel_id=1, source_target_pairs={{0,4},{1,5},{2,6},{3,7},{4,0},{5,1},{6,2},{7,3},{8,12},{9,13},{10,... | collective-permute-start | bytes 393224 | tf_op jit(solution)/shard_map/ppermute | solution.py:33
  18.2 7.5 %collective-permute-start.5 = (f32[8,4096]{1,0:T(8,128)S(1)}, f32[8,4096]{1,0:T(8,128)S(1)}, u32[]{:S(2)}, u32[]{:S(2)}) collective-permute-start(f32[8,4096]{1,0:T(8,128)S(1)} %get-tuple-element.38), channel_id=1, source_target_pairs={{0,8},{1,9},{2,10},{3,11},{4,12},{5,13},{6,14},{7,15},{8,0},{9,1},... | collective-permute-start | bytes 393224 | tf_op jit(solution)/shard_map/ppermute | solution.py:33
  23.8 2.0 %collective-permute-start.4 = (f32[16,4096]{1,0:T(8,128)S(1)}, f32[16,4096]{1,0:T(8,128)S(1)}, u32[]{:S(2)}, u32[]{:S(2)}) collective-permute-start(f32[16,4096]{1,0:T(8,128)S(1)} %get-tuple-element.42), channel_id=1, source_target_pairs={{0,4},{1,5},{2,6},{3,7},{4,0},{5,1},{6,2},{7,3},{8,12},{9,13},{10,... | collective-permute-start | bytes 786440 | tf_op jit(solution)/shard_map/ppermute | solution.py:33
  25.7 1.4 %collective-permute-start.7 = (f32[8,4096]{1,0:T(8,128)S(1)}, f32[8,4096]{1,0:T(8,128)S(1)}, u32[]{:S(2)}, u32[]{:S(2)}) collective-permute-start(f32[8,4096]{1,0:T(8,128)S(1)} %get-tuple-element.49), channel_id=1, source_target_pairs={{0,4},{1,5},{2,6},{3,7},{4,0},{5,1},{6,2},{7,3},{8,12},{9,13},{10,... | collective-permute-start | bytes 393224 | tf_op jit(solution)/shard_map/ppermute | solution.py:33

commit v4 on v3

--- a/solution.py
+++ b/solution.py
@@ -209,7 +209,7 @@
     edge[16:24, :] = drive[rows, :]
 
 
-def middle_kernel(half, own, other, drive, mine, sent, ends, state):
+def middle_kernel(half, own, other, drive, mine, sent, ends):
     core, chip = place()
     first = core == 0
 
@@ -222,6 +222,11 @@
         sent[...] = pltpu.roll(e_b, 24 - CUT, 0)[:16]
         ends[0:24, :] = e_a
         ends[24:48, :] = e_b
+
+
+def state_kernel(half, own, other, drive, state):
+    core, chip = place()
+    first = core == 0
 
     @pl.when(chip > 0)
     def _():
@@ -491,7 +496,7 @@
     _, height, width = starts.shape
     half = height // 2
     groups, rows = lax.axis_size("groups"), lax.axis_size("rows")
-    vmem, anywhere = pl.BlockSpec(memory_space=pltpu.VMEM), pl.BlockSpec(memory_space=pl.ANY)
+    vmem = pl.BlockSpec(memory_space=pltpu.VMEM)
 
     other = routed(starts[0], partner)
     own, held, mine_1, mine_2 = pl.pallas_call(
@@ -500,10 +505,10 @@
             jax.ShapeDtypeStruct((size, width), jnp.float32)
             for size in (height, height, 48, 48)
         ],
-        in_specs=[anywhere] * 2,
+        in_specs=[pl.BlockSpec(memory_space=pltpu.HBM)] * 2,
         out_specs=[vmem] * 4,
         scratch_shapes=[pltpu.SemaphoreType.DMA((6,))],
-        compiler_params=pltpu.CompilerParams(vmem_limit_bytes=16 << 20),
+        compiler_params=pltpu.CompilerParams(vmem_limit_bytes=50 << 20),
         cost_estimate=pl.CostEstimate(
             flops=60 * 48 * width, bytes_accessed=16 * height * width, transcendentals=0
         ),
@@ -517,13 +522,19 @@
     )
     here_1 = routed(sent_1, stage_swap(0))
     got = routed(edge, outward(groups, rows))
-    sent_2, ends_2, state = compute(
+    sent_2, ends_2 = compute(
         functools.partial(middle_kernel, half),
-        [(16, width), (48, width), (3 * (half + WIDE), width)],
+        [(16, width), (48, width)],
         (own, other, held, mine_2),
         name="middle",
     )
     here_2 = routed(sent_2, stage_swap(0))
+    (state,) = compute(
+        functools.partial(state_kernel, half),
+        [(3 * (half + WIDE), width)],
+        (own, other, after(held, sent_2)),
+        name="state",
+    )
     sent_3, ends_3, state_3 = compute(
         functools.partial(outer_kernel, half),
         [(8, width), (32, width), (3 * 24, width)],

time: 28.1 us -> 26.7 us (0.950)
  waiting for transfers between devices: 9.87 us -> 13 us
  starting transfers between devices: 7.57 us -> 4.48 us
  local copies, waits for them, and re-layouts: 2.45 us -> 0 us
  Pallas kernels: 7.95 us -> 9 us
    ppermute x8, waiting for transfers between devices: 9.87 us -> 13 us  [routed(): return lax.ppermute(block, AXES, pairs)]
    ppermute x8, starting transfers between devices: 7.57 us -> 4.48 us  [routed(): return lax.ppermute(block, AXES, pairs)]
    unnamed x4 -> x0, local copies, waits for them, and re-layouts: 2.45 us -> none
    pallas_call x1, Pallas kernels: 1.99 us -> 3.04 us  [two_chips(): pl.pallas_call(functools.partial(load_kernel, half), out_shape=[jax.Shape...]
    pallas_call x6 -> x7, Pallas kernels: 4.33 us -> 4.33 us  [compute(): pl.pallas_call(kernel, out_shape=shapes, in_specs=[vmem] * len(args), out...]
  transfers between devices with their start and end apart: 8 -> 8, of which waited for: 5 -> 5; matrix products, arithmetic and copies ran while one was open for 0% -> 0% of each run, Pallas kernels for 21% -> 26%
where the time goes in v4:
time: 26.7 us; the launch traced here: 26.6 us
  waiting for transfers between devices  13 us (49%)
  Pallas kernels  9 us (34%)
  starting transfers between devices  4.48 us (17%)
    ppermute x8, waiting for transfers between devices, routed(): return lax.ppermute(block, AXES, pairs)  13 us
    ppermute x8, starting transfers between devices, routed(): return lax.ppermute(block, AXES, pairs)  4.48 us
    pallas_call x7, Pallas kernels, compute(): pl.pallas_call(kernel, out_shape=shapes, in_specs=[vmem] * len(args), out...  4.33 us
    pallas_call x1, Pallas kernels, two_chips(): pl.pallas_call(functools.partial(load_kernel, half), out_shape=[jax.Shape...  3.04 us
    pallas_call x2, Pallas kernels, written(): pl.pallas_call(functools.partial(write_kernel, half, order), out_shape=ja...  1.64 us
  transfers between devices with their start and end apart: 8, of which 5 were waited for; matrix products, arithmetic and copies ran while one was open for 0% of the time, Pallas kernels for 26%

profile of v4, /device:TPU:0, one launch (start us, length us, event | category | flops | bytes accessed | tf_op | source)
XLA Modules:
  0.0 26.6 jit_solution(8243653571906557416)
XLA Ops:
  0.0 0.5 %collective-permute-start = (f32[64,4096]{1,0:T(8,128)}, f32[64,4096]{1,0:T(8,128)S(1)}, u32[]{:S(2)}, u32[]{:S(2)}) collective-permute-start(f32[64,4096]{1,0:T(8,128)} %bitcast.1), channel_id=1, source_target_pairs={{0,4},{1,5},{2,6},{3,7},{4,0},{5,1},{6,2},{7,3},{8,12},{9,13},{10,... | collective-permute-start | bytes 3145736 | tf_op jit(solution)/shard_map/ppermute | solution.py:33
  0.5 3.0 %load.1 = (f32[64,4096]{1,0:T(8,128)S(1)}, f32[64,4096]{1,0:T(8,128)S(1)}, f32[48,4096]{1,0:T(8,128)S(1)}, f32[48,4096]{1,0:T(8,128)S(1)}) custom-call(f32[1,64,4096]{2,1,0:T(8,128)} %starts.1, f32[64,4096]{1,0:T(8,128)} %drive.1), custom_call_target="tpu_custom_call" | custom-call | flops 11796480 | bytes 4194304 | tf_op jit(solution)/shard_map/load/pallas_call | solution.py:502
  3.5 0.0 collective-permute-done.other
  3.6 1.3 %inner.1 = (f32[16,4096]{1,0:T(8,128)S(1)}, f32[48,4096]{1,0:T(8,128)S(1)}, f32[24,4096]{1,0:T(8,128)S(1)}) custom-call(f32[64,4096]{1,0:T(8,128)S(1)} %get-tuple-element.28.own, f32[64,4096]{1,0:T(8,128)S(1)} %collective-permute-done.other, f32[64,4096]{1,0:T(8,128)S(1)} %get-tuple-element.34.drive, f32[48,4096]{1,0:T(8,128)S(1)} %get-tuple-element.30.mine), custom_call_target="tpu_custom_call" | custom-call | tf_op jit(solution)/shard_map/inner/pallas_call | solution.py:90
  4.9 2.6 %collective-permute-start.3 = (f32[24,4096]{1,0:T(8,128)S(1)}, f32[24,4096]{1,0:T(8,128)S(1)}, u32[]{:S(2)}, u32[]{:S(2)}) collective-permute-start(f32[24,4096]{1,0:T(8,128)S(1)} %get-tuple-element.37), channel_id=1, source_target_pairs={{0,16},{1,4},{2,5},{3,6},{4,1},{5,2},{6,3},{7,23},{8,24},{9,12},{1... | collective-permute-start | bytes 1179656 | tf_op jit(solution)/shard_map/ppermute | solution.py:33
  7.5 0.0 collective-permute-start.1
  7.5 1.3 %middle.1 = (f32[16,4096]{1,0:T(8,128)S(1)}, f32[48,4096]{1,0:T(8,128)S(1)}) custom-call(f32[64,4096]{1,0:T(8,128)S(1)} %get-tuple-element.28.own, f32[64,4096]{1,0:T(8,128)S(1)} %collective-permute-done.other, f32[64,4096]{1,0:T(8,128)S(1)} %get-tuple-element.34.drive, f32[48,4096]{1,0:T(8,128)S(1)} %get-tuple-element.32.mine), custom_call_target="tpu_custom_call" | custom-call | tf_op jit(solution)/shard_map/middle/pallas_call | solution.py:90
  8.8 0.7 %collective-permute-start.2 = (f32[16,4096]{1,0:T(8,128)S(1)}, f32[16,4096]{1,0:T(8,128)S(1)}, u32[]{:S(2)}, u32[]{:S(2)}) collective-permute-start(f32[16,4096]{1,0:T(8,128)S(1)} %get-tuple-element.33), channel_id=1, source_target_pairs={{0,8},{1,9},{2,10},{3,11},{4,12},{5,13},{6,14},{7,15},{8,0},{9,1},... | collective-permute-start | bytes 786440 | tf_op jit(solution)/shard_map/ppermute | solution.py:33
  9.5 3.7 %collective-permute-done.3.got = f32[24,4096]{1,0:T(8,128)S(1)} collective-permute-done((f32[24,4096]{1,0:T(8,128)S(1)}, f32[24,4096]{1,0:T(8,128)S(1)}, u32[]{:S(2)}, u32[]{:S(2)}) %collective-permute-start.3) | collective-permute-done | bytes 393248 | tf_op jit(solution)/shard_map/ppermute | solution.py:33
  13.2 1.5 %outer.1 = (f32[8,4096]{1,0:T(8,128)S(1)}, f32[32,4096]{1,0:T(8,128)S(1)}, f32[72,4096]{1,0:T(8,128)S(1)}) custom-call(f32[64,4096]{1,0:T(8,128)S(1)} %get-tuple-element.28.own, f32[64,4096]{1,0:T(8,128)S(1)} %collective-permute-done.other, f32[64,4096]{1,0:T(8,128)S(1)} %get-tuple-element.34.drive, f32[24,4096]{1,0:T(8,128)S(1)} %collective-permute-done.3.got, ...), custom_call_target="tpu_custom_call" | custom-call | tf_op jit(solution)/shard_map/outer/pallas_call | solution.py:90
  14.8 1.9 %collective-permute-done.1.arrived.inner = f32[16,4096]{1,0:T(8,128)S(1)} collective-permute-done((f32[16,4096]{1,0:T(8,128)S(1)}, f32[16,4096]{1,0:T(8,128)S(1)}, u32[]{:S(2)}, u32[]{:S(2)}) %collective-permute-start.1) | collective-permute-done | bytes 262176 | tf_op jit(solution)/shard_map/ppermute | solution.py:33
  16.7 0.1 collective-permute-start.6
  16.8 0.5 %collective-permute-start.5 = (f32[8,4096]{1,0:T(8,128)S(1)}, f32[8,4096]{1,0:T(8,128)S(1)}, u32[]{:S(2)}, u32[]{:S(2)}) collective-permute-start(f32[8,4096]{1,0:T(8,128)S(1)} %get-tuple-element.38), channel_id=1, source_target_pairs={{0,8},{1,9},{2,10},{3,11},{4,12},{5,13},{6,14},{7,15},{8,0},{9,1},... | collective-permute-start | bytes 393224 | tf_op jit(solution)/shard_map/ppermute | solution.py:33
  17.2 5.0 %collective-permute-done.2.middle = f32[16,4096]{1,0:T(8,128)S(1)} collective-permute-done((f32[16,4096]{1,0:T(8,128)S(1)}, f32[16,4096]{1,0:T(8,128)S(1)}, u32[]{:S(2)}, u32[]{:S(2)}) %collective-permute-start.2) | collective-permute-done | bytes 262176 | tf_op jit(solution)/shard_map/ppermute | solution.py:33
  22.3 0.1 middle_end.1
  22.4 0.1 collective-permute-start.4
  22.5 0.0 collective-permute-done.6.refs_2_
  22.5 0.8 %shard_map.28.refs_3_ = f32[1,64,4096]{2,1,0:T(8,128)} custom-call(f32[8,4096]{1,0:T(8,128)S(1)} %get-tuple-element.40.refs_0_, f32[16,4096]{1,0:T(8,128)S(1)} %get-tuple-element.44.refs_1_, f32[8,4096]{1,0:T(8,128)S(1)} %collective-permute-done.6.refs_2_), custom_call_target="tpu_custom_call" | custom-call | tf_op jit(solution)/shard_map/pallas_call | solution.py:399
  23.3 1.0 %collective-permute-done.5.outer = f32[8,4096]{1,0:T(8,128)S(1)} collective-permute-done((f32[8,4096]{1,0:T(8,128)S(1)}, f32[8,4096]{1,0:T(8,128)S(1)}, u32[]{:S(2)}, u32[]{:S(2)}) %collective-permute-start.5) | collective-permute-done | bytes 131104 | tf_op jit(solution)/shard_map/ppermute | solution.py:33
  24.3 0.1 collective-permute-start.7
  24.4 0.0 collective-permute-done.4.refs_0_
  24.4 1.3 %collective-permute-done.7.refs_2_ = f32[8,4096]{1,0:T(8,128)S(1)} collective-permute-done((f32[8,4096]{1,0:T(8,128)S(1)}, f32[8,4096]{1,0:T(8,128)S(1)}, u32[]{:S(2)}, u32[]{:S(2)}) %collective-permute-start.7) | collective-permute-done | bytes 131104 | tf_op jit(solution)/shard_map/ppermute | solution.py:33
  25.8 0.8 %shard_map.29 = f32[1,64,4096]{2,1,0:T(8,128)} custom-call(f32[16,4096]{1,0:T(8,128)S(1)} %collective-permute-done.4.refs_0_, f32[8,4096]{1,0:T(8,128)S(1)} %get-tuple-element.48.refs_1_, f32[8,4096]{1,0:T(8,128)S(1)} %collective-permute-done.7.refs_2_, f32[1,64,4096]{2,1,0:T(8,128)} %shard_map.28.refs_3_), custom_call_target="tpu_custom_call", output_to_operand_aliasing={{}: (3, {})} | custom-call | tf_op jit(solution)/shard_map/pallas_call | solution.py:399
  (3 shorter events, 0.1 us)
Async XLA Ops:
  0.0 3.5 %collective-permute-start = (f32[64,4096]{1,0:T(8,128)}, f32[64,4096]{1,0:T(8,128)S(1)}, u32[]{:S(2)}, u32[]{:S(2)}) collective-permute-start(f32[64,4096]{1,0:T(8,128)} %bitcast.1), channel_id=1, source_target_pairs={{0,4},{1,5},{2,6},{3,7},{4,0},{5,1},{6,2},{7,3},{8,12},{9,13},{10,... | collective-permute-start | bytes 3145736 | tf_op jit(solution)/shard_map/ppermute | solution.py:33
  4.9 8.3 %collective-permute-start.3 = (f32[24,4096]{1,0:T(8,128)S(1)}, f32[24,4096]{1,0:T(8,128)S(1)}, u32[]{:S(2)}, u32[]{:S(2)}) collective-permute-start(f32[24,4096]{1,0:T(8,128)S(1)} %get-tuple-element.37), channel_id=1, source_target_pairs={{0,16},{1,4},{2,5},{3,6},{4,1},{5,2},{6,3},{7,23},{8,24},{9,12},{1... | collective-permute-start | bytes 1179656 | tf_op jit(solution)/shard_map/ppermute | solution.py:33
  7.5 9.2 %collective-permute-start.1 = (f32[16,4096]{1,0:T(8,128)S(1)}, f32[16,4096]{1,0:T(8,128)S(1)}, u32[]{:S(2)}, u32[]{:S(2)}) collective-permute-start(f32[16,4096]{1,0:T(8,128)S(1)} %get-tuple-element.31), channel_id=1, source_target_pairs={{0,8},{1,9},{2,10},{3,11},{4,12},{5,13},{6,14},{7,15},{8,0},{9,1},... | collective-permute-start | bytes 786440 | tf_op jit(solution)/shard_map/ppermute | solution.py:33
  8.8 13.5 %collective-permute-start.2 = (f32[16,4096]{1,0:T(8,128)S(1)}, f32[16,4096]{1,0:T(8,128)S(1)}, u32[]{:S(2)}, u32[]{:S(2)}) collective-permute-start(f32[16,4096]{1,0:T(8,128)S(1)} %get-tuple-element.33), channel_id=1, source_target_pairs={{0,8},{1,9},{2,10},{3,11},{4,12},{5,13},{6,14},{7,15},{8,0},{9,1},... | collective-permute-start | bytes 786440 | tf_op jit(solution)/shard_map/ppermute | solution.py:33
  16.7 5.8 %collective-permute-start.6 = (f32[8,4096]{1,0:T(8,128)S(1)}, f32[8,4096]{1,0:T(8,128)S(1)}, u32[]{:S(2)}, u32[]{:S(2)}) collective-permute-start(f32[8,4096]{1,0:T(8,128)S(1)} %get-tuple-element.45), channel_id=1, source_target_pairs={{0,4},{1,5},{2,6},{3,7},{4,0},{5,1},{6,2},{7,3},{8,12},{9,13},{10,... | collective-permute-start | bytes 393224 | tf_op jit(solution)/shard_map/ppermute | solution.py:33
  16.8 7.5 %collective-permute-start.5 = (f32[8,4096]{1,0:T(8,128)S(1)}, f32[8,4096]{1,0:T(8,128)S(1)}, u32[]{:S(2)}, u32[]{:S(2)}) collective-permute-start(f32[8,4096]{1,0:T(8,128)S(1)} %get-tuple-element.38), channel_id=1, source_target_pairs={{0,8},{1,9},{2,10},{3,11},{4,12},{5,13},{6,14},{7,15},{8,0},{9,1},... | collective-permute-start | bytes 393224 | tf_op jit(solution)/shard_map/ppermute | solution.py:33
  22.4 2.0 %collective-permute-start.4 = (f32[16,4096]{1,0:T(8,128)S(1)}, f32[16,4096]{1,0:T(8,128)S(1)}, u32[]{:S(2)}, u32[]{:S(2)}) collective-permute-start(f32[16,4096]{1,0:T(8,128)S(1)} %get-tuple-element.42), channel_id=1, source_target_pairs={{0,4},{1,5},{2,6},{3,7},{4,0},{5,1},{6,2},{7,3},{8,12},{9,13},{10,... | collective-permute-start | bytes 786440 | tf_op jit(solution)/shard_map/ppermute | solution.py:33
  24.3 1.4 %collective-permute-start.7 = (f32[8,4096]{1,0:T(8,128)S(1)}, f32[8,4096]{1,0:T(8,128)S(1)}, u32[]{:S(2)}, u32[]{:S(2)}) collective-permute-start(f32[8,4096]{1,0:T(8,128)S(1)} %get-tuple-element.49), channel_id=1, source_target_pairs={{0,4},{1,5},{2,6},{3,7},{4,0},{5,1},{6,2},{7,3},{8,12},{9,13},{10,... | collective-permute-start | bytes 393224 | tf_op jit(solution)/shard_map/ppermute | solution.py:33

commit v5 on v4

--- a/solution.py
+++ b/solution.py
@@ -138,6 +138,33 @@
     return jnp.where(row < CUT, upper, lower)
 
 
+def sublane(v):
+    return lax.broadcasted_iota(jnp.int32, v.shape, 0)
+
+
+def folded(v):
+    width = v.shape[1]
+    half, quarter = width // 2, width // 4
+    four = mixed(v[:, :half], pltpu.roll(v[:, half:], 4, 0))
+    row = sublane(four[:, :quarter])
+    two = pltpu.roll(v[:, :quarter], 4, 0)
+    for i, shift in ((1, 6), (2, 0), (3, 2)):
+        part = v[:, i * quarter : (i + 1) * quarter]
+        part = pltpu.roll(part, shift, 0) if shift else part
+        two = jnp.where(row < 2 * i, two, part)
+    return jnp.concatenate([four, two], axis=1)
+
+
+def unfolded(v):
+    half = v.shape[1] * 2 // 3
+    four, two = v[:, :half], v[:, half:]
+    low = [pltpu.roll(two, 4, 0), pltpu.roll(two, 2, 0), two, pltpu.roll(two, 6, 0)]
+    return mixed(
+        jnp.concatenate([four, pltpu.roll(four, 4, 0)], axis=1),
+        jnp.concatenate(low, axis=1),
+    )
+
+
 def place():
     t = lax.axis_index("tm")
     return t % 2, t // 2
@@ -160,7 +187,7 @@
     return pl.multiple_of((2 * half - WIDE) * core, 8)
 
 
-def load_kernel(half, starts, drive, own, held, inner, middle, sems):
+def load_kernel(half, starts, drive, own, held, inner, sems):
     core, chip = place()
     copies = []
     for i, (row, size) in enumerate(((half - 16, 32), (0, half - 16), (half + 16, half - 16))):
@@ -173,43 +200,57 @@
             copy.start()
         copies.append(pair)
 
-    def window(row, into):
-        @pl.when(chip == 0)
-        def _():
-            fine, coarse = start_of(own[pl.ds(row, 24), :], held[pl.ds(row, 24), :])
-            into[0:24, :] = fine
-            into[24:48, :] = coarse
-
     for copy in copies[0]:
         copy.wait()
-    window(inner_row(half, core), inner)
+
+    @pl.when(chip == 0)
+    def _():
+        rows = pl.ds(inner_row(half, core), 24)
+        fine, coarse = start_of(own[rows, :], held[rows, :])
+        inner[0:24, :] = fine
+        inner[24:48, :] = coarse
+
     for copy in (*copies[1], *copies[2]):
         copy.wait()
-    window(middle_row(half, core), middle)
-
-
-def inner_kernel(half, own, other, drive, mine, sent, ends, edge):
-    core, chip = place()
-    first = core == 0
+
+
+def inner_kernel(half, side, own, other, drive, mine, sent, ends, edge=None):
+    core, chip = place()
+    first = core == 0
+    width = drive.shape[1]
+    mid = width // 2
+
+    def columns(ref, rows):
+        if side == 0:
+            parts = ref[rows, width - 128 :], ref[rows, : mid + 128]
+        else:
+            parts = ref[rows, mid - 128 :], ref[rows, :128]
+        return jnp.concatenate(parts, axis=1)
 
     @pl.when(chip == 0)
     def _():
         rows = pl.ds(inner_row(half, core), 24)
-        d = drive[rows, :]
-        theirs = start_of(other[rows, :], d)
-        e_a, e_b = ends_of(first, (mine[0:24, :], mine[24:48, :]), theirs, d)
-        sent[...] = pltpu.roll(e_b, 24 - CUT, 0)[:16]
+        d = columns(drive, rows)
+        theirs = start_of(columns(other, rows), d)
+        known = columns(mine, pl.ds(0, 24)), columns(mine, pl.ds(24, 24))
+        e_a, e_b = ends_of(first, known, theirs, d)
+        e_a, e_b = e_a[:, 128:-128], e_b[:, 128:-128]
+        frame = pltpu.roll(e_b, 24 - CUT, 0)
+        whole, part = picked(first, frame[:8], frame[8:16])
+        part = jnp.where(first, part, pltpu.roll(part, 6, 0))
+        sent[...] = jnp.concatenate([whole, folded(part)], axis=1)
         ends[0:24, :] = e_a
         ends[24:48, :] = e_b
 
-    rows = pl.ds(outer_row(half, core), 8)
-    a, b = picked(first, own[rows, :], other[rows, :])
-    edge[0:8, :] = a
-    edge[8:16, :] = b
-    edge[16:24, :] = drive[rows, :]
-
-
-def middle_kernel(half, own, other, drive, mine, sent, ends):
+    if edge is not None:
+        rows = pl.ds(outer_row(half, core), 8)
+        a, b = picked(first, own[rows, :], other[rows, :])
+        edge[0:8, :] = a
+        edge[8:16, :] = b
+        edge[16:24, :] = drive[rows, :]
+
+
+def middle_kernel(half, own, other, drive, sent, ends):
     core, chip = place()
     first = core == 0
 
@@ -217,8 +258,8 @@
     def _():
         rows = pl.ds(middle_row(half, core), 24)
         d = drive[rows, :]
-        theirs = start_of(other[rows, :], d)
-        e_a, e_b = ends_of(first, (mine[0:24, :], mine[24:48, :]), theirs, d)
+        mine, theirs = start_of(own[rows, :], d), start_of(other[rows, :], d)
+        e_a, e_b = ends_of(first, mine, theirs, d)
         sent[...] = pltpu.roll(e_b, 24 - CUT, 0)[:16]
         ends[0:24, :] = e_a
         ends[24:48, :] = e_b
@@ -263,7 +304,8 @@
     def _():
         e_a = g_a + (f_a - g_a)
         e_b = kept(coarse_of(e_a, around(e_a), d)) + (f_b - g_b)
-        sent[...] = pltpu.roll(e_b, 16 - CUT, 0)[:8]
+        frame = pltpu.roll(e_b, 16 - CUT, 0)[:8]
+        sent[...] = folded(jnp.where(first, pltpu.roll(frame, 6, 0), frame))
         ends[0:16, :] = e_a
         ends[16:32, :] = e_b
 
@@ -293,38 +335,63 @@
     send[...] = sent
 
 
-def inner_end(half, arrived, state, ends, keep, send):
-    core, chip = place()
-    first = core == 0
+def inner_end(
+    half, left, right, state, ends_left, ends_right, middle, outer, keep, send, frame
+):
+    core, chip = place()
+    first = core == 0
+    mid = ends_left.shape[1]
 
     @pl.when(chip == 0)
     def _():
-        put_ends(first, ends[8:16, :], ends[32:40, :], keep, send)
+        def rows(kind, tile):
+            into = pl.ds(24 * kind + 8 * tile, 8)
+            return jnp.concatenate([ends_left[into, :], ends_right[into, :]], axis=1)
+
+        def known(kind):
+            lower = [rows(kind, i) for i in range(3)]
+            upper = [field(middle, kind, 2, 8 * i, 8)[...] for i in range(3)]
+            last = [field(outer, kind, 2, 8 * i, 8)[...] for i in range(2)]
+            return jnp.concatenate(
+                [
+                    lower[1],
+                    jnp.where(first, upper[1], mixed(lower[2], upper[0])),
+                    jnp.where(first, mixed(upper[2], lower[0]), upper[1]),
+                    jnp.where(first, mixed(last[1], upper[0]), mixed(upper[2], last[0])),
+                ]
+            )
+
+        kept, sent = picked(first, known(0), known(1))
+        keep[...] = kept
+        send[...] = sent
 
     @pl.when(chip > 0)
     def _():
-        v = arrived[...]
-        current = pltpu.roll(jnp.concatenate([v, v[:8]]), CUT, 0)
+        parts = left[...], right[...]
+        whole = jnp.concatenate([p[:, :mid] for p in parts], axis=1)
+        part = jnp.concatenate([unfolded(p[:, mid:]) for p in parts], axis=1)
+        part = jnp.where(first, part, pltpu.roll(part, 2, 0))
+        top, low = picked(first, whole, part)
+        frame[0:8, :] = top
+        frame[8:16, :] = low
+        current = pltpu.roll(jnp.concatenate([top, low, low]), CUT, 0)
         row = (half - 16) * (1 - core)
         d_a, d_b, d = (field(state, kind, 3, row, 24)[...] for kind in range(3))
         e_a, e_b = chain(current, d_a, d_b, d)
-        put_ends(first, e_a[8:16], e_b[8:16], keep, send)
-
-
-def middle_end(inner, middle, state, inner_ends, ends, keep, send, current):
-    core, chip = place()
-    first = core == 0
-
-    def known(kind):
-        near = field(inner_ends, kind, 2, 16 * core, 8)[...]
-        rows = [field(ends, kind, 2, 8 * i, 8)[...] for i in range(3)]
-        upper = jnp.where(first, rows[1], mixed(near, rows[0]))
-        lower = jnp.where(first, mixed(rows[2], near), rows[1])
-        return jnp.concatenate([upper, lower])
-
-    @pl.when(chip == 0)
-    def _():
-        put_ends(first, known(0), known(1), keep, send)
+        kept, sent = picked(first, e_a[8:16], e_b[8:16])
+        keep[0:8, :] = kept
+        send[0:8, :] = sent
+
+
+def put_ends(first, e_a, e_b, keep, send):
+    kept, sent = picked(first, e_a, e_b)
+    keep[...] = kept
+    send[...] = sent
+
+
+def middle_end(inner, middle, state, keep, send, current):
+    core, chip = place()
+    first = core == 0
 
     @pl.when((chip > 0) & first)
     def _():
@@ -341,26 +408,19 @@
         put_ends(first, e_a[8:24], e_b[8:24], keep, send)
 
 
-def outer_end(middle, outer, state, middle_ends, ends, keep, send, current):
-    core, chip = place()
-    first = core == 0
-
-    def known(kind):
-        near = field(middle_ends, kind, 2, 16 * core, 8)[...]
-        far = field(ends, kind, 2, 8 * (1 - core), 8)[...]
-        return jnp.where(first, mixed(far, near), mixed(near, far))
-
-    @pl.when(chip == 0)
-    def _():
-        put_ends(first, known(0), known(1), keep, send)
+def outer_end(middle, outer, state, keep, send, current):
+    core, chip = place()
+    first = core == 0
 
     @pl.when((chip > 0) & first)
     def _():
-        current[...] = pltpu.roll(jnp.concatenate([outer[...], middle[...]]), CUT, 0)
+        part = pltpu.roll(unfolded(outer[...]), 2, 0)
+        current[...] = pltpu.roll(jnp.concatenate([part, middle[...]]), CUT, 0)
 
     @pl.when((chip > 0) & (core == 1))
     def _():
-        current[...] = pltpu.roll(jnp.concatenate([middle[...], outer[...]]), 24 - CUT, 0)
+        part = unfolded(outer[...])
+        current[...] = pltpu.roll(jnp.concatenate([middle[...], part]), 24 - CUT, 0)
 
     @pl.when(chip > 0)
     def _():
@@ -373,36 +433,57 @@
         put_ends(first, e_a[8:16], e_b[8:16], keep, send)
 
 
-def write_kernel(half, order, *refs):
-    count = len(order)
+def write_kernel(half, last, *refs):
+    count = 3
     pieces, out, sems = refs[:count], refs[-2], refs[-1]
-    core, _ = place()
-    copies = []
-    for i, (mine, part) in enumerate(order):
-        upper = (half - 8, 8, 0)[part]
-        lower = (half, half + 8, 2 * half - 8)[part]
-        row = pl.multiple_of(jnp.where((core == 0) == mine, upper, lower), 8)
-        piece = pieces[i]
-        copy = pltpu.make_async_copy(
-            piece, out.at[0, pl.ds(row, piece.shape[0]), :], sems.at[i]
-        )
-        copy.start()
-        copies.append(copy)
-    for copy in copies:
-        copy.wait()
-
-
-def written(half, order, pieces, shape, into=None):
+    core, chip = place()
+
+    def copy_all(order):
+        copies = []
+        for i, (mine, part, source, begin, size) in enumerate(order):
+            upper = (half - 8, 8, 0)[part]
+            lower = (half, half + 8, 2 * half - 8)[part]
+            row = pl.multiple_of(jnp.where((core == 0) == mine, upper, lower), 8)
+            copy = pltpu.make_async_copy(
+                pieces[source].at[pl.ds(begin, size), :],
+                out.at[0, pl.ds(row, size), :],
+                sems.at[i],
+            )
+            copy.start()
+            copies.append(copy)
+        for copy in copies:
+            copy.wait()
+
+    parts = ((0, 0, 8), (1, 8, half - 16), (2, half - 8, 8))
+    if last:
+
+        @pl.when(chip > 0)
+        def _():
+            copy_all(((False, 1, 0, 0, half - 16), (True, 2, 1, 0, 8), (False, 2, 2, 0, 8)))
+
+    else:
+
+        @pl.when(chip == 0)
+        def _():
+            copy_all(
+                [(mine, part, source, *rows) for mine, source in ((True, 0), (False, 2)) for part, *rows in parts]
+            )
+
+        @pl.when(chip > 0)
+        def _():
+            copy_all(((True, 0, 0, 0, 8), (True, 1, 1, 0, half - 16), (False, 0, 2, 0, 8)))
+
+
+def written(half, pieces, shape, into=None):
     vmem, anywhere = pl.BlockSpec(memory_space=pltpu.VMEM), pl.BlockSpec(memory_space=pl.ANY)
-    count = len(pieces)
     extra = () if into is None else (into,)
     return pl.pallas_call(
-        functools.partial(write_kernel, half, order),
+        functools.partial(write_kernel, half, into is not None),
         out_shape=jax.ShapeDtypeStruct(shape, jnp.float32),
-        in_specs=[vmem] * count + [anywhere] * len(extra),
+        in_specs=[vmem] * 3 + [anywhere] * len(extra),
         out_specs=anywhere,
-        input_output_aliases={count: 0} if extra else {},
-        scratch_shapes=[pltpu.SemaphoreType.DMA((count,))],
+        input_output_aliases={3: 0} if extra else {},
+        scratch_shapes=[pltpu.SemaphoreType.DMA((6,))],
         compiler_params=pltpu.CompilerParams(vmem_limit_bytes=16 << 20),
     )(*pieces, *extra)
 
@@ -499,78 +580,74 @@
     vmem = pl.BlockSpec(memory_space=pltpu.VMEM)
 
     other = routed(starts[0], partner)
-    own, held, mine_1, mine_2 = pl.pallas_call(
+    own, held, mine = pl.pallas_call(
         functools.partial(load_kernel, half),
         out_shape=[
-            jax.ShapeDtypeStruct((size, width), jnp.float32)
-            for size in (height, height, 48, 48)
+            jax.ShapeDtypeStruct((size, width), jnp.float32) for size in (height, height, 48)
         ],
         in_specs=[pl.BlockSpec(memory_space=pltpu.HBM)] * 2,
-        out_specs=[vmem] * 4,
+        out_specs=[vmem] * 3,
         scratch_shapes=[pltpu.SemaphoreType.DMA((6,))],
-        compiler_params=pltpu.CompilerParams(vmem_limit_bytes=50 << 20),
+        compiler_params=pltpu.CompilerParams(vmem_limit_bytes=51 << 20),
         cost_estimate=pl.CostEstimate(
-            flops=60 * 48 * width, bytes_accessed=16 * height * width, transcendentals=0
+            flops=60 * 24 * width, bytes_accessed=16 * height * width, transcendentals=0
         ),
         name="load",
     )(starts, drive)
-    sent_1, ends_1, edge = compute(
-        functools.partial(inner_kernel, half),
-        [(16, width), (48, width), (24, width)],
-        (own, other, held, mine_1),
-        name="inner",
-    )
-    here_1 = routed(sent_1, stage_swap(0))
+    mid = width // 2
+    packed = mid * 7 // 4
+    sent_l, ends_l = compute(
+        functools.partial(inner_kernel, half, 0), [(8, packed), (48, mid)], (own, other, held, mine)
+    )
+    here_l = routed(sent_l, stage_swap(0))
+    sent_r, ends_r, edge = compute(
+        functools.partial(inner_kernel, half, 1),
+        [(8, packed), (48, mid), (24, width)],
+        (own, other, held, after(mine, sent_l)),
+    )
+    here_r = routed(sent_r, stage_swap(0))
     got = routed(edge, outward(groups, rows))
     sent_2, ends_2 = compute(
         functools.partial(middle_kernel, half),
         [(16, width), (48, width)],
-        (own, other, held, mine_2),
-        name="middle",
+        (own, other, after(held, sent_r)),
     )
     here_2 = routed(sent_2, stage_swap(0))
     (state,) = compute(
         functools.partial(state_kernel, half),
         [(3 * (half + WIDE), width)],
         (own, other, after(held, sent_2)),
-        name="state",
     )
     sent_3, ends_3, state_3 = compute(
         functools.partial(outer_kernel, half),
-        [(8, width), (32, width), (3 * 24, width)],
+        [(8, width * 3 // 4), (32, width), (3 * 24, width)],
         (own, other, held, got, state),
-        name="outer",
     )
     here_3 = routed(sent_3, stage_swap(0))
 
-    keep_1, send_1 = compute(
+    keep_1, send_1, frame = compute(
         functools.partial(inner_end, half),
-        [(8, width)] * 2,
-        (here_1, state, after(ends_1, sent_3)),
-        name="inner_end",
+        [(half, width), (half, width), (16, width)],
+        (here_l, here_r, state, ends_l, ends_r, ends_2, ends_3),
     )
     back_1 = routed(send_1, partner)
     keep_2, send_2 = compute(
         middle_end,
-        [(16, width)] * 2,
-        (here_1, here_2, state, ends_1, after(ends_2, keep_1)),
+        [(half - 16, width)] * 2,
+        (frame, here_2, state),
         scratch_shapes=[pltpu.VMEM((32, width), jnp.float32)],
-        name="middle_end",
     )
     back_2 = routed(send_2, partner)
-    out = written(half, ((True, 0), (True, 1), (False, 0)), (keep_1, keep_2, back_1), starts.shape)
-    out, ends_3 = lax.optimization_barrier((out, ends_3))
+    out = written(half, (keep_1, keep_2, back_1), starts.shape)
+    out, state_3 = lax.optimization_barrier((out, state_3))
     keep_3, send_3 = compute(
         outer_end,
         [(8, width)] * 2,
-        (here_2, here_3, state_3, ends_2, ends_3),
+        (here_2, here_3, state_3),
         scratch_shapes=[pltpu.VMEM((24, width), jnp.float32)],
-        name="outer_end",
     )
     back_3 = routed(send_3, partner)
-    return written(
-        half, ((False, 1), (True, 2), (False, 2)), (back_2, keep_3, back_3), starts.shape, into=out
-    )
+    return written(half, (back_2, keep_3, back_3), starts.shape, into=out)
 
 
 def solution(mesh):

time: 26.7 us -> 30.9 us (1.16)
  starting transfers between devices: 4.48 us -> 7.55 us
  waiting for transfers between devices: 13 us -> 14.6 us
  Pallas kernels: 9 us -> 8.53 us
    ppermute x8 -> x9, starting transfers between devices: 4.48 us -> 7.55 us  [routed(): return lax.ppermute(block, AXES, pairs)]
    ppermute x8 -> x9, waiting for transfers between devices: 13 us -> 14.6 us  [routed(): return lax.ppermute(block, AXES, pairs)]
    pallas_call x7 -> x8, Pallas kernels: 4.33 us -> 5.32 us  [compute(): pl.pallas_call(kernel, out_shape=shapes, in_specs=[vmem] * len(args), out...]
    pallas_call x1, Pallas kernels: 3.04 us -> 2.15 us  [two_chips(): pl.pallas_call(functools.partial(load_kernel, half), out_shape=[jax.Shape...]
    pallas_call x2, Pallas kernels: 1.64 us -> 1.06 us  [written(): pl.pallas_call(functools.partial(write_kernel, half, into is not None), o...]
  transfers between devices with their start and end apart: 8 -> 9, of which waited for: 5 -> 6; matrix products, arithmetic and copies ran while one was open for 0% -> 0% of each run, Pallas kernels for 26% -> 22%
where the time goes in v5:
time: 30.9 us; the launch traced here: 30.7 us
  waiting for transfers between devices  14.6 us (47%)
  Pallas kernels  8.53 us (28%)
  starting transfers between devices  7.55 us (24%)
    ppermute x9, waiting for transfers between devices, routed(): return lax.ppermute(block, AXES, pairs)  14.6 us
    ppermute x9, starting transfers between devices, routed(): return lax.ppermute(block, AXES, pairs)  7.55 us
    pallas_call x8, Pallas kernels, compute(): pl.pallas_call(kernel, out_shape=shapes, in_specs=[vmem] * len(args), out...  5.32 us
    pallas_call x1, Pallas kernels, two_chips(): pl.pallas_call(functools.partial(load_kernel, half), out_shape=[jax.Shape...  2.15 us
    pallas_call x2, Pallas kernels, written(): pl.pallas_call(functools.partial(write_kernel, half, into is not None), o...  1.06 us
  transfers between devices with their start and end apart: 9, of which 6 were waited for; matrix products, arithmetic and copies ran while one was open for 0% of the time, Pallas kernels for 22%

profile of v5, /device:TPU:0, one launch (start us, length us, event | category | flops | bytes accessed | tf_op | source)
XLA Modules:
  0.0 30.7 jit_solution(13545262734181070156)
XLA Ops:
  0.0 0.5 %collective-permute-start = (f32[64,4096]{1,0:T(8,128)}, f32[64,4096]{1,0:T(8,128)S(1)}, u32[]{:S(2)}, u32[]{:S(2)}) collective-permute-start(f32[64,4096]{1,0:T(8,128)} %bitcast.1), channel_id=1, source_target_pairs={{0,4},{1,5},{2,6},{3,7},{4,0},{5,1},{6,2},{7,3},{8,12},{9,13},{10,... | collective-permute-start | bytes 3145736 | tf_op jit(solution)/shard_map/ppermute | solution.py:33
  0.5 2.1 %load.1 = (f32[64,4096]{1,0:T(8,128)S(1)}, f32[64,4096]{1,0:T(8,128)S(1)}, f32[48,4096]{1,0:T(8,128)S(1)}) custom-call(f32[1,64,4096]{2,1,0:T(8,128)} %starts.1, f32[64,4096]{1,0:T(8,128)} %drive.1), custom_call_target="tpu_custom_call" | custom-call | flops 5898240 | bytes 4194304 | tf_op jit(solution)/shard_map/load/pallas_call | solution.py:583
  2.6 0.3 %collective-permute-done.other = f32[64,4096]{1,0:T(8,128)S(1)} collective-permute-done((f32[64,4096]{1,0:T(8,128)}, f32[64,4096]{1,0:T(8,128)S(1)}, u32[]{:S(2)}, u32[]{:S(2)}) %collective-permute-start) | collective-permute-done | bytes 1048608 | tf_op jit(solution)/shard_map/ppermute | solution.py:33
  3.0 0.7 %shard_map.28 = (f32[8,3584]{1,0:T(8,128)S(1)}, f32[48,2048]{1,0:T(8,128)S(1)}) custom-call(f32[64,4096]{1,0:T(8,128)S(1)} %get-tuple-element.30.own, f32[64,4096]{1,0:T(8,128)S(1)} %collective-permute-done.other, f32[64,4096]{1,0:T(8,128)S(1)} %get-tuple-element.38.drive, f32[48,4096]{1,0:T(8,128)S(1)} %get-tuple-element.34.mine), custom_call_target="tpu_custom_call" | custom-call | tf_op jit(solution)/shard_map/pallas_call | solution.py:90
  3.7 0.8 %shard_map.29 = (f32[8,3584]{1,0:T(8,128)S(1)}, f32[48,2048]{1,0:T(8,128)S(1)}, f32[24,4096]{1,0:T(8,128)S(1)}) custom-call(f32[64,4096]{1,0:T(8,128)S(1)} %get-tuple-element.30.own, f32[64,4096]{1,0:T(8,128)S(1)} %collective-permute-done.other, f32[64,4096]{1,0:T(8,128)S(1)} %get-tuple-element.38.drive, f32[48,4096]{1,0:T(8,128)S(1)} %get-tuple-element.34.mine), custom_call_target="tpu_custom_call" | custom-call | tf_op jit(solution)/shard_map/pallas_call | solution.py:90
  4.5 2.9 %collective-permute-start.3 = (f32[24,4096]{1,0:T(8,128)S(1)}, f32[24,4096]{1,0:T(8,128)S(1)}, u32[]{:S(2)}, u32[]{:S(2)}) collective-permute-start(f32[24,4096]{1,0:T(8,128)S(1)} %get-tuple-element.42), channel_id=1, source_target_pairs={{0,16},{1,4},{2,5},{3,6},{4,1},{5,2},{6,3},{7,23},{8,24},{9,12},{1... | collective-permute-start | bytes 1179656 | tf_op jit(solution)/shard_map/ppermute | solution.py:33
  7.5 0.0 collective-permute-start.2
  7.5 2.0 %collective-permute-start.1 = (f32[8,3584]{1,0:T(8,128)S(1)}, f32[8,3584]{1,0:T(8,128)S(1)}, u32[]{:S(2)}, u32[]{:S(2)}) collective-permute-start(f32[8,3584]{1,0:T(8,128)S(1)} %get-tuple-element.33), channel_id=1, source_target_pairs={{0,8},{1,9},{2,10},{3,11},{4,12},{5,13},{6,14},{7,15},{8,0},{9,1},... | collective-permute-start | bytes 344072 | tf_op jit(solution)/shard_map/ppermute | solution.py:33
  9.5 2.1 %shard_map.30 = (f32[16,4096]{1,0:T(8,128)S(1)}, f32[48,4096]{1,0:T(8,128)S(1)}) custom-call(f32[64,4096]{1,0:T(8,128)S(1)} %get-tuple-element.30.own, f32[64,4096]{1,0:T(8,128)S(1)} %collective-permute-done.other, f32[64,4096]{1,0:T(8,128)S(1)} %get-tuple-element.38.drive), custom_call_target="tpu_custom_call" | custom-call | tf_op jit(solution)/shard_map/pallas_call | solution.py:90
  11.6 1.6 %collective-permute-done.3.got = f32[24,4096]{1,0:T(8,128)S(1)} collective-permute-done((f32[24,4096]{1,0:T(8,128)S(1)}, f32[24,4096]{1,0:T(8,128)S(1)}, u32[]{:S(2)}, u32[]{:S(2)}) %collective-permute-start.3) | collective-permute-done | bytes 393248 | tf_op jit(solution)/shard_map/ppermute | solution.py:33
  13.2 1.5 %shard_map.32 = (f32[8,3072]{1,0:T(8,128)S(1)}, f32[32,4096]{1,0:T(8,128)S(1)}, f32[72,4096]{1,0:T(8,128)S(1)}) custom-call(f32[64,4096]{1,0:T(8,128)S(1)} %get-tuple-element.30.own, f32[64,4096]{1,0:T(8,128)S(1)} %collective-permute-done.other, f32[64,4096]{1,0:T(8,128)S(1)} %get-tuple-element.38.drive, f32[24,4096]{1,0:T(8,128)S(1)} %collective-permute-done.3.got, ...), custom_call_target="tpu_custom_call" | custom-call | tf_op jit(solution)/shard_map/pallas_call | solution.py:90
  14.8 0.0 collective-permute-done.2.right
  14.8 0.4 %collective-permute-done.1.left = f32[8,3584]{1,0:T(8,128)S(1)} collective-permute-done((f32[8,3584]{1,0:T(8,128)S(1)}, f32[8,3584]{1,0:T(8,128)S(1)}, u32[]{:S(2)}, u32[]{:S(2)}) %collective-permute-start.1) | collective-permute-done | bytes 114720 | tf_op jit(solution)/shard_map/ppermute | solution.py:33
  15.1 0.2 shard_map.33
  15.3 0.1 collective-permute-start.7
  15.4 0.6 %collective-permute-start.4 = (f32[16,4096]{1,0:T(8,128)S(1)}, f32[16,4096]{1,0:T(8,128)S(1)}, u32[]{:S(2)}, u32[]{:S(2)}) collective-permute-start(f32[16,4096]{1,0:T(8,128)S(1)} %get-tuple-element.37), channel_id=1, source_target_pairs={{0,8},{1,9},{2,10},{3,11},{4,12},{5,13},{6,14},{7,15},{8,0},{9,1},... | collective-permute-start | bytes 786440 | tf_op jit(solution)/shard_map/ppermute | solution.py:33
  16.0 8.1 %collective-permute-done.4.middle = f32[16,4096]{1,0:T(8,128)S(1)} collective-permute-done((f32[16,4096]{1,0:T(8,128)S(1)}, f32[16,4096]{1,0:T(8,128)S(1)}, u32[]{:S(2)}, u32[]{:S(2)}) %collective-permute-start.4) | collective-permute-done | bytes 262176 | tf_op jit(solution)/shard_map/ppermute | solution.py:33
  24.1 0.0 collective-permute-start.5
  24.1 1.4 %collective-permute-start.6 = (f32[8,3072]{1,0:T(8,128)S(1)}, f32[8,3072]{1,0:T(8,128)S(1)}, u32[]{:S(2)}, u32[]{:S(2)}) collective-permute-start(f32[8,3072]{1,0:T(8,128)S(1)} %get-tuple-element.46), channel_id=1, source_target_pairs={{0,8},{1,9},{2,10},{3,11},{4,12},{5,13},{6,14},{7,15},{8,0},{9,1},... | collective-permute-start | bytes 294920 | tf_op jit(solution)/shard_map/ppermute | solution.py:33
  25.5 0.0 collective-permute-done.7.refs_2_
  25.5 1.0 %shard_map.35.refs_3_ = f32[1,64,4096]{2,1,0:T(8,128)} custom-call(f32[32,4096]{1,0:T(8,128)S(1)} %get-tuple-element.47.refs_0_, f32[16,4096]{1,0:T(8,128)S(1)} %get-tuple-element.48.refs_1_, f32[32,4096]{1,0:T(8,128)S(1)} %collective-permute-done.7.refs_2_), custom_call_target="tpu_custom_call" | custom-call | tf_op jit(solution)/shard_map/pallas_call | solution.py:480
  26.5 2.8 %collective-permute-done.6.outer = f32[8,3072]{1,0:T(8,128)S(1)} collective-permute-done((f32[8,3072]{1,0:T(8,128)S(1)}, f32[8,3072]{1,0:T(8,128)S(1)}, u32[]{:S(2)}, u32[]{:S(2)}) %collective-permute-start.6) | collective-permute-done | bytes 98336 | tf_op jit(solution)/shard_map/ppermute | solution.py:33
  29.3 0.0 collective-permute-start.8
  29.3 0.0 collective-permute-done.5.refs_0_
  29.3 1.3 %collective-permute-done.8.refs_2_ = f32[8,4096]{1,0:T(8,128)S(1)} collective-permute-done((f32[8,4096]{1,0:T(8,128)S(1)}, f32[8,4096]{1,0:T(8,128)S(1)}, u32[]{:S(2)}, u32[]{:S(2)}) %collective-permute-start.8) | collective-permute-done | bytes 131104 | tf_op jit(solution)/shard_map/ppermute | solution.py:33
  30.7 0.1 shard_map.37
  (3 shorter events, 0.0 us)
Async XLA Ops:
  0.0 3.0 %collective-permute-start = (f32[64,4096]{1,0:T(8,128)}, f32[64,4096]{1,0:T(8,128)S(1)}, u32[]{:S(2)}, u32[]{:S(2)}) collective-permute-start(f32[64,4096]{1,0:T(8,128)} %bitcast.1), channel_id=1, source_target_pairs={{0,4},{1,5},{2,6},{3,7},{4,0},{5,1},{6,2},{7,3},{8,12},{9,13},{10,... | collective-permute-start | bytes 3145736 | tf_op jit(solution)/shard_map/ppermute | solution.py:33
  4.5 8.7 %collective-permute-start.3 = (f32[24,4096]{1,0:T(8,128)S(1)}, f32[24,4096]{1,0:T(8,128)S(1)}, u32[]{:S(2)}, u32[]{:S(2)}) collective-permute-start(f32[24,4096]{1,0:T(8,128)S(1)} %get-tuple-element.42), channel_id=1, source_target_pairs={{0,16},{1,4},{2,5},{3,6},{4,1},{5,2},{6,3},{7,23},{8,24},{9,12},{1... | collective-permute-start | bytes 1179656 | tf_op jit(solution)/shard_map/ppermute | solution.py:33
  7.5 7.3 %collective-permute-start.2 = (f32[8,3584]{1,0:T(8,128)S(1)}, f32[8,3584]{1,0:T(8,128)S(1)}, u32[]{:S(2)}, u32[]{:S(2)}) collective-permute-start(f32[8,3584]{1,0:T(8,128)S(1)} %get-tuple-element.35), channel_id=1, source_target_pairs={{0,8},{1,9},{2,10},{3,11},{4,12},{5,13},{6,14},{7,15},{8,0},{9,1},... | collective-permute-start | bytes 344072 | tf_op jit(solution)/shard_map/ppermute | solution.py:33
  7.5 7.7 %collective-permute-start.1 = (f32[8,3584]{1,0:T(8,128)S(1)}, f32[8,3584]{1,0:T(8,128)S(1)}, u32[]{:S(2)}, u32[]{:S(2)}) collective-permute-start(f32[8,3584]{1,0:T(8,128)S(1)} %get-tuple-element.33), channel_id=1, source_target_pairs={{0,8},{1,9},{2,10},{3,11},{4,12},{5,13},{6,14},{7,15},{8,0},{9,1},... | collective-permute-start | bytes 344072 | tf_op jit(solution)/shard_map/ppermute | solution.py:33
  15.3 10.2 %collective-permute-start.7 = (f32[32,4096]{1,0:T(8,128)S(1)}, f32[32,4096]{1,0:T(8,128)S(1)}, u32[]{:S(2)}, u32[]{:S(2)}) collective-permute-start(f32[32,4096]{1,0:T(8,128)S(1)} %get-tuple-element.49), channel_id=1, source_target_pairs={{0,4},{1,5},{2,6},{3,7},{4,0},{5,1},{6,2},{7,3},{8,12},{9,13},{10,... | collective-permute-start | bytes 1572872 | tf_op jit(solution)/shard_map/ppermute | solution.py:33
  15.4 8.7 %collective-permute-start.4 = (f32[16,4096]{1,0:T(8,128)S(1)}, f32[16,4096]{1,0:T(8,128)S(1)}, u32[]{:S(2)}, u32[]{:S(2)}) collective-permute-start(f32[16,4096]{1,0:T(8,128)S(1)} %get-tuple-element.37), channel_id=1, source_target_pairs={{0,8},{1,9},{2,10},{3,11},{4,12},{5,13},{6,14},{7,15},{8,0},{9,1},... | collective-permute-start | bytes 786440 | tf_op jit(solution)/shard_map/ppermute | solution.py:33
  24.1 5.2 %collective-permute-start.5 = (f32[16,4096]{1,0:T(8,128)S(1)}, f32[16,4096]{1,0:T(8,128)S(1)}, u32[]{:S(2)}, u32[]{:S(2)}) collective-permute-start(f32[16,4096]{1,0:T(8,128)S(1)} %get-tuple-element.45), channel_id=1, source_target_pairs={{0,4},{1,5},{2,6},{3,7},{4,0},{5,1},{6,2},{7,3},{8,12},{9,13},{10,... | collective-permute-start | bytes 786440 | tf_op jit(solution)/shard_map/ppermute | solution.py:33
  24.1 5.2 %collective-permute-start.6 = (f32[8,3072]{1,0:T(8,128)S(1)}, f32[8,3072]{1,0:T(8,128)S(1)}, u32[]{:S(2)}, u32[]{:S(2)}) collective-permute-start(f32[8,3072]{1,0:T(8,128)S(1)} %get-tuple-element.46), channel_id=1, source_target_pairs={{0,8},{1,9},{2,10},{3,11},{4,12},{5,13},{6,14},{7,15},{8,0},{9,1},... | collective-permute-start | bytes 294920 | tf_op jit(solution)/shard_map/ppermute | solution.py:33
  29.3 1.3 %collective-permute-start.8 = (f32[8,4096]{1,0:T(8,128)S(1)}, f32[8,4096]{1,0:T(8,128)S(1)}, u32[]{:S(2)}, u32[]{:S(2)}) collective-permute-start(f32[8,4096]{1,0:T(8,128)S(1)} %get-tuple-element.53), channel_id=1, source_target_pairs={{0,4},{1,5},{2,6},{3,7},{4,0},{5,1},{6,2},{7,3},{8,12},{9,13},{10,... | collective-permute-start | bytes 393224 | tf_op jit(solution)/shard_map/ppermute | solution.py:33

commit v6 on v5

--- a/solution.py
+++ b/solution.py
@@ -245,12 +245,11 @@
     if edge is not None:
         rows = pl.ds(outer_row(half, core), 8)
         a, b = picked(first, own[rows, :], other[rows, :])
-        edge[0:8, :] = a
-        edge[8:16, :] = b
-        edge[16:24, :] = drive[rows, :]
-
-
-def middle_kernel(half, own, other, drive, sent, ends):
+        fields = (jnp.where(first, v, pltpu.roll(v, 6, 0)) for v in (a, b, drive[rows, :]))
+        edge[...] = jnp.concatenate([folded(v) for v in fields], axis=1)
+
+
+def middle_kernel(half, own, other, drive, sent, ends, delta):
     core, chip = place()
     first = core == 0
 
@@ -264,44 +263,55 @@
         ends[0:24, :] = e_a
         ends[24:48, :] = e_b
 
-
-def state_kernel(half, own, other, drive, state):
-    core, chip = place()
-    first = core == 0
-
     @pl.when(chip > 0)
     def _():
-        size = half + WIDE
-        rows = pl.ds(pl.multiple_of((half - WIDE) * core, 8), size)
-        d = drive[rows, :]
-        state[2 * size : 3 * size, :] = d
-        for mine_first, ref in ((True, own), (False, other)):
-            fine, coarse = start_of(ref[rows, :], d)
-            kind = jnp.where(first == mine_first, 0, 1)
-            field(state, kind, 3, 0, size)[...] = fine - coarse
-
-
-def outer_kernel(half, own, other, drive, got, inner_state, sent, ends, state):
-    core, chip = place()
+        rows = receiver_rows(half, core)
+        fine, coarse = start_of(own[rows, :], drive[rows, :])
+        delta[...] = fine - coarse
+
+
+def receiver_rows(half, core):
+    return pl.ds(pl.multiple_of((half - WIDE) * core, 8), half + WIDE)
+
+
+def state_kernel(half, other, drive, theirs):
+    core, chip = place()
+
+    @pl.when(chip > 0)
+    def _():
+        rows = receiver_rows(half, core)
+        fine, coarse = start_of(other[rows, :], drive[rows, :])
+        theirs[...] = fine - coarse
+
+
+def outer_window(half, own, other, drive, got):
+    core, _ = place()
     first = core == 0
     rows = pl.ds(outer_row(half, core), 8)
     a, b = picked(first, own[rows, :], other[rows, :])
     near = (a, b, drive[rows, :])
-    far = [got[8 * i : 8 * i + 8, :] for i in range(3)]
+    size = got.shape[1] // 3
+    far = [unfolded(got[:, i * size : (i + 1) * size]) for i in range(3)]
+    far = [jnp.where(first, pltpu.roll(v, 2, 0), v) for v in far]
     upper = [jnp.where(first, f, n) for f, n in zip(far, near)]
     lower = [jnp.where(first, n, f) for f, n in zip(far, near)]
     a, b, d = (jnp.concatenate(p) for p in zip(upper, lower))
-    tile = lax.broadcasted_iota(jnp.int32, a.shape, 0) // 8
-    inside = ~(at_edge(core) & (tile == core))
+    inside = ~(at_edge(core) & (sublane(a) // 8 == core))
 
     def kept(v):
         return jnp.where(inside, v, 0.0)
 
-    f_a, g_a = start_of(kept(a), d, kept)
-    f_b, g_b = start_of(kept(b), d, kept)
+    return kept(a), kept(b), d, kept
+
+
+def outer_kernel(half, own, other, drive, got, sent, ends):
+    core, chip = place()
+    first = core == 0
 
     @pl.when(chip == 0)
     def _():
+        a, b, d, kept = outer_window(half, own, other, drive, got)
+        (f_a, g_a), (f_b, g_b) = start_of(a, d, kept), start_of(b, d, kept)
         e_a = g_a + (f_a - g_a)
         e_b = kept(coarse_of(e_a, around(e_a), d)) + (f_b - g_b)
         frame = pltpu.roll(e_b, 16 - CUT, 0)[:8]
@@ -309,38 +319,51 @@
         ends[0:16, :] = e_a
         ends[16:32, :] = e_b
 
-    size = half + WIDE
-    fields = (f_a - g_a, f_b - g_b, d)
-
-    @pl.when((chip > 0) & first)
-    def _():
-        for kind, v in enumerate(fields):
-            before = field(inner_state, kind, 3, 0, 16)[...]
-            field(state, kind, 3, 0, 8)[...] = v[:8]
-            field(state, kind, 3, 8, 8)[...] = mixed(v[8:], before[:8])
-            field(state, kind, 3, 16, 8)[...] = before[8:]
-
-    @pl.when((chip > 0) & (core == 1))
-    def _():
-        for kind, v in enumerate(fields):
-            before = field(inner_state, kind, 3, size - 16, 16)[...]
-            field(state, kind, 3, 0, 8)[...] = before[:8]
-            field(state, kind, 3, 8, 8)[...] = mixed(before[8:], v[:8])
-            field(state, kind, 3, 16, 8)[...] = v[8:]
-
-
-def put_ends(first, e_a, e_b, keep, send):
-    kept, sent = picked(first, e_a, e_b)
-    keep[...] = kept
-    send[...] = sent
-
-
-def inner_end(
-    half, left, right, state, ends_left, ends_right, middle, outer, keep, send, frame
-):
-    core, chip = place()
-    first = core == 0
-    mid = ends_left.shape[1]
+
+def outer_state_kernel(half, own, other, drive, got, mine, theirs, state):
+    core, chip = place()
+    first = core == 0
+
+    @pl.when(chip > 0)
+    def _():
+        a, b, d, kept = outer_window(half, own, other, drive, got)
+        (f_a, g_a), (f_b, g_b) = start_of(a, d, kept), start_of(b, d, kept)
+        rows = pl.ds(pl.multiple_of((half - WIDE) * core, 8), 16)
+        before = picked(first, mine[rows, :], theirs[rows, :])
+        d_rows = pl.ds(pl.multiple_of((2 * half - 16) * core, 8), 16)
+        fields = zip((f_a - g_a, f_b - g_b, d), (*before, drive[d_rows, :]))
+        for kind, (v, near) in enumerate(fields):
+            top = jnp.where(first, v[:8], near[:8])
+            mid = jnp.where(first, mixed(v[8:], near[:8]), mixed(near[8:], v[:8]))
+            low = jnp.where(first, near[8:], v[8:])
+            state[24 * kind : 24 * kind + 24, :] = jnp.concatenate([top, mid, low])
+
+
+def inner_end(half, left, right, drive, mine, theirs, keep, send, frame):
+    core, chip = place()
+    first = core == 0
+
+    @pl.when(chip > 0)
+    def _():
+        mid = left.shape[1] * 4 // 7
+        parts = left[...], right[...]
+        whole = jnp.concatenate([p[:, :mid] for p in parts], axis=1)
+        part = jnp.concatenate([unfolded(p[:, mid:]) for p in parts], axis=1)
+        part = jnp.where(first, part, pltpu.roll(part, 2, 0))
+        top, low = picked(first, whole, part)
+        frame[0:8, :] = top
+        frame[8:16, :] = low
+        current = pltpu.roll(jnp.concatenate([top, low, low]), CUT, 0)
+        rows = pl.ds(pl.multiple_of((half - 16) * (1 - core), 8), 24)
+        d_a, d_b = picked(first, mine[rows, :], theirs[rows, :])
+        d = drive[pl.ds(inner_row(half, core), 24), :]
+        e_a, e_b = chain(current, d_a, d_b, d)
+        put_ends(first, e_a[8:16], e_b[8:16], keep, send)
+
+
+def gather_kernel(ends_left, ends_right, middle, outer, keep_8, send_8, keep, send):
+    core, chip = place()
+    first = core == 0
 
     @pl.when(chip == 0)
     def _():
@@ -361,26 +384,12 @@
                 ]
             )
 
-        kept, sent = picked(first, known(0), known(1))
-        keep[...] = kept
-        send[...] = sent
+        put_ends(first, known(0), known(1), keep, send)
 
     @pl.when(chip > 0)
     def _():
-        parts = left[...], right[...]
-        whole = jnp.concatenate([p[:, :mid] for p in parts], axis=1)
-        part = jnp.concatenate([unfolded(p[:, mid:]) for p in parts], axis=1)
-        part = jnp.where(first, part, pltpu.roll(part, 2, 0))
-        top, low = picked(first, whole, part)
-        frame[0:8, :] = top
-        frame[8:16, :] = low
-        current = pltpu.roll(jnp.concatenate([top, low, low]), CUT, 0)
-        row = (half - 16) * (1 - core)
-        d_a, d_b, d = (field(state, kind, 3, row, 24)[...] for kind in range(3))
-        e_a, e_b = chain(current, d_a, d_b, d)
-        kept, sent = picked(first, e_a[8:16], e_b[8:16])
-        keep[0:8, :] = kept
-        send[0:8, :] = sent
+        keep[0:8, :] = keep_8[...]
+        send[0:8, :] = send_8[...]
 
 
 def put_ends(first, e_a, e_b, keep, send):
@@ -389,7 +398,7 @@
     send[...] = sent
 
 
-def middle_end(inner, middle, state, keep, send, current):
+def middle_end(half, inner, middle, drive, mine, theirs, keep, send, current):
     core, chip = place()
     first = core == 0
 
@@ -399,13 +408,15 @@
 
     @pl.when((chip > 0) & (core == 1))
     def _():
-        current[...] = pltpu.roll(jnp.concatenate([inner[...], middle[...]]), 32 - CUT, 0)
+        current[...] = pltpu.roll(jnp.concatenate([inner[...], middle[...]]), half - CUT, 0)
 
     @pl.when(chip > 0)
     def _():
-        d_a, d_b, d = (field(state, kind, 3, 8 * core, 32)[...] for kind in range(3))
+        rows = pl.ds(pl.multiple_of(8 * core, 8), half)
+        d_a, d_b = picked(first, mine[rows, :], theirs[rows, :])
+        d = drive[pl.ds(pl.multiple_of(half * core, 8), half), :]
         e_a, e_b = chain(current[...], d_a, d_b, d)
-        put_ends(first, e_a[8:24], e_b[8:24], keep, send)
+        put_ends(first, e_a[8 : half - 8], e_b[8 : half - 8], keep, send)
 
 
 def outer_end(middle, outer, state, keep, send, current):
@@ -602,40 +613,45 @@
     here_l = routed(sent_l, stage_swap(0))
     sent_r, ends_r, edge = compute(
         functools.partial(inner_kernel, half, 1),
-        [(8, packed), (48, mid), (24, width)],
+        [(8, packed), (48, mid), (8, width * 9 // 4)],
         (own, other, held, after(mine, sent_l)),
     )
     here_r = routed(sent_r, stage_swap(0))
     got = routed(edge, outward(groups, rows))
-    sent_2, ends_2 = compute(
+    sent_2, ends_2, delta_own = compute(
         functools.partial(middle_kernel, half),
-        [(16, width), (48, width)],
+        [(16, width), (48, width), (half + WIDE, width)],
         (own, other, after(held, sent_r)),
     )
     here_2 = routed(sent_2, stage_swap(0))
-    (state,) = compute(
-        functools.partial(state_kernel, half),
-        [(3 * (half + WIDE), width)],
-        (own, other, after(held, sent_2)),
-    )
-    sent_3, ends_3, state_3 = compute(
+    (delta_other,) = compute(
+        functools.partial(state_kernel, half), [(half + WIDE, width)], (other, after(held, sent_2))
+    )
+    keep_8, send_8, frame = compute(
+        functools.partial(inner_end, half),
+        [(8, width), (8, width), (16, width)],
+        (here_l, here_r, held, delta_own, delta_other),
+    )
+    sent_3, ends_3 = compute(
         functools.partial(outer_kernel, half),
-        [(8, width * 3 // 4), (32, width), (3 * 24, width)],
-        (own, other, held, got, state),
+        [(8, width * 3 // 4), (32, width)],
+        (own, other, after(held, frame), got),
     )
     here_3 = routed(sent_3, stage_swap(0))
-
-    keep_1, send_1, frame = compute(
-        functools.partial(inner_end, half),
-        [(half, width), (half, width), (16, width)],
-        (here_l, here_r, state, ends_l, ends_r, ends_2, ends_3),
+    (state_3,) = compute(
+        functools.partial(outer_state_kernel, half),
+        [(3 * 24, width)],
+        (own, other, after(held, sent_3), got, delta_own, delta_other),
+    )
+    keep_1, send_1 = compute(
+        gather_kernel, [(half, width)] * 2, (ends_l, ends_r, ends_2, ends_3, keep_8, send_8)
     )
     back_1 = routed(send_1, partner)
     keep_2, send_2 = compute(
-        middle_end,
+        functools.partial(middle_end, half),
         [(half - 16, width)] * 2,
-        (frame, here_2, state),
-        scratch_shapes=[pltpu.VMEM((32, width), jnp.float32)],
+        (frame, here_2, held, delta_own, after(delta_other, state_3)),
+        scratch_shapes=[pltpu.VMEM((half, width), jnp.float32)],
     )
     back_2 = routed(send_2, partner)
     out = written(half, (keep_1, keep_2, back_1), starts.shape)

time: 30.9 us -> 32.6 us (1.055)
  waiting for transfers between devices: 14.6 us -> 16.7 us
  starting transfers between devices: 7.55 us -> 6.8 us
    ppermute x9, waiting for transfers between devices: 14.6 us -> 16.7 us  [routed(): return lax.ppermute(block, AXES, pairs)]
    ppermute x9, starting transfers between devices: 7.55 us -> 6.8 us  [routed(): return lax.ppermute(block, AXES, pairs)]
    pallas_call x8 -> x10, Pallas kernels: 5.32 us -> 5.51 us  [compute(): pl.pallas_call(kernel, out_shape=shapes, in_specs=[vmem] * len(args), out...]
  transfers between devices with their start and end apart: 9 -> 9, of which waited for: 6 -> 6; matrix products, arithmetic and copies ran while one was open for 0% -> 0% of each run, Pallas kernels for 22% -> 17%
where the time goes in v6:
time: 32.6 us; the launch traced here: 32.4 us
  waiting for transfers between devices  16.7 us (51%)
  Pallas kernels  8.72 us (27%)
  starting transfers between devices  6.8 us (21%)
    ppermute x9, waiting for transfers between devices, routed(): return lax.ppermute(block, AXES, pairs)  16.7 us
    ppermute x9, starting transfers between devices, routed(): return lax.ppermute(block, AXES, pairs)  6.8 us
    pallas_call x10, Pallas kernels, compute(): pl.pallas_call(kernel, out_shape=shapes, in_specs=[vmem] * len(args), out...  5.51 us
    pallas_call x1, Pallas kernels, two_chips(): pl.pallas_call(functools.partial(load_kernel, half), out_shape=[jax.Shape...  2.15 us
    pallas_call x2, Pallas kernels, written(): pl.pallas_call(functools.partial(write_kernel, half, into is not None), o...  1.06 us
  transfers between devices with their start and end apart: 9, of which 6 were waited for; matrix products, arithmetic and copies ran while one was open for 0% of the time, Pallas kernels for 17%

profile of v6, /device:TPU:0, one launch (start us, length us, event | category | flops | bytes accessed | tf_op | source)
XLA Modules:
  0.0 32.4 jit_solution(5025135973853921585)
XLA Ops:
  0.0 0.5 %collective-permute-start = (f32[64,4096]{1,0:T(8,128)}, f32[64,4096]{1,0:T(8,128)S(1)}, u32[]{:S(2)}, u32[]{:S(2)}) collective-permute-start(f32[64,4096]{1,0:T(8,128)} %bitcast.1), channel_id=1, source_target_pairs={{0,4},{1,5},{2,6},{3,7},{4,0},{5,1},{6,2},{7,3},{8,12},{9,13},{10,... | collective-permute-start | bytes 3145736 | tf_op jit(solution)/shard_map/ppermute | solution.py:33
  0.5 2.1 %load.1 = (f32[64,4096]{1,0:T(8,128)S(1)}, f32[64,4096]{1,0:T(8,128)S(1)}, f32[48,4096]{1,0:T(8,128)S(1)}) custom-call(f32[1,64,4096]{2,1,0:T(8,128)} %starts.1, f32[64,4096]{1,0:T(8,128)} %drive.1), custom_call_target="tpu_custom_call" | custom-call | flops 5898240 | bytes 4194304 | tf_op jit(solution)/shard_map/load/pallas_call | solution.py:594
  2.6 0.3 %collective-permute-done.other = f32[64,4096]{1,0:T(8,128)S(1)} collective-permute-done((f32[64,4096]{1,0:T(8,128)}, f32[64,4096]{1,0:T(8,128)S(1)}, u32[]{:S(2)}, u32[]{:S(2)}) %collective-permute-start) | collective-permute-done | bytes 1048608 | tf_op jit(solution)/shard_map/ppermute | solution.py:33
  3.0 0.7 %shard_map.28 = (f32[8,3584]{1,0:T(8,128)S(1)}, f32[48,2048]{1,0:T(8,128)S(1)}) custom-call(f32[64,4096]{1,0:T(8,128)S(1)} %get-tuple-element.35.own, f32[64,4096]{1,0:T(8,128)S(1)} %collective-permute-done.other, f32[64,4096]{1,0:T(8,128)S(1)} %get-tuple-element.49.drive, f32[48,4096]{1,0:T(8,128)S(1)} %get-tuple-element.39.mine), custom_call_target="tpu_custom_call" | custom-call | tf_op jit(solution)/shard_map/pallas_call | solution.py:90
  3.7 0.8 %shard_map.29 = (f32[8,3584]{1,0:T(8,128)S(1)}, f32[48,2048]{1,0:T(8,128)S(1)}, f32[8,9216]{1,0:T(8,128)S(1)}) custom-call(f32[64,4096]{1,0:T(8,128)S(1)} %get-tuple-element.35.own, f32[64,4096]{1,0:T(8,128)S(1)} %collective-permute-done.other, f32[64,4096]{1,0:T(8,128)S(1)} %get-tuple-element.49.drive, f32[48,4096]{1,0:T(8,128)S(1)} %get-tuple-element.39.mine), custom_call_target="tpu_custom_call" | custom-call | tf_op jit(solution)/shard_map/pallas_call | solution.py:90
  4.6 2.9 %collective-permute-start.4 = (f32[8,9216]{1,0:T(8,128)S(1)}, f32[8,9216]{1,0:T(8,128)S(1)}, u32[]{:S(2)}, u32[]{:S(2)}) collective-permute-start(f32[8,9216]{1,0:T(8,128)S(1)} %get-tuple-element.47), channel_id=1, source_target_pairs={{0,16},{1,4},{2,5},{3,6},{4,1},{5,2},{6,3},{7,23},{8,24},{9,12},{1... | collective-permute-start | bytes 884744 | tf_op jit(solution)/shard_map/ppermute | solution.py:33
  7.5 0.0 collective-permute-start.2
  7.5 2.0 %collective-permute-start.1 = (f32[8,3584]{1,0:T(8,128)S(1)}, f32[8,3584]{1,0:T(8,128)S(1)}, u32[]{:S(2)}, u32[]{:S(2)}) collective-permute-start(f32[8,3584]{1,0:T(8,128)S(1)} %get-tuple-element.38), channel_id=1, source_target_pairs={{0,8},{1,9},{2,10},{3,11},{4,12},{5,13},{6,14},{7,15},{8,0},{9,1},... | collective-permute-start | bytes 344072 | tf_op jit(solution)/shard_map/ppermute | solution.py:33
  9.5 2.1 %shard_map.30 = (f32[16,4096]{1,0:T(8,128)S(1)}, f32[48,4096]{1,0:T(8,128)S(1)}, f32[40,4096]{1,0:T(8,128)S(1)}) custom-call(f32[64,4096]{1,0:T(8,128)S(1)} %get-tuple-element.35.own, f32[64,4096]{1,0:T(8,128)S(1)} %collective-permute-done.other, f32[64,4096]{1,0:T(8,128)S(1)} %get-tuple-element.49.drive), custom_call_target="tpu_custom_call" | custom-call | tf_op jit(solution)/shard_map/pallas_call | solution.py:90
  11.6 1.9 %collective-permute-done.2.right = f32[8,3584]{1,0:T(8,128)S(1)} collective-permute-done((f32[8,3584]{1,0:T(8,128)S(1)}, f32[8,3584]{1,0:T(8,128)S(1)}, u32[]{:S(2)}, u32[]{:S(2)}) %collective-permute-start.2) | collective-permute-done | bytes 114720 | tf_op jit(solution)/shard_map/ppermute | solution.py:33
  13.5 1.7 %collective-permute-done.1.left = f32[8,3584]{1,0:T(8,128)S(1)} collective-permute-done((f32[8,3584]{1,0:T(8,128)S(1)}, f32[8,3584]{1,0:T(8,128)S(1)}, u32[]{:S(2)}, u32[]{:S(2)}) %collective-permute-start.1) | collective-permute-done | bytes 114720 | tf_op jit(solution)/shard_map/ppermute | solution.py:33
  15.2 0.0 collective-permute-done.4.got
  15.2 1.5 %shard_map.33 = (f32[8,3072]{1,0:T(8,128)S(1)}, f32[32,4096]{1,0:T(8,128)S(1)}) custom-call(f32[64,4096]{1,0:T(8,128)S(1)} %get-tuple-element.35.own, f32[64,4096]{1,0:T(8,128)S(1)} %collective-permute-done.other, f32[64,4096]{1,0:T(8,128)S(1)} %get-tuple-element.49.drive, f32[8,9216]{1,0:T(8,128)S(1)} %collective-permute-done.4.got), custom_call_target="tpu_custom_call" | custom-call | tf_op jit(solution)/shard_map/pallas_call | solution.py:90
  16.7 0.2 shard_map.36
  16.9 0.1 collective-permute-start.7
  16.9 0.1 collective-permute-start.3
  17.0 0.2 shard_map.34.state
  17.2 8.4 %collective-permute-done.3.middle = f32[16,4096]{1,0:T(8,128)S(1)} collective-permute-done((f32[16,4096]{1,0:T(8,128)S(1)}, f32[16,4096]{1,0:T(8,128)S(1)}, u32[]{:S(2)}, u32[]{:S(2)}) %collective-permute-start.3) | collective-permute-done | bytes 262176 | tf_op jit(solution)/shard_map/ppermute | solution.py:33
  25.7 0.0 collective-permute-start.5
  25.7 1.2 %collective-permute-start.6 = (f32[8,3072]{1,0:T(8,128)S(1)}, f32[8,3072]{1,0:T(8,128)S(1)}, u32[]{:S(2)}, u32[]{:S(2)}) collective-permute-start(f32[8,3072]{1,0:T(8,128)S(1)} %get-tuple-element.48), channel_id=1, source_target_pairs={{0,8},{1,9},{2,10},{3,11},{4,12},{5,13},{6,14},{7,15},{8,0},{9,1},... | collective-permute-start | bytes 294920 | tf_op jit(solution)/shard_map/ppermute | solution.py:33
  26.8 0.0 collective-permute-done.7.refs_2_
  26.9 1.0 %shard_map.37.refs_3_ = f32[1,64,4096]{2,1,0:T(8,128)} custom-call(f32[32,4096]{1,0:T(8,128)S(1)} %get-tuple-element.58.refs_0_, f32[16,4096]{1,0:T(8,128)S(1)} %get-tuple-element.59.refs_1_, f32[32,4096]{1,0:T(8,128)S(1)} %collective-permute-done.7.refs_2_), custom_call_target="tpu_custom_call" | custom-call | tf_op jit(solution)/shard_map/pallas_call | solution.py:491
  27.9 3.0 %collective-permute-done.6.outer = f32[8,3072]{1,0:T(8,128)S(1)} collective-permute-done((f32[8,3072]{1,0:T(8,128)S(1)}, f32[8,3072]{1,0:T(8,128)S(1)}, u32[]{:S(2)}, u32[]{:S(2)}) %collective-permute-start.6) | collective-permute-done | bytes 98336 | tf_op jit(solution)/shard_map/ppermute | solution.py:33
  30.9 0.0 collective-permute-start.8
  30.9 0.0 collective-permute-done.5.refs_0_
  30.9 1.3 %collective-permute-done.8.refs_2_ = f32[8,4096]{1,0:T(8,128)S(1)} collective-permute-done((f32[8,4096]{1,0:T(8,128)S(1)}, f32[8,4096]{1,0:T(8,128)S(1)}, u32[]{:S(2)}, u32[]{:S(2)}) %collective-permute-start.8) | collective-permute-done | bytes 131104 | tf_op jit(solution)/shard_map/ppermute | solution.py:33
  32.2 0.1 shard_map.39
  (4 shorter events, 0.0 us)
Async XLA Ops:
  0.0 3.0 %collective-permute-start = (f32[64,4096]{1,0:T(8,128)}, f32[64,4096]{1,0:T(8,128)S(1)}, u32[]{:S(2)}, u32[]{:S(2)}) collective-permute-start(f32[64,4096]{1,0:T(8,128)} %bitcast.1), channel_id=1, source_target_pairs={{0,4},{1,5},{2,6},{3,7},{4,0},{5,1},{6,2},{7,3},{8,12},{9,13},{10,... | collective-permute-start | bytes 3145736 | tf_op jit(solution)/shard_map/ppermute | solution.py:33
  4.6 10.6 %collective-permute-start.4 = (f32[8,9216]{1,0:T(8,128)S(1)}, f32[8,9216]{1,0:T(8,128)S(1)}, u32[]{:S(2)}, u32[]{:S(2)}) collective-permute-start(f32[8,9216]{1,0:T(8,128)S(1)} %get-tuple-element.47), channel_id=1, source_target_pairs={{0,16},{1,4},{2,5},{3,6},{4,1},{5,2},{6,3},{7,23},{8,24},{9,12},{1... | collective-permute-start | bytes 884744 | tf_op jit(solution)/shard_map/ppermute | solution.py:33
  7.5 6.0 %collective-permute-start.2 = (f32[8,3584]{1,0:T(8,128)S(1)}, f32[8,3584]{1,0:T(8,128)S(1)}, u32[]{:S(2)}, u32[]{:S(2)}) collective-permute-start(f32[8,3584]{1,0:T(8,128)S(1)} %get-tuple-element.40), channel_id=1, source_target_pairs={{0,8},{1,9},{2,10},{3,11},{4,12},{5,13},{6,14},{7,15},{8,0},{9,1},... | collective-permute-start | bytes 344072 | tf_op jit(solution)/shard_map/ppermute | solution.py:33
  7.5 7.7 %collective-permute-start.1 = (f32[8,3584]{1,0:T(8,128)S(1)}, f32[8,3584]{1,0:T(8,128)S(1)}, u32[]{:S(2)}, u32[]{:S(2)}) collective-permute-start(f32[8,3584]{1,0:T(8,128)S(1)} %get-tuple-element.38), channel_id=1, source_target_pairs={{0,8},{1,9},{2,10},{3,11},{4,12},{5,13},{6,14},{7,15},{8,0},{9,1},... | collective-permute-start | bytes 344072 | tf_op jit(solution)/shard_map/ppermute | solution.py:33
  16.9 10.0 %collective-permute-start.7 = (f32[32,4096]{1,0:T(8,128)S(1)}, f32[32,4096]{1,0:T(8,128)S(1)}, u32[]{:S(2)}, u32[]{:S(2)}) collective-permute-start(f32[32,4096]{1,0:T(8,128)S(1)} %get-tuple-element.60), channel_id=1, source_target_pairs={{0,4},{1,5},{2,6},{3,7},{4,0},{5,1},{6,2},{7,3},{8,12},{9,13},{10,... | collective-permute-start | bytes 1572872 | tf_op jit(solution)/shard_map/ppermute | solution.py:33
  16.9 8.7 %collective-permute-start.3 = (f32[16,4096]{1,0:T(8,128)S(1)}, f32[16,4096]{1,0:T(8,128)S(1)}, u32[]{:S(2)}, u32[]{:S(2)}) collective-permute-start(f32[16,4096]{1,0:T(8,128)S(1)} %get-tuple-element.43), channel_id=1, source_target_pairs={{0,8},{1,9},{2,10},{3,11},{4,12},{5,13},{6,14},{7,15},{8,0},{9,1},... | collective-permute-start | bytes 786440 | tf_op jit(solution)/shard_map/ppermute | solution.py:33
  25.7 5.2 %collective-permute-start.5 = (f32[16,4096]{1,0:T(8,128)S(1)}, f32[16,4096]{1,0:T(8,128)S(1)}, u32[]{:S(2)}, u32[]{:S(2)}) collective-permute-start(f32[16,4096]{1,0:T(8,128)S(1)} %get-tuple-element.51), channel_id=1, source_target_pairs={{0,4},{1,5},{2,6},{3,7},{4,0},{5,1},{6,2},{7,3},{8,12},{9,13},{10,... | collective-permute-start | bytes 786440 | tf_op jit(solution)/shard_map/ppermute | solution.py:33
  25.7 5.2 %collective-permute-start.6 = (f32[8,3072]{1,0:T(8,128)S(1)}, f32[8,3072]{1,0:T(8,128)S(1)}, u32[]{:S(2)}, u32[]{:S(2)}) collective-permute-start(f32[8,3072]{1,0:T(8,128)S(1)} %get-tuple-element.48), channel_id=1, source_target_pairs={{0,8},{1,9},{2,10},{3,11},{4,12},{5,13},{6,14},{7,15},{8,0},{9,1},... | collective-permute-start | bytes 294920 | tf_op jit(solution)/shard_map/ppermute | solution.py:33
  30.9 1.3 %collective-permute-start.8 = (f32[8,4096]{1,0:T(8,128)S(1)}, f32[8,4096]{1,0:T(8,128)S(1)}, u32[]{:S(2)}, u32[]{:S(2)}) collective-permute-start(f32[8,4096]{1,0:T(8,128)S(1)} %get-tuple-element.63), channel_id=1, source_target_pairs={{0,4},{1,5},{2,6},{3,7},{4,0},{5,1},{6,2},{7,3},{8,12},{9,13},{10,... | collective-permute-start | bytes 393224 | tf_op jit(solution)/shard_map/ppermute | solution.py:33

commit v7 on v6

--- a/solution.py
+++ b/solution.py
@@ -304,14 +304,14 @@
     return kept(a), kept(b), d, kept
 
 
-def outer_kernel(half, own, other, drive, got, sent, ends):
-    core, chip = place()
-    first = core == 0
+def outer_kernel(half, own, other, drive, got, mine, theirs, sent, ends, state):
+    core, chip = place()
+    first = core == 0
+    a, b, d, kept = outer_window(half, own, other, drive, got)
+    (f_a, g_a), (f_b, g_b) = start_of(a, d, kept), start_of(b, d, kept)
 
     @pl.when(chip == 0)
     def _():
-        a, b, d, kept = outer_window(half, own, other, drive, got)
-        (f_a, g_a), (f_b, g_b) = start_of(a, d, kept), start_of(b, d, kept)
         e_a = g_a + (f_a - g_a)
         e_b = kept(coarse_of(e_a, around(e_a), d)) + (f_b - g_b)
         frame = pltpu.roll(e_b, 16 - CUT, 0)[:8]
@@ -319,15 +319,8 @@
         ends[0:16, :] = e_a
         ends[16:32, :] = e_b
 
-
-def outer_state_kernel(half, own, other, drive, got, mine, theirs, state):
-    core, chip = place()
-    first = core == 0
-
     @pl.when(chip > 0)
     def _():
-        a, b, d, kept = outer_window(half, own, other, drive, got)
-        (f_a, g_a), (f_b, g_b) = start_of(a, d, kept), start_of(b, d, kept)
         rows = pl.ds(pl.multiple_of((half - WIDE) * core, 8), 16)
         before = picked(first, mine[rows, :], theirs[rows, :])
         d_rows = pl.ds(pl.multiple_of((2 * half - 16) * core, 8), 16)
@@ -445,8 +438,7 @@
 
 
 def write_kernel(half, last, *refs):
-    count = 3
-    pieces, out, sems = refs[:count], refs[-2], refs[-1]
+    pieces, out, sems = refs[: 1 if last else 5], refs[-2], refs[-1]
     core, chip = place()
 
     def copy_all(order):
@@ -465,24 +457,33 @@
         for copy in copies:
             copy.wait()
 
-    parts = ((0, 0, 8), (1, 8, half - 16), (2, half - 8, 8))
     if last:
 
         @pl.when(chip > 0)
         def _():
-            copy_all(((False, 1, 0, 0, half - 16), (True, 2, 1, 0, 8), (False, 2, 2, 0, 8)))
+            copy_all(((False, 2, 0, 0, 8),))
 
     else:
+        rest = half - 16
 
         @pl.when(chip == 0)
         def _():
+            parts = ((0, 0, 8), (1, 8, rest), (2, half - 8, 8))
             copy_all(
-                [(mine, part, source, *rows) for mine, source in ((True, 0), (False, 2)) for part, *rows in parts]
+                [(mine, part, source, *rows) for mine, source in ((True, 0), (False, 1)) for part, *rows in parts]
             )
 
         @pl.when(chip > 0)
         def _():
-            copy_all(((True, 0, 0, 0, 8), (True, 1, 1, 0, half - 16), (False, 0, 2, 0, 8)))
+            copy_all(
+                (
+                    (True, 0, 0, 0, 8),
+                    (False, 0, 1, 0, 8),
+                    (True, 1, 2, 0, rest),
+                    (False, 1, 3, 0, rest),
+                    (True, 2, 4, 0, 8),
+                )
+            )
 
 
 def written(half, pieces, shape, into=None):
@@ -491,9 +492,9 @@
     return pl.pallas_call(
         functools.partial(write_kernel, half, into is not None),
         out_shape=jax.ShapeDtypeStruct(shape, jnp.float32),
-        in_specs=[vmem] * 3 + [anywhere] * len(extra),
+        in_specs=[vmem] * len(pieces) + [anywhere] * len(extra),
         out_specs=anywhere,
-        input_output_aliases={3: 0} if extra else {},
+        input_output_aliases={len(pieces): 0} if extra else {},
         scratch_shapes=[pltpu.SemaphoreType.DMA((6,))],
         compiler_params=pltpu.CompilerParams(vmem_limit_bytes=16 << 20),
     )(*pieces, *extra)
@@ -632,17 +633,12 @@
         [(8, width), (8, width), (16, width)],
         (here_l, here_r, held, delta_own, delta_other),
     )
-    sent_3, ends_3 = compute(
+    sent_3, ends_3, state_3 = compute(
         functools.partial(outer_kernel, half),
-        [(8, width * 3 // 4), (32, width)],
-        (own, other, after(held, frame), got),
+        [(8, width * 3 // 4), (32, width), (3 * 24, width)],
+        (own, other, after(held, frame), got, delta_own, delta_other),
     )
     here_3 = routed(sent_3, stage_swap(0))
-    (state_3,) = compute(
-        functools.partial(outer_state_kernel, half),
-        [(3 * 24, width)],
-        (own, other, after(held, sent_3), got, delta_own, delta_other),
-    )
     keep_1, send_1 = compute(
         gather_kernel, [(half, width)] * 2, (ends_l, ends_r, ends_2, ends_3, keep_8, send_8)
     )
@@ -654,16 +650,15 @@
         scratch_shapes=[pltpu.VMEM((half, width), jnp.float32)],
     )
     back_2 = routed(send_2, partner)
-    out = written(half, (keep_1, keep_2, back_1), starts.shape)
-    out, state_3 = lax.optimization_barrier((out, state_3))
     keep_3, send_3 = compute(
         outer_end,
         [(8, width)] * 2,
-        (here_2, here_3, state_3),
+        (here_2, here_3, after(state_3, keep_2)),
         scratch_shapes=[pltpu.VMEM((24, width), jnp.float32)],
     )
     back_3 = routed(send_3, partner)
-    return written(half, (back_2, keep_3, back_3), starts.shape, into=out)
+    out = written(half, (keep_1, back_1, keep_2, back_2, keep_3), starts.shape)
+    return written(half, (back_3,), starts.shape, into=out)
 
 
 def solution(mesh):

time: 32.6 us -> 27.6 us (0.85)
  waiting for transfers between devices: 16.7 us -> 11.9 us
    ppermute x9, waiting for transfers between devices: 16.7 us -> 11.9 us  [routed(): return lax.ppermute(block, AXES, pairs)]
    pallas_call x10 -> x9, Pallas kernels: 5.51 us -> 5.38 us  [compute(): pl.pallas_call(kernel, out_shape=shapes, in_specs=[vmem] * len(args), out...]
  transfers between devices with their start and end apart: 9 -> 9, of which waited for: 6 -> 6; matrix products, arithmetic and copies ran while one was open for 0% -> 0% of each run, Pallas kernels for 17% -> 26%
where the time goes in v7:
time: 27.6 us; the launch traced here: 27.4 us
  waiting for transfers between devices  11.9 us (43%)
  Pallas kernels  8.61 us (31%)
  starting transfers between devices  6.8 us (25%)
    ppermute x9, waiting for transfers between devices, routed(): return lax.ppermute(block, AXES, pairs)  11.9 us
    ppermute x9, starting transfers between devices, routed(): return lax.ppermute(block, AXES, pairs)  6.8 us
    pallas_call x9, Pallas kernels, compute(): pl.pallas_call(kernel, out_shape=shapes, in_specs=[vmem] * len(args), out...  5.38 us
    pallas_call x1, Pallas kernels, two_chips(): pl.pallas_call(functools.partial(load_kernel, half), out_shape=[jax.Shape...  2.15 us
    pallas_call x2, Pallas kernels, written(): pl.pallas_call(functools.partial(write_kernel, half, into is not None), o...  1.08 us
  transfers between devices with their start and end apart: 9, of which 6 were waited for; matrix products, arithmetic and copies ran while one was open for 0% of the time, Pallas kernels for 26%

profile of v7, /device:TPU:0, one launch (start us, length us, event | category | flops | bytes accessed | tf_op | source)
XLA Modules:
  0.0 27.4 jit_solution(13705117338474239904)
XLA Ops:
  0.0 0.5 %collective-permute-start = (f32[64,4096]{1,0:T(8,128)}, f32[64,4096]{1,0:T(8,128)S(1)}, u32[]{:S(2)}, u32[]{:S(2)}) collective-permute-start(f32[64,4096]{1,0:T(8,128)} %bitcast.1), channel_id=1, source_target_pairs={{0,4},{1,5},{2,6},{3,7},{4,0},{5,1},{6,2},{7,3},{8,12},{9,13},{10,... | collective-permute-start | bytes 3145736 | tf_op jit(solution)/shard_map/ppermute | solution.py:33
  0.5 2.1 %load.1 = (f32[64,4096]{1,0:T(8,128)S(1)}, f32[64,4096]{1,0:T(8,128)S(1)}, f32[48,4096]{1,0:T(8,128)S(1)}) custom-call(f32[1,64,4096]{2,1,0:T(8,128)} %starts.1, f32[64,4096]{1,0:T(8,128)} %drive.1), custom_call_target="tpu_custom_call" | custom-call | flops 5898240 | bytes 4194304 | tf_op jit(solution)/shard_map/load/pallas_call | solution.py:595
  2.6 0.3 %collective-permute-done.other = f32[64,4096]{1,0:T(8,128)S(1)} collective-permute-done((f32[64,4096]{1,0:T(8,128)}, f32[64,4096]{1,0:T(8,128)S(1)}, u32[]{:S(2)}, u32[]{:S(2)}) %collective-permute-start) | collective-permute-done | bytes 1048608 | tf_op jit(solution)/shard_map/ppermute | solution.py:33
  3.0 0.7 %shard_map.28 = (f32[8,3584]{1,0:T(8,128)S(1)}, f32[48,2048]{1,0:T(8,128)S(1)}) custom-call(f32[64,4096]{1,0:T(8,128)S(1)} %get-tuple-element.34.own, f32[64,4096]{1,0:T(8,128)S(1)} %collective-permute-done.other, f32[64,4096]{1,0:T(8,128)S(1)} %get-tuple-element.45.drive, f32[48,4096]{1,0:T(8,128)S(1)} %get-tuple-element.38.mine), custom_call_target="tpu_custom_call" | custom-call | tf_op jit(solution)/shard_map/pallas_call | solution.py:90
  3.7 0.8 %shard_map.29 = (f32[8,3584]{1,0:T(8,128)S(1)}, f32[48,2048]{1,0:T(8,128)S(1)}, f32[8,9216]{1,0:T(8,128)S(1)}) custom-call(f32[64,4096]{1,0:T(8,128)S(1)} %get-tuple-element.34.own, f32[64,4096]{1,0:T(8,128)S(1)} %collective-permute-done.other, f32[64,4096]{1,0:T(8,128)S(1)} %get-tuple-element.45.drive, f32[48,4096]{1,0:T(8,128)S(1)} %get-tuple-element.38.mine), custom_call_target="tpu_custom_call" | custom-call | tf_op jit(solution)/shard_map/pallas_call | solution.py:90
  4.6 2.9 %collective-permute-start.4 = (f32[8,9216]{1,0:T(8,128)S(1)}, f32[8,9216]{1,0:T(8,128)S(1)}, u32[]{:S(2)}, u32[]{:S(2)}) collective-permute-start(f32[8,9216]{1,0:T(8,128)S(1)} %get-tuple-element.46), channel_id=1, source_target_pairs={{0,16},{1,4},{2,5},{3,6},{4,1},{5,2},{6,3},{7,23},{8,24},{9,12},{1... | collective-permute-start | bytes 884744 | tf_op jit(solution)/shard_map/ppermute | solution.py:33
  7.5 0.0 collective-permute-start.3
  7.5 2.0 %collective-permute-start.2 = (f32[8,3584]{1,0:T(8,128)S(1)}, f32[8,3584]{1,0:T(8,128)S(1)}, u32[]{:S(2)}, u32[]{:S(2)}) collective-permute-start(f32[8,3584]{1,0:T(8,128)S(1)} %get-tuple-element.37), channel_id=1, source_target_pairs={{0,8},{1,9},{2,10},{3,11},{4,12},{5,13},{6,14},{7,15},{8,0},{9,1},... | collective-permute-start | bytes 344072 | tf_op jit(solution)/shard_map/ppermute | solution.py:33
  9.5 2.1 %shard_map.30 = (f32[16,4096]{1,0:T(8,128)S(1)}, f32[48,4096]{1,0:T(8,128)S(1)}, f32[40,4096]{1,0:T(8,128)S(1)}) custom-call(f32[64,4096]{1,0:T(8,128)S(1)} %get-tuple-element.34.own, f32[64,4096]{1,0:T(8,128)S(1)} %collective-permute-done.other, f32[64,4096]{1,0:T(8,128)S(1)} %get-tuple-element.45.drive), custom_call_target="tpu_custom_call" | custom-call | tf_op jit(solution)/shard_map/pallas_call | solution.py:90
  11.6 0.1 collective-permute-start.1
  11.7 1.8 %collective-permute-done.3.right = f32[8,3584]{1,0:T(8,128)S(1)} collective-permute-done((f32[8,3584]{1,0:T(8,128)S(1)}, f32[8,3584]{1,0:T(8,128)S(1)}, u32[]{:S(2)}, u32[]{:S(2)}) %collective-permute-start.3) | collective-permute-done | bytes 114720 | tf_op jit(solution)/shard_map/ppermute | solution.py:33
  13.5 2.5 %collective-permute-done.2.left = f32[8,3584]{1,0:T(8,128)S(1)} collective-permute-done((f32[8,3584]{1,0:T(8,128)S(1)}, f32[8,3584]{1,0:T(8,128)S(1)}, u32[]{:S(2)}, u32[]{:S(2)}) %collective-permute-start.2) | collective-permute-done | bytes 114720 | tf_op jit(solution)/shard_map/ppermute | solution.py:33
  16.0 0.0 collective-permute-done.4.got
  16.0 1.5 %shard_map.33 = (f32[8,3072]{1,0:T(8,128)S(1)}, f32[32,4096]{1,0:T(8,128)S(1)}, f32[72,4096]{1,0:T(8,128)S(1)}) custom-call(f32[64,4096]{1,0:T(8,128)S(1)} %get-tuple-element.34.own, f32[64,4096]{1,0:T(8,128)S(1)} %collective-permute-done.other, f32[64,4096]{1,0:T(8,128)S(1)} %get-tuple-element.45.drive, f32[8,9216]{1,0:T(8,128)S(1)} %collective-permute-done.4.got, ...), custom_call_target="tpu_custom_call" | custom-call | tf_op jit(solution)/shard_map/pallas_call | solution.py:90
  17.5 0.2 shard_map.36
  17.7 0.1 collective-permute-start.7
  17.8 3.0 %collective-permute-done.1.middle = f32[16,4096]{1,0:T(8,128)S(1)} collective-permute-done((f32[16,4096]{1,0:T(8,128)S(1)}, f32[16,4096]{1,0:T(8,128)S(1)}, u32[]{:S(2)}, u32[]{:S(2)}) %collective-permute-start.1) | collective-permute-done | bytes 262176 | tf_op jit(solution)/shard_map/ppermute | solution.py:33
  20.8 0.0 collective-permute-start.8
  20.8 1.2 %collective-permute-start.5 = (f32[8,3072]{1,0:T(8,128)S(1)}, f32[8,3072]{1,0:T(8,128)S(1)}, u32[]{:S(2)}, u32[]{:S(2)}) collective-permute-start(f32[8,3072]{1,0:T(8,128)S(1)} %get-tuple-element.47), channel_id=1, source_target_pairs={{0,8},{1,9},{2,10},{3,11},{4,12},{5,13},{6,14},{7,15},{8,0},{9,1},... | collective-permute-start | bytes 294920 | tf_op jit(solution)/shard_map/ppermute | solution.py:33
  22.0 4.0 %collective-permute-done.5.outer = f32[8,3072]{1,0:T(8,128)S(1)} collective-permute-done((f32[8,3072]{1,0:T(8,128)S(1)}, f32[8,3072]{1,0:T(8,128)S(1)}, u32[]{:S(2)}, u32[]{:S(2)}) %collective-permute-start.5) | collective-permute-done | bytes 98336 | tf_op jit(solution)/shard_map/ppermute | solution.py:33
  26.0 0.0 collective-permute-start.6
  26.0 0.0 collective-permute-done.8.refs_3_
  26.0 0.0 collective-permute-done.7.refs_1_
  26.0 1.0 %shard_map.37.refs_1_ = f32[1,64,4096]{2,1,0:T(8,128)} custom-call(f32[32,4096]{1,0:T(8,128)S(1)} %get-tuple-element.59.refs_0_, f32[32,4096]{1,0:T(8,128)S(1)} %collective-permute-done.7.refs_1_, f32[16,4096]{1,0:T(8,128)S(1)} %get-tuple-element.50.refs_2_, f32[16,4096]{1,0:T(8,128)S(1)} %collective-permute-done.8.refs_3_, ...), custom_call_target="tpu_custom_call" | custom-call | tf_op jit(solution)/shard_map/pallas_call | solution.py:492
  27.1 0.3 %collective-permute-done.6.refs_0_ = f32[8,4096]{1,0:T(8,128)S(1)} collective-permute-done((f32[8,4096]{1,0:T(8,128)S(1)}, f32[8,4096]{1,0:T(8,128)S(1)}, u32[]{:S(2)}, u32[]{:S(2)}) %collective-permute-start.6) | collective-permute-done | bytes 131104 | tf_op jit(solution)/shard_map/ppermute | solution.py:33
  27.4 0.1 shard_map.38
  (4 shorter events, 0.0 us)
Async XLA Ops:
  0.0 3.0 %collective-permute-start = (f32[64,4096]{1,0:T(8,128)}, f32[64,4096]{1,0:T(8,128)S(1)}, u32[]{:S(2)}, u32[]{:S(2)}) collective-permute-start(f32[64,4096]{1,0:T(8,128)} %bitcast.1), channel_id=1, source_target_pairs={{0,4},{1,5},{2,6},{3,7},{4,0},{5,1},{6,2},{7,3},{8,12},{9,13},{10,... | collective-permute-start | bytes 3145736 | tf_op jit(solution)/shard_map/ppermute | solution.py:33
  4.6 11.4 %collective-permute-start.4 = (f32[8,9216]{1,0:T(8,128)S(1)}, f32[8,9216]{1,0:T(8,128)S(1)}, u32[]{:S(2)}, u32[]{:S(2)}) collective-permute-start(f32[8,9216]{1,0:T(8,128)S(1)} %get-tuple-element.46), channel_id=1, source_target_pairs={{0,16},{1,4},{2,5},{3,6},{4,1},{5,2},{6,3},{7,23},{8,24},{9,12},{1... | collective-permute-start | bytes 884744 | tf_op jit(solution)/shard_map/ppermute | solution.py:33
  7.5 6.0 %collective-permute-start.3 = (f32[8,3584]{1,0:T(8,128)S(1)}, f32[8,3584]{1,0:T(8,128)S(1)}, u32[]{:S(2)}, u32[]{:S(2)}) collective-permute-start(f32[8,3584]{1,0:T(8,128)S(1)} %get-tuple-element.39), channel_id=1, source_target_pairs={{0,8},{1,9},{2,10},{3,11},{4,12},{5,13},{6,14},{7,15},{8,0},{9,1},... | collective-permute-start | bytes 344072 | tf_op jit(solution)/shard_map/ppermute | solution.py:33
  7.5 8.5 %collective-permute-start.2 = (f32[8,3584]{1,0:T(8,128)S(1)}, f32[8,3584]{1,0:T(8,128)S(1)}, u32[]{:S(2)}, u32[]{:S(2)}) collective-permute-start(f32[8,3584]{1,0:T(8,128)S(1)} %get-tuple-element.37), channel_id=1, source_target_pairs={{0,8},{1,9},{2,10},{3,11},{4,12},{5,13},{6,14},{7,15},{8,0},{9,1},... | collective-permute-start | bytes 344072 | tf_op jit(solution)/shard_map/ppermute | solution.py:33
  11.6 9.2 %collective-permute-start.1 = (f32[16,4096]{1,0:T(8,128)S(1)}, f32[16,4096]{1,0:T(8,128)S(1)}, u32[]{:S(2)}, u32[]{:S(2)}) collective-permute-start(f32[16,4096]{1,0:T(8,128)S(1)} %get-tuple-element.41), channel_id=1, source_target_pairs={{0,8},{1,9},{2,10},{3,11},{4,12},{5,13},{6,14},{7,15},{8,0},{9,1},... | collective-permute-start | bytes 786440 | tf_op jit(solution)/shard_map/ppermute | solution.py:33
  17.7 8.3 %collective-permute-start.7 = (f32[32,4096]{1,0:T(8,128)S(1)}, f32[32,4096]{1,0:T(8,128)S(1)}, u32[]{:S(2)}, u32[]{:S(2)}) collective-permute-start(f32[32,4096]{1,0:T(8,128)S(1)} %get-tuple-element.60), channel_id=1, source_target_pairs={{0,4},{1,5},{2,6},{3,7},{4,0},{5,1},{6,2},{7,3},{8,12},{9,13},{10,... | collective-permute-start | bytes 1572872 | tf_op jit(solution)/shard_map/ppermute | solution.py:33
  20.8 5.2 %collective-permute-start.8 = (f32[16,4096]{1,0:T(8,128)S(1)}, f32[16,4096]{1,0:T(8,128)S(1)}, u32[]{:S(2)}, u32[]{:S(2)}) collective-permute-start(f32[16,4096]{1,0:T(8,128)S(1)} %get-tuple-element.61), channel_id=1, source_target_pairs={{0,4},{1,5},{2,6},{3,7},{4,0},{5,1},{6,2},{7,3},{8,12},{9,13},{10,... | collective-permute-start | bytes 786440 | tf_op jit(solution)/shard_map/ppermute | solution.py:33
  20.8 5.2 %collective-permute-start.5 = (f32[8,3072]{1,0:T(8,128)S(1)}, f32[8,3072]{1,0:T(8,128)S(1)}, u32[]{:S(2)}, u32[]{:S(2)}) collective-permute-start(f32[8,3072]{1,0:T(8,128)S(1)} %get-tuple-element.47), channel_id=1, source_target_pairs={{0,8},{1,9},{2,10},{3,11},{4,12},{5,13},{6,14},{7,15},{8,0},{9,1},... | collective-permute-start | bytes 294920 | tf_op jit(solution)/shard_map/ppermute | solution.py:33
  26.0 1.3 %collective-permute-start.6 = (f32[8,4096]{1,0:T(8,128)S(1)}, f32[8,4096]{1,0:T(8,128)S(1)}, u32[]{:S(2)}, u32[]{:S(2)}) collective-permute-start(f32[8,4096]{1,0:T(8,128)S(1)} %get-tuple-element.52), channel_id=1, source_target_pairs={{0,4},{1,5},{2,6},{3,7},{4,0},{5,1},{6,2},{7,3},{8,12},{9,13},{10,... | collective-permute-start | bytes 393224 | tf_op jit(solution)/shard_map/ppermute | solution.py:33
